TPU v7x, 32 devices: a whole 2x2x4 slice. The times are simulated.
32 devices in a mesh: ctx: 16 (over z, y, x), fsdp: 2 (over core).
Axes of the slice: x: 2, y: 2, z: 4, core: 2. Of those that a mesh axis runs over, the one named last changes fastest.
Arguments:
- tokens: bfloat16 [2, 2, 2048, 512], P(None, 'fsdp', 'ctx'), may hold values from -6 to 6
- cotangent: bfloat16 [2, 2, 2048, 512], P(None, 'fsdp', 'ctx'), may hold values from -6 to 6
- lengths: int32 [2, 2, 8], P(None, 'fsdp'), may hold values from 1 to 1024, 2048 in all within a row
- deal_order: int32 [2, 2, 2048], P(None, 'fsdp'), may hold values from 0 to 2047, as said below
- w_query: bfloat16 [512, 512], P('fsdp'), may hold values from -0.25 to 0.25
- w_key: bfloat16 [512, 512], P('fsdp'), may hold values from -0.25 to 0.25
- w_value: bfloat16 [512, 512], P('fsdp'), may hold values from -0.25 to 0.25
- w_out: bfloat16 [512, 512], P('fsdp'), may hold values from -1 to 1
- w_up: bfloat16 [512, 2048], P('fsdp'), may hold values from -0.25 to 0.25
- w_down: bfloat16 [2048, 512], P('fsdp'), may hold values from -0.1875 to 0.1875
- b_query: bfloat16 [512], P('fsdp'), may hold values from -1.796875 to 1.796875
- b_value: bfloat16 [512], P('fsdp'), may hold values from -1.796875 to 1.796875
- b_out: bfloat16 [512], P('fsdp'), may hold values from -1.796875 to 1.796875
- b_up: bfloat16 [2048], P('fsdp'), may hold values from -1.796875 to 1.796875
- b_down: bfloat16 [512], P('fsdp'), may hold values from -1.796875 to 1.796875
- gain_one: bfloat16 [512], P('fsdp'), may hold values from 0.5 to 1.5
- shift_one: bfloat16 [512], P('fsdp'), may hold values from -1.796875 to 1.796875
- gain_two: bfloat16 [512], P('fsdp'), may hold values from 0.5 to 1.5
- shift_two: bfloat16 [512], P('fsdp'), may hold values from -1.796875 to 1.796875
- positions: bfloat16 [1024, 512], P('fsdp'), may hold values from -6 to 6
Outputs:
- output: bfloat16 [2, 2, 2048, 512], P(None, 'fsdp', 'ctx')
- grad_tokens: bfloat16 [2, 2, 2048, 512], P(None, 'fsdp', 'ctx')
- grad_w_query: float32 [512, 512], P('fsdp')
- grad_w_key: float32 [512, 512], P('fsdp')
- grad_w_value: float32 [512, 512], P('fsdp')
- grad_w_out: float32 [512, 512], P('fsdp')
- grad_w_up: float32 [512, 2048], P('fsdp')
- grad_w_down: float32 [2048, 512], P('fsdp')
- grad_b_query: float32 [512], P('fsdp')
- grad_b_value: float32 [512], P('fsdp')
- grad_b_out: float32 [512], P('fsdp')
- grad_b_up: float32 [2048], P('fsdp')
- grad_b_down: float32 [512], P('fsdp')
- grad_gain_one: float32 [512], P('fsdp')
- grad_shift_one: float32 [512], P('fsdp')
- grad_gain_two: float32 [512], P('fsdp')
- grad_shift_two: float32 [512], P('fsdp')
- grad_positions: float32 [1024, 512], P('fsdp')
Inputs may be any that keep to these rules, and one draw needn't show every extreme that they name: In every micro-batch and stream the 8 lengths sum to 2048, and the largest is exactly 1024. `deal_order`: for every micro-batch and stream, a permutation of the 2048 places. Dealt place p holds a token of initial places b * 128 to (b + 1) * 128 - 1, with b = (p // 8) % 16.
All inputs are finite; a program needn't handle non-finite values.
Results may differ from a plain program's by a relative error of at most 0.015.
The roundings to bfloat16 on the way count: a program that leaves them out, or rounds other values in their place, can miss the bound.
Values may be sent and summed in bfloat16 or wider, within the bound.
No kernel may reach another device: no remote copies, remote signals or barrier semaphores. Data moves between devices by JAX's collectives and lax.ppermute only.
A program may use at most 448 MiB of HBM per device.

v0:
```python
import jax
import jax.numpy as jnp
from jax import lax
from jax.sharding import PartitionSpec as P

HEADS = 8


epsilon = 1e-05
negative = -1e30
scale_factor = 0.125
gelu_coeff = 0.7978845608028654
cubic_coeff = 0.044715


def as_sent(value):

    def short(part):
        return part.astype(jnp.bfloat16) if part.dtype == jnp.float32 else part

    return jax.tree.map(short, value)


def gelu(values):
    return (
        0.5
        * values
        * (1.0 + jnp.tanh(gelu_coeff * (values + cubic_coeff * values * values * values)))
    )


def gelu_slope(values):
    bent = jnp.tanh(gelu_coeff * (values + cubic_coeff * values * values * values))
    return 0.5 * (1.0 + bent) + 0.5 * values * (1.0 - bent * bent) * gelu_coeff * (
        1.0 + 3.0 * cubic_coeff * values * values
    )


def locate(anchor, seq_lens):
    seg_ends = jnp.cumsum(seq_lens)
    starts = seg_ends - seq_lens
    segment = jnp.sum((anchor[:, None] >= seg_ends[None, :]).astype(jnp.int32), axis=1)
    picked = segment[:, None] == jnp.arange(seq_lens.shape[0], dtype=jnp.int32)[None, :]
    seg_first = jnp.sum(jnp.where(picked, starts[None, :], 0), axis=1)
    return (segment, anchor - seg_first)


def normalize(values, gain_vec, shift_vec):
    center = values - jnp.mean(values, axis=-1, keepdims=True)
    inv_std = lax.rsqrt(jnp.mean(center * center, axis=-1, keepdims=True) + epsilon)
    normed = center * inv_std
    return (normed * gain_vec + shift_vec, normed, inv_std)


def normalize_back(grad_in, normed, inv_std, gain_vec):
    scaled = grad_in * gain_vec
    grad_z = inv_std * (
        scaled
        - jnp.mean(scaled, axis=-1, keepdims=True)
        - normed * jnp.mean(scaled * normed, axis=-1, keepdims=True)
    )
    return (grad_z, jnp.sum(grad_in * normed, axis=0), jnp.sum(grad_in, axis=0))


def project(left_side, right_side):
    return jnp.dot(left_side, right_side, preferred_element_type=jnp.float32)


def project_back(left_side, right_side):
    return lax.dot_general(
        left_side, right_side, (((0,), (0,)), ((), ())), preferred_element_type=jnp.float32
    )


def project_trans(left_side, right_side):
    return lax.dot_general(
        left_side, right_side, (((1,), (1,)), ((), ())), preferred_element_type=jnp.float32
    )


def masked_scores(query_heads, key_heads, query_seg, query_orig, tile_seg, tile_orig):
    raw_scores = (
        jnp.einsum("qhd,khd->hqk", query_heads, key_heads, preferred_element_type=jnp.float32)
        * scale_factor
    )
    allowed = (query_seg[:, None] == tile_seg[None, :]) & (
        tile_orig[None, :] <= query_orig[:, None]
    )
    return jnp.where(allowed[None], raw_scores, negative)


def split_tiles(values, tile_count):
    return values.reshape((tile_count, values.shape[0] // tile_count) + values.shape[1:])


def make_tiles(key_heads, value_heads, key_seg, key_orig):
    tile_count = max(1, key_heads.shape[0] // 2048)
    return (
        split_tiles(key_heads, tile_count),
        split_tiles(value_heads, tile_count),
        split_tiles(key_seg, tile_count),
        split_tiles(key_orig, tile_count),
    )


def attend_forward(query_heads, key_tiles, query_seg, query_orig):
    head_count, tok_rows = (query_heads.shape[1], query_heads.shape[0])

    def stats_step(carry_in, key_tile):
        run_max, run_sum = carry_in
        scores = masked_scores(
            query_heads, key_tile[0], query_seg, query_orig, key_tile[2], key_tile[3]
        )
        new_max = jnp.maximum(run_max, jnp.max(scores, axis=-1))
        run_sum = run_sum * jnp.exp(run_max - new_max) + jnp.sum(
            jnp.exp(scores - new_max[..., None]), axis=-1
        )
        return ((new_max, run_sum), None)

    start_stats = (
        jnp.full((head_count, tok_rows), negative, jnp.float32),
        jnp.zeros((head_count, tok_rows), jnp.float32),
    )
    (run_max, run_sum), unused = lax.scan(stats_step, start_stats, key_tiles)
    log_total = run_max + jnp.log(run_sum)

    def value_step(running, key_tile):
        scores = masked_scores(
            query_heads, key_tile[0], query_seg, query_orig, key_tile[2], key_tile[3]
        )
        attn_probs = jnp.exp(scores - log_total[..., None]).astype(jnp.bfloat16)
        running = running + jnp.einsum(
            "hqk,khd->qhd", attn_probs, key_tile[1], preferred_element_type=jnp.float32
        )
        return (running, None)

    attended, unused = lax.scan(value_step, jnp.zeros(query_heads.shape, jnp.float32), key_tiles)
    return (attended, log_total)


def attend_backward(query_heads, key_tiles, query_seg, query_orig, log_total, grad_heads):
    head_count, tok_rows = (query_heads.shape[1], query_heads.shape[0])

    def delta_step(delta_sum, key_tile):
        scores = masked_scores(
            query_heads, key_tile[0], query_seg, query_orig, key_tile[2], key_tile[3]
        )
        attn_probs = jnp.exp(scores - log_total[..., None])
        grad_probs = jnp.einsum(
            "qhd,khd->hqk", grad_heads, key_tile[1], preferred_element_type=jnp.float32
        )
        grad_value = None
        grad_value = jnp.einsum(
            "hqk,qhd->khd",
            attn_probs.astype(jnp.bfloat16),
            grad_heads,
            preferred_element_type=jnp.float32,
        )
        return (delta_sum + jnp.sum(attn_probs * grad_probs, axis=-1), grad_value)

    row_delta, value_parts = lax.scan(
        delta_step, jnp.zeros((head_count, tok_rows), jnp.float32), key_tiles
    )

    def score_step(grad_query, key_tile):
        scores = masked_scores(
            query_heads, key_tile[0], query_seg, query_orig, key_tile[2], key_tile[3]
        )
        attn_probs = jnp.exp(scores - log_total[..., None])
        grad_probs = jnp.einsum(
            "qhd,khd->hqk", grad_heads, key_tile[1], preferred_element_type=jnp.float32
        )
        grad_scores = (attn_probs * (grad_probs - row_delta[..., None])).astype(jnp.bfloat16)
        grad_query = (
            grad_query
            + jnp.einsum(
                "hqk,khd->qhd", grad_scores, key_tile[0], preferred_element_type=jnp.float32
            )
            * scale_factor
        )
        grad_key = None
        grad_key = (
            jnp.einsum("hqk,qhd->khd", grad_scores, query_heads, preferred_element_type=jnp.float32)
            * scale_factor
        )
        return (grad_query, grad_key)

    grad_query, key_parts = lax.scan(
        score_step, jnp.zeros(query_heads.shape, jnp.float32), key_tiles
    )
    return (grad_query, key_parts, value_parts, row_delta)


def shards(
    tokens,
    cotangent,
    lengths,
    deal_order,
    w_query,
    w_key,
    w_value,
    w_out,
    w_up,
    w_down,
    b_query,
    b_value,
    b_out,
    b_up,
    b_down,
    gain_one,
    shift_one,
    gain_two,
    shift_two,
    positions,
):
    tok_rows = tokens.shape[2]
    feat_width = tokens.shape[3]
    rank_count = lax.axis_size("ctx")
    my_rank = lax.axis_index("ctx")
    slot_rows = max(1, tok_rows // rank_count)
    unit_count = tok_rows // slot_rows
    peers = jnp.arange(rank_count, dtype=jnp.int32)
    within = jnp.arange(slot_rows, dtype=jnp.int32)
    send_offset = (my_rank - peers * unit_count) % rank_count
    send_valid = (send_offset < unit_count)[:, None] & (within[None, :] >= 0)
    send_places = (peers * unit_count + send_offset)[:, None] * slot_rows + within[None, :]
    send_places = jnp.where(send_valid, send_places, 0).reshape(rank_count * slot_rows)
    send_mask = send_valid.reshape(rank_count * slot_rows, 1)
    dealt_global = my_rank * tok_rows + jnp.arange(tok_rows, dtype=jnp.int32)
    recv_rows = dealt_global // slot_rows % rank_count * slot_rows + dealt_global % slot_rows
    back_offset = (peers - my_rank * unit_count) % rank_count
    back_valid = (back_offset < unit_count)[:, None] & (within[None, :] >= 0)
    back_places = back_offset[:, None] * slot_rows + within[None, :]
    back_places = jnp.where(back_valid, back_places, 0).reshape(rank_count * slot_rows)
    back_mask = back_valid.reshape(rank_count * slot_rows, 1)
    attn_local = (
        w_query,
        w_key,
        w_value,
        w_out,
        b_query,
        b_value,
        b_out,
        gain_one,
        shift_one,
        positions,
    )
    ffn_local = (w_up, w_down, b_up, b_down, gain_two, shift_two)
    outputs_all = []
    returned_all = []
    summed = None
    for micro_idx in range(tokens.shape[0]):
        order_row = deal_order[micro_idx, 0]
        seq_lens = lengths[micro_idx, 0]
        sent_rows = jnp.where(
            send_mask[:, 0], jnp.take(order_row, send_places, axis=0) - my_rank * tok_rows, 0
        )
        outgoing = jnp.where(
            send_mask,
            jnp.take(tokens[micro_idx, 0], sent_rows, axis=0),
            jnp.zeros((), jnp.bfloat16),
        )
        arrived = lax.all_to_all(outgoing, "ctx", split_axis=0, concat_axis=0, tiled=True)
        dealt_rows = jnp.take(arrived, recv_rows, axis=0)
        query_orig = lax.dynamic_slice_in_dim(order_row, my_rank * tok_rows, tok_rows)
        query_seg, query_place = locate(query_orig, seq_lens)
        key_seg = locate(order_row, seq_lens)[0]
        (
            w_query_all,
            w_key_all,
            w_value_all,
            w_out_all,
            b_query_all,
            b_value_all,
            b_out_all,
            gain_one_all,
            shift_one_all,
            positions_all,
        ) = (
            lax.all_gather(attn_local[0], "fsdp", axis=0, tiled=True),
            lax.all_gather(attn_local[1], "fsdp", axis=0, tiled=True),
            lax.all_gather(attn_local[2], "fsdp", axis=0, tiled=True),
            lax.all_gather(attn_local[3], "fsdp", axis=0, tiled=True),
            lax.all_gather(attn_local[4], "fsdp", axis=0, tiled=True),
            lax.all_gather(attn_local[5], "fsdp", axis=0, tiled=True),
            lax.all_gather(attn_local[6], "fsdp", axis=0, tiled=True),
            lax.all_gather(attn_local[7], "fsdp", axis=0, tiled=True),
            lax.all_gather(attn_local[8], "fsdp", axis=0, tiled=True),
            lax.all_gather(attn_local[9], "fsdp", axis=0, tiled=True),
        )
        w_up_all, w_down_all, b_up_all, b_down_all, gain_two_all, shift_two_all = (
            lax.all_gather(ffn_local[0], "fsdp", axis=0, tiled=True),
            lax.all_gather(ffn_local[1], "fsdp", axis=0, tiled=True),
            lax.all_gather(ffn_local[2], "fsdp", axis=0, tiled=True),
            lax.all_gather(ffn_local[3], "fsdp", axis=0, tiled=True),
            lax.all_gather(ffn_local[4], "fsdp", axis=0, tiled=True),
            lax.all_gather(ffn_local[5], "fsdp", axis=0, tiled=True),
        )
        hidden = dealt_rows.astype(jnp.float32) + jnp.take(
            positions_all, query_place, axis=0
        ).astype(jnp.float32)
        hidden_low = hidden.astype(jnp.bfloat16)
        query_low = (project(hidden_low, w_query_all) + b_query_all.astype(jnp.float32)).astype(
            jnp.bfloat16
        )
        key_low = project(hidden_low, w_key_all).astype(jnp.bfloat16)
        value_low = (project(hidden_low, w_value_all) + b_value_all.astype(jnp.float32)).astype(
            jnp.bfloat16
        )
        key_group, value_group = (
            lax.all_gather(key_low, "ctx", axis=0, tiled=True),
            lax.all_gather(value_low, "ctx", axis=0, tiled=True),
        )
        group_rows = key_group.shape[0]
        query_heads = query_low.reshape(tok_rows, HEADS, -1)
        key_tiles = make_tiles(
            key_group.reshape(group_rows, HEADS, -1),
            value_group.reshape(group_rows, HEADS, -1),
            key_seg,
            order_row,
        )
        attended, log_total = attend_forward(query_heads, key_tiles, query_seg, query_orig)
        att_low = attended.reshape(tok_rows, feat_width).astype(jnp.bfloat16)
        first_in = hidden + project(att_low, w_out_all) + b_out_all.astype(jnp.float32)
        first_norm, normed_one, inv_one = normalize(
            first_in, gain_one_all.astype(jnp.float32), shift_one_all.astype(jnp.float32)
        )
        first_low = first_norm.astype(jnp.bfloat16)
        up_pre = project(first_low, w_up_all) + b_up_all.astype(jnp.float32)
        gelu_low = gelu(up_pre).astype(jnp.bfloat16)
        second_in = first_norm + project(gelu_low, w_down_all) + b_down_all.astype(jnp.float32)
        final_norm, normed_two, inv_two = normalize(
            second_in, gain_two_all.astype(jnp.float32), shift_two_all.astype(jnp.float32)
        )
        outputs_all.append(final_norm.astype(jnp.bfloat16))
        grad_out = cotangent[micro_idx, 0].astype(jnp.float32)
        grad_second, g_gain_two, g_shift_two = normalize_back(
            grad_out, normed_two, inv_two, gain_two_all.astype(jnp.float32)
        )
        grad_ffn = grad_second.astype(jnp.bfloat16)
        g_w_down = project_back(gelu_low, grad_ffn)
        g_b_down = jnp.sum(grad_ffn.astype(jnp.float32), axis=0)
        grad_up = (project_trans(grad_ffn, w_down_all) * gelu_slope(up_pre)).astype(jnp.bfloat16)
        g_w_up = project_back(first_low, grad_up)
        g_b_up = jnp.sum(grad_up.astype(jnp.float32), axis=0)
        grad_first = grad_second + project_trans(grad_up, w_up_all)
        grad_mix, g_gain_one, g_shift_one = normalize_back(
            grad_first, normed_one, inv_one, gain_one_all.astype(jnp.float32)
        )
        grad_branch = grad_mix.astype(jnp.bfloat16)
        g_w_out = project_back(att_low, grad_branch)
        g_b_out = jnp.sum(grad_branch.astype(jnp.float32), axis=0)
        grad_att = project_trans(grad_branch, w_out_all).astype(jnp.bfloat16)
        grad_query, key_parts, value_parts, row_delta = attend_backward(
            query_heads,
            key_tiles,
            query_seg,
            query_orig,
            log_total,
            grad_att.reshape(tok_rows, HEADS, -1),
        )
        grad_key_sum, grad_value_sum = (
            lax.psum_scatter(
                key_parts.reshape(group_rows, feat_width), "ctx", scatter_dimension=0, tiled=True
            ),
            lax.psum_scatter(
                value_parts.reshape(group_rows, feat_width), "ctx", scatter_dimension=0, tiled=True
            ),
        )
        grad_query_low = grad_query.reshape(tok_rows, feat_width).astype(jnp.bfloat16)
        grad_key_low = grad_key_sum.astype(jnp.bfloat16)
        grad_value_low = grad_value_sum.astype(jnp.bfloat16)
        g_w_query = project_back(hidden_low, grad_query_low)
        g_b_query = jnp.sum(grad_query_low.astype(jnp.float32), axis=0)
        g_w_key = project_back(hidden_low, grad_key_low)
        g_w_value = project_back(hidden_low, grad_value_low)
        g_b_value = jnp.sum(grad_value_low.astype(jnp.float32), axis=0)
        grad_hidden = (
            grad_mix
            + project_trans(grad_query_low, w_query_all)
            + project_trans(grad_key_low, w_key_all)
            + project_trans(grad_value_low, w_value_all)
        )
        onehot = (
            query_place[:, None] == jnp.arange(positions_all.shape[0], dtype=jnp.int32)[None, :]
        ).astype(jnp.float32)
        g_positions = lax.dot_general(
            onehot,
            grad_hidden,
            (((0,), (0,)), ((), ())),
            precision=lax.Precision.HIGHEST,
            preferred_element_type=jnp.float32,
        )
        hidden_grad_low = grad_hidden.astype(jnp.bfloat16)
        going_back = jnp.where(
            back_mask, jnp.take(hidden_grad_low, back_places, axis=0), jnp.zeros((), jnp.bfloat16)
        )
        back_grad = lax.all_to_all(going_back, "ctx", split_axis=0, concat_axis=0, tiled=True)
        back_grad = jnp.where(send_mask, back_grad, jnp.zeros((), jnp.bfloat16))
        returned_all.append(
            jnp.zeros((tok_rows, feat_width), jnp.bfloat16).at[sent_rows].add(back_grad)
        )
        grad_terms = (
            g_w_query,
            g_w_key,
            g_w_value,
            g_w_out,
            g_w_up,
            g_w_down,
            g_b_query,
            g_b_value,
            g_b_out,
            g_b_up,
            g_b_down,
            g_gain_one,
            g_shift_one,
            g_gain_two,
            g_shift_two,
            g_positions,
        )
        summed = grad_terms if summed is None else jax.tree.map(jnp.add, summed, grad_terms)
    shares = jax.tree.map(
        lambda part: part.astype(jnp.float32),
        lax.psum_scatter(as_sent(summed), "fsdp", scatter_dimension=0, tiled=True),
    )
    totals = lax.psum(shares, "ctx")
    output = jnp.stack(outputs_all)[:, None]
    grad_tokens = jnp.stack(returned_all)[:, None]
    return (output, grad_tokens) + tuple(totals)


def solution(mesh):
    placed = (
        P(None, "fsdp", "ctx", None),
        P(None, "fsdp", "ctx", None),
        P(None, "fsdp", None),
        P(None, "fsdp", None),
        P("fsdp", None),
        P("fsdp", None),
        P("fsdp", None),
        P("fsdp", None),
        P("fsdp", None),
        P("fsdp", None),
        P("fsdp"),
        P("fsdp"),
        P("fsdp"),
        P("fsdp"),
        P("fsdp"),
        P("fsdp"),
        P("fsdp"),
        P("fsdp"),
        P("fsdp"),
        P("fsdp", None),
    )
    return jax.shard_map(
        shards,
        mesh=mesh,
        in_specs=placed,
        out_specs=(
            P(None, "fsdp", "ctx", None),
            P(None, "fsdp", "ctx", None),
            P("fsdp", None),
            P("fsdp", None),
            P("fsdp", None),
            P("fsdp", None),
            P("fsdp", None),
            P("fsdp", None),
            P("fsdp"),
            P("fsdp"),
            P("fsdp"),
            P("fsdp"),
            P("fsdp"),
            P("fsdp"),
            P("fsdp"),
            P("fsdp"),
            P("fsdp"),
            P("fsdp", None),
        ),
        check_vma=False,
    )
```

profile of v0, /device:TPU:16, one launch (start us, length us, event | category | flops | bytes accessed | tf_op | source)
XLA Modules:
  0.0 1146.1 jit_solution(16316901160239398401)
XLA Ops:
  15.8 7.2 all-to-all-start
  28.9 5.4 all-to-all-start.1
  81.3 24.6 %all-gather.20.cloned.1.call-done = bf16[2048,512]{1,0:T(8,128)(2,1)} async-done(((bf16[128,512]{1,0:T(8,128)(2,1)}), bf16[2048,512]{1,0:T(8,128)(2,1)}) %all-gather.20.cloned.1.call-update) | async-done | bytes 2097168 | tf_op jit(solution)/shard_map/all_gather | solution.py:311
  114.9 53.7 %all-gather.18.cloned.1.call-done = bf16[2048,512]{1,0:T(8,128)(2,1)} async-done(((bf16[128,512]{1,0:T(8,128)(2,1)}), bf16[2048,512]{1,0:T(8,128)(2,1)}) %all-gather.18.cloned.1.call-update) | async-done | bytes 2097168 | tf_op jit(solution)/shard_map/all_gather | solution.py:312
  172.5 6.8 convolution_convert_fusion.4
  179.3 51.4 %all-gather.28.cloned.1.call-done = bf16[2048,512]{1,0:T(8,128)(2,1)} async-done(((bf16[128,512]{1,0:T(8,128)(2,1)}), bf16[2048,512]{1,0:T(8,128)(2,1)}) %all-gather.28.cloned.1.call-update) | async-done | bytes 2097168 | tf_op jit(solution)/shard_map/all_gather | solution.py:311
  245.4 10.0 all-gather.24.cloned.1.call-done
  264.5 55.2 %all-gather.26.cloned.1.call-done = bf16[2048,512]{1,0:T(8,128)(2,1)} async-done(((bf16[128,512]{1,0:T(8,128)(2,1)}), bf16[2048,512]{1,0:T(8,128)(2,1)}) %all-gather.26.cloned.1.call-update) | async-done | bytes 2097168 | tf_op jit(solution)/shard_map/all_gather | solution.py:312
  323.9 6.3 convolution_convert_fusion.2
  345.7 7.4 multiply_reduce_fusion.1
  365.0 7.4 multiply_reduce_fusion
  379.2 7.8 fusion.95
  387.1 7.8 fusion.92
  422.4 29.5 %reduce-scatter.12.cloned.1.call-done = f32[128,512]{0,1:T(8,128)} async-done(((f32[2048,512]{0,1:T(8,128)}), f32[128,512]{0,1:T(8,128)}) %reduce-scatter.12.cloned.1.call-update) | async-done | bytes 262160 | tf_op jit(solution)/shard_map/reduce_scatter | solution.py:363
  453.2 95.8 %reduce-scatter.16.cloned.1.call-done = f32[128,512]{0,1:T(8,128)} async-done(((f32[2048,512]{0,1:T(8,128)}), f32[128,512]{0,1:T(8,128)}) %reduce-scatter.16.cloned.1.call-update) | async-done | bytes 262160 | tf_op jit(solution)/shard_map/reduce_scatter | solution.py:363
  554.8 91.1 %reduce-scatter.14.cloned.1.call-done = f32[128,512]{0,1:T(8,128)} async-done(((f32[2048,512]{0,1:T(8,128)}), f32[128,512]{0,1:T(8,128)}) %reduce-scatter.14.cloned.1.call-update) | async-done | bytes 262160 | tf_op jit(solution)/shard_map/reduce_scatter | solution.py:366
  647.3 95.7 %reduce-scatter.18.cloned.1.call-done = f32[128,512]{0,1:T(8,128)} async-done(((f32[2048,512]{0,1:T(8,128)}), f32[128,512]{0,1:T(8,128)}) %reduce-scatter.18.cloned.1.call-update) | async-done | bytes 262160 | tf_op jit(solution)/shard_map/reduce_scatter | solution.py:366
  755.2 11.5 reduce-scatter.26.cloned.1.call-done
  766.6 13.5 %reduce-scatter.28.cloned.1.call-done = bf16[256,2048]{1,0:T(8,128)(2,1)} async-done(((bf16[512,2048]{1,0:T(8,128)(2,1)}), bf16[256,2048]{1,0:T(8,128)(2,1)}) %reduce-scatter.28.cloned.1.call-update) | async-done | bytes 1048592 | tf_op jit(solution)/shard_map/reduce_scatter | solution.py:424
  780.1 13.6 %reduce-scatter.30.cloned.1.call-done = bf16[1024,512]{1,0:T(8,128)(2,1)} async-done(((bf16[2048,512]{1,0:T(8,128)(2,1)}), bf16[1024,512]{1,0:T(8,128)(2,1)}) %reduce-scatter.30.cloned.1.call-update) | async-done | bytes 1048592 | tf_op jit(solution)/shard_map/reduce_scatter | solution.py:424
  796.5 7.0 all-to-all-start.3
  809.4 5.5 all-to-all-start.2
  823.2 6.6 reduce-scatter.32.cloned.1.call-done
  829.8 309.2 %all-reduce.12 = (f32[256,512]{1,0:T(8,128)}, f32[256,512]{1,0:T(8,128)}, f32[256,512]{1,0:T(8,128)}, f32[256,512]{1,0:T(8,128)}, f32[256,2048]{1,0:T(8,128)}, /...) all-reduce(bf16[256,512]{1,0:T(8,128)(2,1)S(1)} %copy-done.63, ...), channel_id=1, replica_groups=mesh['ctx'=16,'fsdp'=2] {'ctx'}, use_global_device_ids=true, to_apply=%region_37.41 | all-reduce | flops 1838080 | bytes 11034624 | tf_op jit(solution)/shard_map/psum | solution.py:426
  (510 shorter events, 198.4 us)
Async XLA Ops:
  15.8 13.1 %all-to-all-start = ((bf16[16,8,512]{2,1,0:T(8,128)(2,1)}), bf16[16,8,512]{2,1,0:T(8,128)(2,1)S(1)}, u32[]{:S(2)}, u32[]{:S(2)}) async-start(bf16[16,8,512]{2,1,0:T(8,128)(2,1)} %get-tuple-element.441), calls=%async_computation | async-start | bytes 262144 | tf_op jit(solution)/shard_map/all_to_all | solution.py:263
  23.0 18.2 %all-gather.16.cloned.1.call-start = ((), (), s32[]{:S(2)}) async-start(), calls=%async_computation.15 | async-start | bytes 1572864 | tf_op jit(solution)/shard_map/all_gather | solution.py:289
  28.9 11.3 all-to-all-start.1
  34.3 71.6 %all-gather.20.cloned.1.call-start = ((), (), s32[]{:S(2)}) async-start(), calls=%async_computation.17 | async-start | bytes 2228224 | tf_op jit(solution)/shard_map/all_gather | solution.py:311
  47.0 121.6 %all-gather.18.cloned.1.call-start = ((), (), s32[]{:S(2)}) async-start(), calls=%async_computation.16 | async-start | bytes 2228224 | tf_op jit(solution)/shard_map/all_gather | solution.py:312
  52.0 178.7 %all-gather.28.cloned.1.call-start = ((), (), s32[]{:S(2)}) async-start(), calls=%async_computation.21 | async-start | bytes 2228224 | tf_op jit(solution)/shard_map/all_gather | solution.py:311
  53.0 189.3 %all-gather.22.cloned.1.call-start = ((), (), s32[]{:S(2)}) async-start(), calls=%async_computation.18 | async-start | bytes 3145728 | tf_op jit(solution)/shard_map/all_gather | solution.py:292
  53.5 201.9 %all-gather.24.cloned.1.call-start = ((), (), s32[]{:S(2)}) async-start(), calls=%async_computation.19 | async-start | bytes 3145728 | tf_op jit(solution)/shard_map/all_gather | solution.py:293
  54.1 265.6 %all-gather.26.cloned.1.call-start = ((), (), s32[]{:S(2)}) async-start(), calls=%async_computation.20 | async-start | bytes 2228224 | tf_op jit(solution)/shard_map/all_gather | solution.py:312
  80.7 371.3 %reduce-scatter.12.cloned.1.call-start = ((), (), s32[]{:S(2)}) async-start(), calls=%async_computation.22 | async-start | bytes 4456448 | tf_op jit(solution)/shard_map/reduce_scatter | solution.py:363
  359.1 189.9 %reduce-scatter.16.cloned.1.call-start = ((), (), s32[]{:S(2)}) async-start(), calls=%async_computation.24 | async-start | bytes 4456448 | tf_op jit(solution)/shard_map/reduce_scatter | solution.py:363
  378.2 267.7 %reduce-scatter.14.cloned.1.call-start = ((), (), s32[]{:S(2)}) async-start(), calls=%async_computation.23 | async-start | bytes 4456448 | tf_op jit(solution)/shard_map/reduce_scatter | solution.py:366
  387.0 355.9 %reduce-scatter.18.cloned.1.call-start = ((), (), s32[]{:S(2)}) async-start(), calls=%async_computation.25 | async-start | bytes 4456448 | tf_op jit(solution)/shard_map/reduce_scatter | solution.py:366
  394.9 360.3 %reduce-scatter.20.cloned.1.call-start = ((), (), s32[]{:S(2)}) async-start(), calls=%async_computation.26 | async-start | bytes 786432 | tf_op jit(solution)/shard_map/reduce_scatter | solution.py:424
  403.2 363.4 %reduce-scatter.26.cloned.1.call-start = ((), (), s32[]{:S(2)}) async-start(), calls=%async_computation.29 | async-start | bytes 786432 | tf_op jit(solution)/shard_map/reduce_scatter | solution.py:424
  406.5 373.6 %reduce-scatter.28.cloned.1.call-start = ((), (), s32[]{:S(2)}) async-start(), calls=%async_computation.30 | async-start | bytes 3145728 | tf_op jit(solution)/shard_map/reduce_scatter | solution.py:424
  411.3 382.4 %reduce-scatter.30.cloned.1.call-start = ((), (), s32[]{:S(2)}) async-start(), calls=%async_computation.31 | async-start | bytes 3145728 | tf_op jit(solution)/shard_map/reduce_scatter | solution.py:424
  415.5 407.7 %reduce-scatter.22.cloned.1.call-start = ((), (), s32[]{:S(2)}) async-start(), calls=%async_computation.27 | async-start | bytes 786432 | tf_op jit(solution)/shard_map/reduce_scatter | solution.py:424
  551.1 195.4 %copy-start.11 = (bf16[512,512]{1,0:T(8,128)(2,1)S(1)}, bf16[512,512]{1,0:T(8,128)(2,1)}, u32[]{:S(2)}) copy-start(bf16[512,512]{1,0:T(8,128)(2,1)} %copy-done.10) | copy-start | bytes 1572868
  551.1 272.1 %reduce-scatter.24.cloned.1.call-start = ((), (), s32[]{:S(2)}) async-start(), calls=%async_computation.28 | async-start | bytes 786432 | tf_op jit(solution)/shard_map/reduce_scatter | solution.py:424
  553.8 193.1 %copy-start.53 = (f32[128,512]{0,1:T(8,128)S(1)}, f32[128,512]{0,1:T(8,128)}, u32[]{:S(2)}) copy-start(f32[128,512]{0,1:T(8,128)} %reduce-scatter.16.cloned.1.call-done) | copy-start | bytes 786436
  745.1 84.7 %reduce-scatter.32.cloned.1.call-start = ((), (), s32[]{:S(2)}) async-start(), calls=%async_computation.32 | async-start | bytes 1572864 | tf_op jit(solution)/shard_map/reduce_scatter | solution.py:424
  796.5 13.0 %all-to-all-start.3 = ((bf16[16,8,512]{2,1,0:T(8,128)(2,1)}), bf16[16,8,512]{2,1,0:T(8,128)(2,1)S(1)}, u32[]{:S(2)}, u32[]{:S(2)}) async-start(bf16[16,8,512]{2,1,0:T(8,128)(2,1)} %get-tuple-element.432), calls=%async_computation.7 | async-start | bytes 262144 | tf_op jit(solution)/shard_map/all_to_all | solution.py:398
  809.4 11.5 all-to-all-start.2
  (132 other events, 2174.1 us)
Sparse Core Ops, SparseCore 0:
  25.4 10.1 all-gather.15
  47.1 58.7 all-gather.19
  109.2 59.3 all-gather.17
  171.2 59.3 all-gather.27
  232.0 10.1 all-gather.21
  243.6 11.7 all-gather.23
  258.8 60.9 all-gather.25
  359.2 92.6 reduce-scatter.11
  454.3 94.6 reduce-scatter.15
  551.1 94.7 reduce-scatter.13
  648.2 94.7 reduce-scatter.17
  745.6 9.5 reduce-scatter.19
  757.5 9.0 reduce-scatter.25
  769.3 10.7 reduce-scatter.27
  782.9 10.7 reduce-scatter.29
  796.4 9.1 reduce-scatter.21
  808.3 9.0 reduce-scatter.23
  820.1 9.6 reduce-scatter.31
where the time goes:
time: 1160 us; the launch traced here: 1150 us
  waiting for transfers between devices  575 us (50%)
  blocking collectives  337 us (29%)
  matrix products  111 us (10%)
  local copies, waits for them, and re-layouts  41.8 us (4%)
  other arithmetic  36.9 us (3%)
  starting transfers between devices  26.8 us (2%)
  between operations  17.8 us (2%)
    psum x1, blocking collectives, shards(): totals = lax.psum(shares, 'ctx')  309 us
    reduce_scatter x2, waiting for transfers between devices, shards(): lax.psum_scatter(value_parts.reshape(group_rows, feat_width), 'ctx', scat...  187 us
    reduce_scatter x2, waiting for transfers between devices, shards(): lax.psum_scatter(key_parts.reshape(group_rows, feat_width), 'ctx', scatte...  125 us
    all_gather x2, waiting for transfers between devices, shards(): lax.all_gather(value_low, 'ctx', axis=0, tiled=True)  109 us
    all_gather x2, waiting for transfers between devices, shards(): lax.all_gather(key_low, 'ctx', axis=0, tiled=True)  75.9 us
    reduce_scatter x7, waiting for transfers between devices, shards(): lax.psum_scatter(as_sent(summed), 'fsdp', scatter_dimension=0, tiled=True)  48.5 us
  transfers between devices with their start and end apart: 22, of which 19 were waited for; matrix products, arithmetic and copies ran while one was open for 11% of the time, Pallas kernels for 0%

commit v1 on v0

v1 whole, which is shorter than its diff:
```python
import functools

import jax
import jax.numpy as jnp
from jax import lax
from jax.experimental import pallas as pl
from jax.experimental.pallas import tpu as pltpu
from jax.sharding import PartitionSpec as P

HEADS = 8
epsilon = 1e-05
gelu_coeff = 0.7978845608028654
cubic_coeff = 0.044715
BF = jnp.bfloat16
F32 = jnp.float32
SWAP = ((0, 1), (1, 0))
BOTH = ("ctx", "fsdp")
FAR = 1 << 30


def dot(a, b):
    return jnp.dot(a, b, preferred_element_type=F32)


def dot_tn(a, b):
    return lax.dot_general(a, b, (((0,), (0,)), ((), ())), preferred_element_type=F32)


def dot_nt(a, b):
    return lax.dot_general(a, b, (((1,), (1,)), ((), ())), preferred_element_type=F32)


def gelu_parts(u):
    inner = gelu_coeff * (u + cubic_coeff * u * u * u)
    bent = jnp.tanh(inner)
    value = 0.5 * u * (1.0 + bent)
    slope = 0.5 * (1.0 + bent) + 0.5 * u * (1.0 - bent * bent) * gelu_coeff * (
        1.0 + 3.0 * cubic_coeff * u * u
    )
    return value, slope


def normalize(z):
    center = z - jnp.mean(z, axis=-1, keepdims=True)
    inv = lax.rsqrt(jnp.mean(center * center, axis=-1, keepdims=True) + epsilon)
    return center * inv, inv


def normalize_back(t, normed, inv):
    return inv * (
        t
        - jnp.mean(t, axis=-1, keepdims=True)
        - normed * jnp.mean(t * normed, axis=-1, keepdims=True)
    )


def first_places(info, spots):
    first, end = jnp.zeros_like(spots), 0
    for n in range(3, info.shape[0]):
        end = end + info[n]
        first = first + jnp.where(spots >= end, info[n], 0)
    return first


def lay(info, whole, own, other):
    n = own.shape[0]
    mine = info[0] == 0
    whole[0:n, :] = jnp.where(mine, own[...], other[...])
    whole[n : 2 * n, :] = jnp.where(mine, other[...], own[...])


def full_row(info, own, other, at, count=1):
    mine = info[0] == 0
    rows = [x[at + n : at + n + 1, :] for x in (own, other) for n in range(count)]
    first = [jnp.where(mine, rows[n], rows[count + n]) for n in range(count)]
    second = [jnp.where(mine, rows[count + n], rows[n]) for n in range(count)]
    return jnp.concatenate(first + second, axis=1)


def stack_vectors(vectors, width):
    row, at = iota((16, width), 0), 0
    table = jnp.zeros((16, width), F32)
    for x in vectors:
        for n in range(x.shape[0] // width):
            part = x[n * width : n * width + width].astype(F32)
            table = jnp.where(row == at, part[None, :], table)
            at += 1
    return table


def iota(shape, axis):
    return lax.broadcasted_iota(jnp.int32, shape, axis)


def params(limit=56):
    return pltpu.CompilerParams(vmem_limit_bytes=limit * 1024 * 1024)


def lasting(us):
    return pl.CostEstimate(flops=us, transcendentals=0, bytes_accessed=us)


def fixed(shape):
    return pl.BlockSpec(shape, lambda *_: (0,) * len(shape), pipeline_mode=pl.Buffered(1))


def paired(rows):
    return pl.BlockSpec((rows, 128), lambda p, *_: (0, p))


def project_kernel(info, *refs, blocks, offset, own):
    toks = refs[:blocks]
    pos_a, pos_b, wk_a, wk_b, wv_a, wv_b, wq_a, wq_b, vec_a, vec_b = refs[blocks : blocks + 10]
    outs = refs[blocks + 10 :]
    k_ref, v_ref = outs[:2]
    wk, wv, wq, tok = outs[-4:]
    step = pl.program_id(0)
    rows = tok.shape[0]

    @pl.when(step == 0)
    def _():
        lay(info, wk, wk_a, wk_b)
        lay(info, wv, wv_a, wv_b)
        if own:
            lay(info, wq, wq_a, wq_b)

    for n in range(blocks):

        @pl.when(step == n)
        def _():
            tok[...] = toks[n][...]

    spots = info[1] + offset + step * rows + iota((rows, 1), 0)
    place = spots - first_places(info, spots)
    hidden = tok[...].astype(F32)
    half = pos_a.shape[0]
    chunk = min(half, 512)
    for part, begin in ((pos_a, info[0] * half), (pos_b, (1 - info[0]) * half)):
        for at in range(0, half, chunk):
            hot = (place - begin - at == iota((rows, chunk), 1)).astype(F32).astype(BF)
            hidden = hidden + dot(hot, part[at : at + chunk, :])
    low = hidden.astype(BF)
    k_ref[...] = dot(low, wk[...]).astype(BF)
    v_ref[...] = (dot(low, wv[...]) + full_row(info, vec_a, vec_b, 7)).astype(BF)
    if own:
        q_ref, hidden_ref, low_ref = outs[2:5]
        q_ref[...] = ((dot(low, wq[...]) + full_row(info, vec_a, vec_b, 6)).astype(BF).astype(F32) * 0.125).astype(BF)
        hidden_ref[...] = hidden
        low_ref[...] = low


def project(info, toks, offset, own, pos, wk, wv, wq, vec):
    rows, width = toks[0].shape
    blocks = len(toks)
    tall = pl.BlockSpec((rows, width), lambda n, *_: (n, 0))
    flat = jax.ShapeDtypeStruct((rows * blocks, width), BF)
    square = pltpu.VMEM((width, width), BF)
    args = (*toks, *pos, *wk, *wv, *wq, *vec)
    return pl.pallas_call(
        functools.partial(project_kernel, blocks=blocks, offset=offset, own=own),
        grid_spec=pltpu.PrefetchScalarGridSpec(
            num_scalar_prefetch=1,
            grid=(blocks,),
            in_specs=[fixed(x.shape) for x in args],
            out_specs=[tall] * (5 if own else 2),
            scratch_shapes=[square, square, square, pltpu.VMEM((rows, width), BF)],
        ),
        out_shape=[flat] * 3 + [jax.ShapeDtypeStruct((rows, width), F32), flat] if own else [flat] * 2,
        compiler_params=params(),
        cost_estimate=lasting(2 * blocks + 2),
        name="project",
    )(info, *args)


def stat_rows(table):
    high = table.astype(BF).astype(F32)
    middle = (table - high).astype(BF).astype(F32)
    low = table - high - middle
    count = table.shape[1] // 128
    rows = [
        part[half : half + 1, 128 * n : 128 * n + 128]
        for part in (high, middle, low)
        for half in range(2)
        for n in range(count)
    ]
    rows.append(jnp.zeros((16 - len(rows), 128), F32))
    return jnp.concatenate(rows, axis=0).astype(BF)


def stat_row(rows16, half, queries):
    count = queries // 128
    wide = rows16.astype(F32)
    total = wide[0 : 2 * count] + wide[2 * count : 4 * count] + wide[4 * count : 6 * count]
    return jnp.concatenate([total[half * count + n : half * count + n + 1] for n in range(count)], axis=1)


def chunks_of(cols):
    step = cols if cols <= 2048 else 768
    return [slice(at, min(at + step, cols)) for at in range(0, cols, step)]


def bias_scratch(rows, cols):
    return pltpu.VMEM((rows, cols) if len(chunks_of(cols)) == 1 else (8, 128), F32)


def query_bias(info, rows, before, chunk):
    spots = info[1] + iota((rows, 1), 0)
    first = first_places(info, spots) - (info[1] - before)
    last = iota((rows, 1), 0) + before
    col = iota((rows, chunk.stop - chunk.start), 1) + chunk.start
    return jnp.where((col >= first) & (col <= last), 0.0, -1e30)


def key_bias(info, rows, chunk):
    spots = info[1] + chunk.start + iota((1, chunk.stop - chunk.start), 1)
    first = jnp.where(spots < info[2], first_places(info, spots) - info[1], FAR)
    shape = (rows, chunk.stop - chunk.start)
    row = iota(shape, 0)
    return jnp.where((row >= first) & (row <= iota(shape, 1) + chunk.start), 0.0, -1e30)


def forward_kernel(info, q_ref, kp_ref, k_ref, vp_ref, v_ref, a_ref, exact_ref, log_ref, stat_ref, bias, keys, values):
    rows, before = q_ref.shape[0], kp_ref.shape[0]

    chunks = chunks_of(keys.shape[0])
    make_bias = functools.partial(query_bias, info, rows, before)

    @pl.when(pl.program_id(0) == 0)
    def _():
        if len(chunks) == 1:
            bias[...] = make_bias(chunks[0])

    keys[0:before, :] = kp_ref[...]
    keys[before:, :] = k_ref[...]
    values[0:before, :] = vp_ref[...]
    values[before:, :] = v_ref[...]
    logs = []
    for half in range(2):
        lanes = slice(64 * half, 64 * half + 64)


        def scores_of(chunk):
            mask = bias[...] if len(chunks) == 1 else make_bias(chunk)
            return dot_nt(q_ref[:, lanes], keys[chunk, lanes]) + mask

        if len(chunks) == 1:
            scores = scores_of(chunks[0])
            top = jnp.max(scores, axis=1, keepdims=True)
            raised = jnp.exp(scores - top)
            total = jnp.sum(raised, axis=1, keepdims=True)
            probs = raised * (1.0 / total)
            low = probs.astype(BF)
            rest = (probs - low.astype(F32)).astype(BF)
            attended = dot(low, values[:, lanes])
            exact = attended + dot(rest, values[:, lanes])
        else:
            top = jnp.full((rows, 1), -1e30, F32)
            for chunk in chunks:
                top = jnp.maximum(top, jnp.max(scores_of(chunk), axis=1, keepdims=True))
            total = jnp.zeros((rows, 1), F32)
            for chunk in chunks:
                total = total + jnp.sum(jnp.exp(scores_of(chunk) - top), axis=1, keepdims=True)
            attended, exact = jnp.zeros((rows, 64), F32), jnp.zeros((rows, 64), F32)
            for chunk in chunks:
                probs = jnp.exp(scores_of(chunk) - top) * (1.0 / total)
                low = probs.astype(BF)
                rest = (probs - low.astype(F32)).astype(BF)
                attended = attended + dot(low, values[chunk, lanes])
                exact = exact + dot(rest, values[chunk, lanes])
            exact = exact + attended
        a_ref[:, lanes] = attended.astype(BF)
        exact_ref[:, lanes] = exact
        logs.append(jnp.broadcast_to(top + jnp.log(total), (rows, 64)))
    wide = jnp.concatenate(logs, axis=1)
    log_ref[...] = wide
    turned = wide.T
    stat_ref[...] = stat_rows(jnp.concatenate([turned[0:1], turned[64:65]], axis=0))


def attend_forward(info, q, kp, k, vp, v):
    rows, width = q.shape
    before = kp.shape[0]
    cols = before + rows
    return pl.pallas_call(
        forward_kernel,
        grid_spec=pltpu.PrefetchScalarGridSpec(
            num_scalar_prefetch=1,
            grid=(width // 128,),
            in_specs=[paired(x.shape[0]) for x in (q, kp, k, vp, v)],
            out_specs=[paired(rows), paired(rows), paired(rows), paired(16)],
            scratch_shapes=[
                bias_scratch(rows, cols),
                pltpu.VMEM((cols, 128), BF),
                pltpu.VMEM((cols, 128), BF),
            ],
        ),
        out_shape=[
            jax.ShapeDtypeStruct((rows, width), BF),
            jax.ShapeDtypeStruct((rows, width), F32),
            jax.ShapeDtypeStruct((rows, width), F32),
            jax.ShapeDtypeStruct((16, width), BF),
        ],
        compiler_params=params(),
        cost_estimate=lasting(12),
        name="attend_forward",
    )(info, q, kp, k, vp, v)


def ffn_kernel(
    info, a_ref, exact_ref, stat_ref, hidden_ref, arrived_ref, row_ref, col_ref, wo_a, wo_b, wu_a, wu_b, wd_a, wd_b, vec_a, vec_b,
    leaving_ref, msg_ref, dz1_ref, active_ref, df_ref, h1_ref, du_ref, do_ref, sums_ref,
    wo, wu, wd, slopes, stats,
):
    lay(info, wo, wo_a, wo_b)
    lay(info, wu, wu_a, wu_b)
    lay(info, wd, wd_a, wd_b)
    rows, width = hidden_ref.shape
    hidden_units = wu.shape[1]
    bo, bd, g1, s1, g2, s2 = (full_row(info, vec_a, vec_b, n) for n in range(6))
    bu = full_row(info, vec_a, vec_b, 8, hidden_units // width)
    pick = (iota((rows, rows), 0) == row_ref[...]).astype(F32).astype(BF)
    pick_back = (col_ref[...] == iota((rows, rows), 1)).astype(F32).astype(BF)
    dy = dot(pick, arrived_ref[...])

    n1, r1 = normalize(hidden_ref[...] + dot(a_ref[...], wo[...]) + bo)
    h1 = n1 * g1 + s1
    h1_low = h1.astype(BF)
    h1_ref[...] = h1_low
    z2 = h1 + bd
    for at in range(0, hidden_units, width):
        block = slice(at, at + width)
        value, slope = gelu_parts(dot(h1_low, wu[:, block]) + bu[:, block])
        slopes[:, block] = slope
        low = value.astype(BF)
        active_ref[:, block] = low
        z2 = z2 + dot(low, wd[block, :])
    n2, r2 = normalize(z2)
    leaving_ref[...] = dot(pick_back, (n2 * g2 + s2).astype(BF)).astype(BF)

    def add(x):
        return jnp.sum(x, axis=0, keepdims=True)

    dz2 = normalize_back(dy * g2, n2, r2)
    df = dz2.astype(BF)
    df_ref[...] = df
    sums_ref[0:1, :] = add(df.astype(F32))
    sums_ref[3:4, :] = add(dy * n2)
    sums_ref[4:5, :] = add(dy)
    dh1 = dz2
    for at in range(0, hidden_units, width):
        block = slice(at, at + width)
        du = (dot_nt(df, wd[block, :]) * slopes[:, block]).astype(BF)
        du_ref[:, block] = du
        n = 7 + at // width
        sums_ref[n : n + 1, :] = add(du.astype(F32))
        dh1 = dh1 + dot_nt(du, wu[:, block])
    dz1 = normalize_back(dh1 * g1, n1, r1)
    dz1_ref[...] = dz1
    sums_ref[1:2, :] = add(dh1 * n1)
    sums_ref[2:3, :] = add(dh1)
    do = dz1.astype(BF)
    do_ref[...] = do
    sums_ref[5:6, :] = add(do.astype(F32))
    sums_ref[6:7, :] = jnp.zeros((1, width), F32)
    sums_ref[11:16, :] = jnp.zeros((5, width), F32)
    da = dot_nt(do, wo[...]).astype(BF)
    msg_ref[0:rows, :] = da
    terms = da.astype(F32) * exact_ref[...]
    head = iota((HEADS, width), 0)
    lane = iota((HEADS, width), 1) // (width // HEADS)
    ones = (head == lane).astype(F32).astype(BF)
    delta = jnp.zeros((HEADS, rows), F32)
    for _ in range(3):
        part = terms.astype(BF)
        terms = terms - part.astype(F32)
        delta = delta + dot_nt(ones, part)
    for p in range(HEADS // 2):
        stats[:, 128 * p : 128 * p + 128] = stat_rows(delta[2 * p : 2 * p + 2, :])
    msg_ref[rows : rows + 16, :] = stat_ref[...]
    msg_ref[rows + 16 : rows + 32, :] = stats[...]


def feed_forward(info, a, exact, log_stats, hidden, arrived, mine, wo, wu, wd, vec):
    rows, width = hidden.shape
    units = wu[0].shape[1]
    args = (a, exact, log_stats, hidden, arrived, mine.reshape(1, rows), mine.reshape(rows, 1), *wo, *wu, *wd, *vec)
    low = jax.ShapeDtypeStruct((rows, width), BF)
    tall = jax.ShapeDtypeStruct((rows, units), BF)
    outs = [
        low,
        jax.ShapeDtypeStruct((rows + 32, width), BF),
        jax.ShapeDtypeStruct((rows, width), F32),
        tall,
        low,
        low,
        tall,
        low,
        jax.ShapeDtypeStruct((16, width), F32),
    ]
    return pl.pallas_call(
        ffn_kernel,
        grid_spec=pltpu.PrefetchScalarGridSpec(
            num_scalar_prefetch=1,
            grid=(1,),
            in_specs=[fixed(x.shape) for x in args],
            out_specs=[fixed(x.shape) for x in outs],
            scratch_shapes=[
                pltpu.VMEM((width, width), BF),
                pltpu.VMEM((width, units), BF),
                pltpu.VMEM((units, width), BF),
                pltpu.VMEM((rows, units), F32),
                pltpu.VMEM((16, width), BF),
            ],
        ),
        out_shape=outs,
        compiler_params=params(),
        cost_estimate=lasting(10),
        name="feed_forward",
    )(info, *args)


def keep_or_send(info, half, mine, send, at, value):
    at, value = pl.multiple_of(at, 8), value.astype(BF)

    @pl.when(info[0] == half)
    def _():
        mine[pl.ds(at, value.shape[0]), :] = value

    @pl.when(info[0] != half)
    def _():
        send[pl.ds(at, value.shape[0]), :] = value


def split_halves(info, mine, send, starts, value):
    half, step = value.shape[0] // 2, value.shape[0] // 8
    first = info[0] == 0
    own = jnp.where(first, value[:half], value[half:]).astype(BF)
    other = jnp.where(first, value[half:], value[:half]).astype(BF)
    for n, at in enumerate(starts):
        mine[at : at + step, :] = own[n * step : n * step + step]
        send[at : at + step, :] = other[n * step : n * step + step]


def grads_kernel(
    info, a_own, a_other, do_ref, active_own, active_other, df_ref, h1_ref, du_ref, sums_ref, mine, send, *, quarter
):
    width = df_ref.shape[1]
    step = pl.program_id(0)
    part = active_own.shape[1]
    mine[0:part, :] = dot_tn(active_own[...], df_ref[...]).astype(BF)
    send[0:part, :] = dot_tn(active_other[...], df_ref[...]).astype(BF)
    up = dot_tn(h1_ref[...], du_ref[...])
    low, high = up[: width // 2].astype(BF), up[width // 2 :].astype(BF)
    at = part + width // 2
    mine[part:at, :] = jnp.where(info[0] == 0, low, high)
    send[part:at, :] = jnp.where(info[0] == 0, high, low)
    for out, a_ref in ((mine, a_own), (send, a_other)):
        both = dot_tn(a_ref[...], do_ref[...]).astype(BF)
        out[at : at + 64, :] = jnp.where(step % 2 == 0, both[:64], both[64:])
        out[at + 64 :, :] = jnp.zeros((quarter - at - 64, width), BF)

        @pl.when(step == 0)
        def _():
            out[at + 64 : at + 80, :] = sums_ref[...].astype(BF)


def ffn_grads(info, a, do, active, df, h1, du, sums, quarter):
    rows, width = df.shape
    units = active.shape[1]
    out = jax.ShapeDtypeStruct((4 * quarter, width), BF)
    columns = lambda n, index: pl.BlockSpec((rows, n), lambda j, info: (0, index(j, info[0])))
    return pl.pallas_call(
        functools.partial(grads_kernel, quarter=quarter),
        grid_spec=pltpu.PrefetchScalarGridSpec(
            num_scalar_prefetch=1,
            grid=(4,),
            in_specs=[
                columns(128, lambda j, core: core * 2 + j // 2),
                columns(128, lambda j, core: (1 - core) * 2 + j // 2),
                fixed(do.shape),
                columns(units // 8, lambda j, core: core * 4 + j),
                columns(units // 8, lambda j, core: (1 - core) * 4 + j),
                fixed(df.shape),
                fixed(h1.shape),
                columns(units // 4, lambda j, core: j),
                fixed(sums.shape),
            ],
            out_specs=[pl.BlockSpec((quarter, width), lambda j, *_: (j, 0))] * 2,
        ),
        out_shape=[out, out],
        compiler_params=params(),
        cost_estimate=lasting(10),
        name="ffn_grads",
    )(info, a, a, do, active, active, df, h1, du, sums)


def query_kernel(
    info, q_ref, kp_ref, k_ref, vp_ref, v_ref, log_ref, da_ref, exact_ref, dz1_ref, wq_a, wq_b,
    dq_ref, dh_ref, bias, keys, values, wq,
):
    rows, before = q_ref.shape[0], kp_ref.shape[0]
    width = dq_ref.shape[1]
    step = pl.program_id(0)
    chunks = chunks_of(keys.shape[0])
    make_bias = functools.partial(query_bias, info, rows, before)

    @pl.when(step == 0)
    def _():
        if len(chunks) == 1:
            bias[...] = make_bias(chunks[0])
        lay(info, wq, wq_a, wq_b)

    keys[0:before, :] = kp_ref[...]
    keys[before:, :] = k_ref[...]
    values[0:before, :] = vp_ref[...]
    values[before:, :] = v_ref[...]
    both = []
    for half in range(2):
        lanes = slice(64 * half, 64 * half + 64)
        delta = jnp.sum(da_ref[:, lanes].astype(F32) * exact_ref[:, lanes], axis=1, keepdims=True)
        dq = jnp.zeros((rows, 64), F32)
        for chunk in chunks:
            mask = bias[...] if len(chunks) == 1 else make_bias(chunk)
            scores = dot_nt(q_ref[:, lanes], keys[chunk, lanes]) + mask
            probs = jnp.exp(scores - log_ref[:, 64 * half : 64 * half + 1])
            dp = dot_nt(da_ref[:, lanes], values[chunk, lanes])
            ds = (probs * (dp - delta)).astype(BF)
            dq = dq + dot(ds, keys[chunk, lanes])
        both.append((dq * 0.125).astype(BF))
    pair = jnp.concatenate(both, axis=1)
    for n in range(width // 128):

        @pl.when(step == n)
        def _():
            dq_ref[:, 128 * n : 128 * n + 128] = pair

    @pl.when(step == pl.num_programs(0) - 1)
    def _():
        dh_ref[...] = dz1_ref[...] + dot_nt(dq_ref[...], wq[...])


def attend_query(info, q, kp, k, vp, v, logs, da, exact, dz1, wq):
    rows, width = q.shape
    before = kp.shape[0]
    cols = before + rows
    outs = [jax.ShapeDtypeStruct((rows, width), BF), jax.ShapeDtypeStruct((rows, width), F32)]
    return pl.pallas_call(
        query_kernel,
        grid_spec=pltpu.PrefetchScalarGridSpec(
            num_scalar_prefetch=1,
            grid=(width // 128,),
            in_specs=[paired(x.shape[0]) for x in (q, kp, k, vp, v, logs)]
            + [paired(rows), paired(rows), fixed(dz1.shape), fixed(wq[0].shape), fixed(wq[1].shape)],
            out_specs=[fixed(x.shape) for x in outs],
            scratch_shapes=[
                bias_scratch(rows, cols),
                pltpu.VMEM((cols, 128), BF),
                pltpu.VMEM((cols, 128), BF),
                pltpu.VMEM((width, width), BF),
            ],
        ),
        out_shape=outs,
        compiler_params=params(),
        cost_estimate=lasting(10),
        name="attend_query",
    )(info, q, kp, k, vp, v, logs, da, exact, dz1, *wq)


def last_kernel(info, *refs, reach, quarter, table):
    count = 2 * reach + 1
    q_parts, da_parts = refs[:count], refs[count : 2 * count]
    k_ref, v_ref, low_ref, dq_ref, dh_ref, wk_a, wk_b, wv_a, wv_b = refs[2 * count : 2 * count + 9]
    mine, send, dh_out, bias, queries, grads, dk_all, dv_all, wk, wv = refs[2 * count + 9 :]
    rows, width = low_ref.shape
    cols = queries.shape[0]
    step = pl.program_id(0)

    chunks = chunks_of(cols)
    make_bias = functools.partial(key_bias, info, rows)

    @pl.when(step == 0)
    def _():
        lay(info, wk, wk_a, wk_b)
        lay(info, wv, wv_a, wv_b)
        if len(chunks) == 1:
            bias[...] = make_bias(chunks[0])

    for n in range(count):
        queries[n * rows : n * rows + rows, :] = q_parts[n][...]
        grads[n * rows : n * rows + rows, :] = da_parts[n][0:rows, :]
    dks, dvs = [], []
    for half in range(2):
        lanes = slice(64 * half, 64 * half + 64)
        logs = jnp.concatenate([stat_row(x[rows : rows + 16, :], half, rows) for x in da_parts], axis=1)
        delta = jnp.concatenate([stat_row(x[rows + 16 : rows + 32, :], half, rows) for x in da_parts], axis=1)
        dk, dv = jnp.zeros((rows, 64), F32), jnp.zeros((rows, 64), F32)
        for chunk in chunks:
            mask = bias[...] if len(chunks) == 1 else make_bias(chunk)
            scores = dot_nt(k_ref[:, lanes], queries[chunk, lanes]) + mask
            probs = jnp.exp(scores - logs[:, chunk])
            dv = dv + dot(probs.astype(BF), grads[chunk, lanes])
            dp = dot_nt(v_ref[:, lanes], grads[chunk, lanes])
            ds = (probs * (dp - delta[:, chunk])).astype(BF)
            dk = dk + dot(ds, queries[chunk, lanes])
        dks.append(dk.astype(BF))
        dvs.append(dv.astype(BF))
    dk_pair, dv_pair = jnp.concatenate(dks, axis=1), jnp.concatenate(dvs, axis=1)
    for n in range(width // 128):

        @pl.when(step == n)
        def _():
            dk_all[:, 128 * n : 128 * n + 128] = dk_pair
            dv_all[:, 128 * n : 128 * n + 128] = dv_pair

    @pl.when(step == pl.num_programs(0) - 1)
    def _():
        dk, dv = dk_all[...], dv_all[...]
        step_rows = width // 8
        split_halves(info, mine, send, [n * quarter for n in range(4)], dot_tn(low_ref[...], dk))
        split_halves(info, mine, send, [n * quarter + step_rows for n in range(4)], dot_tn(low_ref[...], dv))
        dq = dq_ref[...]
        split_halves(info, mine, send, [n * quarter + 2 * step_rows for n in range(4)], dot_tn(low_ref[...], dq))
        dh = dh_ref[...] + dot_nt(dk, wk[...]) + dot_nt(dv, wv[...])
        dh_out[...] = dh.astype(BF)
        parts = []
        for _ in range(3):
            parts.append(dh.astype(BF))
            dh = dh - parts[-1].astype(F32)
        spots = info[1] + iota((1, rows), 1)
        place = spots - first_places(info, spots)
        base = 3 * step_rows
        fourth = table // 8
        for half in range(2):
            for n in range(4):
                hot = (place - (half * 4 + n) * fourth == iota((fourth, rows), 0)).astype(F32).astype(BF)
                total = dot(hot, parts[0]) + dot(hot, parts[1]) + dot(hot, parts[2])
                keep_or_send(info, half, mine, send, n * quarter + base, total)
        base += fourth
        spare = quarter - base
        for n in range(4):
            mine[n * quarter + base : (n + 1) * quarter, :] = jnp.zeros((spare, width), BF)
            send[n * quarter + base : (n + 1) * quarter, :] = jnp.zeros((spare, width), BF)
        total_v = jnp.sum(dv.astype(F32), axis=0, keepdims=True)
        total_q = jnp.sum(dq.astype(F32), axis=0, keepdims=True)
        total = jnp.where(iota((8, width), 0) == 0, total_v, total_q)
        mine[base : base + 8, :] = total.astype(BF)
        send[base : base + 8, :] = total.astype(BF)


def last(info, q_parts, da_parts, k, v, low, dq, dh, wk, wv, quarter, table):
    rows, width = k.shape
    count = len(q_parts)
    cols = count * rows
    outs = [
        jax.ShapeDtypeStruct((4 * quarter, width), BF),
        jax.ShapeDtypeStruct((4 * quarter, width), BF),
        jax.ShapeDtypeStruct((rows, width), BF),
    ]
    rest = (low, dq, dh, *wk, *wv)
    return pl.pallas_call(
        functools.partial(last_kernel, reach=count // 2, quarter=quarter, table=table),
        grid_spec=pltpu.PrefetchScalarGridSpec(
            num_scalar_prefetch=1,
            grid=(width // 128,),
            in_specs=[paired(x.shape[0]) for x in (*q_parts, *da_parts, k, v)] + [fixed(x.shape) for x in rest],
            out_specs=[fixed(x.shape) for x in outs],
            scratch_shapes=[
                bias_scratch(rows, cols),
                pltpu.VMEM((cols, 128), BF),
                pltpu.VMEM((cols, 128), BF),
                pltpu.VMEM((rows, width), BF),
                pltpu.VMEM((rows, width), BF),
                pltpu.VMEM((width, width), BF),
                pltpu.VMEM((width, width), BF),
            ],
        ),
        out_shape=outs,
        compiler_params=params(),
        cost_estimate=lasting(15),
        name="last",
    )(info, *q_parts, *da_parts, k, v, *rest)


def cut_kernel(digit_ref, *refs, terms, radix):
    ins, outs = refs[: terms * radix], refs[terms * radix :]
    for k in range(radix):
        total = ins[k * terms][...].astype(F32)
        for n in range(1, terms):
            total = total + ins[k * terms + n][...].astype(F32)
        outs[k][...] = total.astype(outs[k].dtype)


def cut(terms, digit, radix, kept):
    rows, width = terms[0].shape[0] // radix, terms[0].shape[1]
    subs = max(n for n in (1, 2, 3, 4) if rows % (8 * n) == 0 and rows // n >= 64 or n == 1)
    specs = [
        pl.BlockSpec((rows // subs, width), lambda n, d, k=k: ((d[0] ^ k) * subs + n, 0))
        for k in range(radix)
        for _ in terms
    ]
    return pl.pallas_call(
        functools.partial(cut_kernel, terms=len(terms), radix=radix),
        grid_spec=pltpu.PrefetchScalarGridSpec(
            num_scalar_prefetch=1,
            grid=(subs,),
            in_specs=specs,
            out_specs=[pl.BlockSpec((rows // subs, width), lambda n, d: (n, 0))] * radix,
        ),
        out_shape=[jax.ShapeDtypeStruct((rows, width), BF if k else kept) for k in range(radix)],
        compiler_params=params(),
        cost_estimate=lasting(3),
        name="cut",
    )(digit.reshape(1), *([*terms] * radix))


def place_kernel(digit_ref, *refs, radix, sizes):
    parts, outs = refs[:radix], refs[radix:]
    for k in range(radix):

        @pl.when(pl.program_id(0) == k)
        def _():
            at = 0
            for out, size in zip(outs, sizes):
                out[...] = parts[k][at : at + size, :].astype(out.dtype)
                at += size


def place(parts, digit, sizes, dtype, across):
    radix, (rows, width) = len(parts), parts[0].shape
    below = lambda k, d: (k ^ d[0], 0)
    beside = lambda k, d: (0, k ^ d[0])
    return pl.pallas_call(
        functools.partial(place_kernel, radix=radix, sizes=sizes),
        grid_spec=pltpu.PrefetchScalarGridSpec(
            num_scalar_prefetch=1,
            grid=(radix,),
            in_specs=[fixed((rows, width))] * radix,
            out_specs=[
                pl.BlockSpec((n, width), beside if i == across else below) for i, n in enumerate(sizes)
            ],
        ),
        out_shape=[
            jax.ShapeDtypeStruct((n, width * radix) if i == across else (n * radix, width), dtype)
            for i, n in enumerate(sizes)
        ],
        compiler_params=params(),
        cost_estimate=lasting(3),
        name="place",
    )(digit.reshape(1), *parts)


def exchange(pieces, here, stride, ranks):
    return [
        lax.ppermute(piece, "ctx", [(i, i ^ ((k + 1) * stride)) for i in range(ranks)])
        for k, piece in enumerate(pieces)
    ]


def stages_of(ranks):
    stages, stride = [], 1
    while stride < ranks:
        radix = 4 if (ranks // stride) % 4 == 0 else 2
        stages.append((stride, radix))
        stride *= radix
    return stages


def after(first, then):
    return lax.optimization_barrier((first, then))[1]


class Reduction:
    def __init__(self, here, ranks, sizes, across):
        self.here, self.ranks, self.sizes, self.across = here, ranks, sizes, across
        self.stages = stages_of(ranks)

    def digit(self, level):
        stride, radix = self.stages[level]
        return (self.here // stride) % radix

    def cut(self, terms, level):
        if level == len(self.stages):
            return cut(terms, self.here * 0, 1, BF)
        return cut(terms, self.digit(level), self.stages[level][1], F32)

    def scatter(self, pieces, level):
        return [pieces[0]] + exchange(pieces[1:], self.here, self.stages[level][0], self.ranks)

    def gather(self, held, level):
        stride, radix = self.stages[level]
        return [held] + exchange([held] * (radix - 1), self.here, stride, self.ranks)

    def place(self, parts, level):
        if level:
            return place(parts, self.digit(level), [parts[0].shape[0]], BF, None)[0]
        return place(parts, self.digit(0), self.sizes, F32, self.across)


def padded(rows, ranks):
    step = 2 * ranks
    return -(-rows // step) * step


def swap_core(x):
    return lax.ppermute(x, "fsdp", SWAP)


def by_core(core, own, other):
    return jnp.where(core == 0, jnp.stack([own, other]), jnp.stack([other, own]))


def next_chip(block, chips, step):
    pairs = [(i, i + 4) for i in range(4 * (chips - 1))]
    return lax.ppermute(block, "ctx", pairs if step > 0 else [(b, a) for a, b in pairs])


def send_window(own, reach, chips, step):
    far = [own]
    for k in range(1, reach + 1):
        if step > 0:
            pairs = [(i, i + 4 * k) for i in range(4 * (chips - k))]
        else:
            pairs = [(i + 4 * k, i) for i in range(4 * (chips - k))]
        far.append(lax.ppermute(own, "ctx", pairs))
    return far


def both_cores(far, core, step):
    near = core == (0 if step > 0 else 1)
    parts = []
    for k in range(len(far) - 1):
        parts += [swap_core(jnp.where(near, far[k], far[k + 1])), far[k + 1]]
    return parts


def shards(
    tokens,
    cotangent,
    lengths,
    deal_order,
    w_query,
    w_key,
    w_value,
    w_out,
    w_up,
    w_down,
    b_query,
    b_value,
    b_out,
    b_up,
    b_down,
    gain_one,
    shift_one,
    gain_two,
    shift_two,
    positions,
):
    block, width = tokens.shape[2], tokens.shape[3]
    ranks = lax.axis_size("ctx")
    chips = ranks // 4
    slot = block // ranks
    rows = 2 * block
    group = ranks * block
    longest = 2 * positions.shape[0]
    reach = longest // (2 * rows)
    here = lax.axis_index("ctx")
    core = lax.axis_index("fsdp")
    chip, micro, stream = here // 4, here % 2, (here // 2) % 2
    base = chip * (2 * rows) + core * rows

    index = lambda i, t: 2 * i + t
    straight, crossing = [], []
    for i in range(ranks):
        c, a, b = i // 4, (i // 2) % 2, i % 2
        for t in range(2):
            straight.append((index(i, t), index(4 * c + 2 * t + b, a)))
            crossing.append((index(i, t), index(4 * c + 2 * t + 1 - b, a)))
    even = here % 2 == 0
    same = jnp.where(even, tokens[0, 0], tokens[1, 0])
    cross = jnp.where(even, tokens[1, 0], tokens[0, 0])
    got_same = lax.ppermute(same, BOTH, straight)
    got_cross = lax.ppermute(cross, BOTH, crossing)
    first_half = jnp.where(micro == 0, got_same, got_cross)
    second_half = jnp.where(micro == 0, got_cross, got_same)
    own = jnp.concatenate([first_half, second_half], axis=0)

    table = jnp.concatenate([deal_order[:, 0], lengths[:, 0]], axis=1)
    table = jnp.where(micro == 0, table[0], table[1])
    table = jnp.where(stream == core, table, swap_core(table))
    order, lens = table[:group], table[group:]

    head = jnp.stack([core, base, jnp.int32(group)]).astype(jnp.int32)
    info = jnp.concatenate([head, lens])

    whole = lambda x: (x, swap_core(x))
    pos, wq, wk, wv = whole(positions), whole(w_query), whole(w_key), whole(w_value)
    vectors = [b_out, b_down, gain_one, shift_one, gain_two, shift_two, b_query, b_value, b_up]
    vec = whole(stack_vectors(vectors, width // 2))
    wo, wu, wd = whole(w_out), whole(w_up), whole(w_down)

    mine = order.reshape(ranks, ranks, slot)
    mine = lax.dynamic_slice_in_dim(mine, 4 * chip + 2 * core, 2, axis=1).reshape(rows) - base
    dealt = cotangent[:, 0].reshape(2, chips, 2, 2 * slot, width)
    keep = jnp.where(core == 0, dealt[:, :, 0], dealt[:, :, 1])
    give = jnp.where(core == 0, dealt[:, :, 1], dealt[:, :, 0])
    streams = by_core(core, keep, swap_core(give))
    sends = jnp.transpose(streams, (2, 0, 1, 3, 4)).reshape(rows, width)
    arrived = lax.all_to_all(sends, "ctx", split_axis=0, concat_axis=0, tiled=True)

    own = after(arrived, own)
    fixed_args = (pos, wk, wv, wq, vec)
    far = send_window(own, reach, chips, 1)
    k, v, q, hidden, low = project(info, [own], 0, True, *fixed_args)
    earlier = both_cores(far, core, 1)[::-1]
    before = len(earlier) * rows
    far_q = send_window(after(far[1:], q), reach, chips, -1)
    kp, vp = project(info, earlier, -before, False, *fixed_args)
    att, exact, logs, log_stats = attend_forward(info, q, kp, k, vp, v)
    exact = after(far_q[1:], exact)
    later_q = [q] + both_cores(far_q, core, -1)
    leaving, da_msg, dz1, active, df, h1, du, do, sums = feed_forward(
        info, att, exact, log_stats, hidden, arrived, mine, wo, wu, wd, vec
    )
    far_da = [da_msg, next_chip(da_msg, chips, -1)]

    half = width // 2
    units = 2 * b_up.shape[0]
    sizes = [units // 8, half, width // 8]
    quarter = padded(sum(sizes) + 16, ranks)
    sizes.append(quarter - sum(sizes))
    sizes_last = [width // 8, width // 8, width // 8, longest // 8]
    quarter_last = padded(sum(sizes_last) + 8, ranks)
    sizes_last.append(quarter_last - sum(sizes_last))
    one = Reduction(here, ranks, sizes, 1)
    two = Reduction(here, ranks, sizes_last, None)
    levels = len(one.stages)

    keep, give = ffn_grads(info, att, do, active, df, h1, du, sums, quarter)
    give = after(far_da[1], give)
    for _ in range(reach - 1):
        far_da.append(next_chip(far_da[-1], chips, -1))
    pieces = one.cut([keep, swap_core(give)], 0)
    exact = after(pieces, exact)
    terms = one.scatter(pieces, 0)
    dq, dh = attend_query(info, q, kp, k, vp, v, logs, da_msg, exact, dz1, wq)
    later_da = [da_msg] + both_cores(far_da, core, -1)
    keep, give, dh0_low = last(info, later_q, later_da, k, v, low, dq, dh, wk, wv, quarter_last, longest)

    terms_last = [keep, swap_core(give)]
    for level in range(levels):
        pieces_last = two.cut(terms_last, level)
        terms_last = two.scatter(pieces_last, level)
        pieces = one.cut(after(pieces_last, terms), level + 1)
        if level + 1 < levels:
            terms = one.scatter(pieces, level + 1)
        if level == 0:
            leaving, dh0_low = after(pieces_last, (leaving, dh0_low))
    held = pieces[0]
    (held_last,) = two.cut(terms_last, levels)
    for level in reversed(range(levels)):
        parts = one.gather(held, level)
        parts_last = two.gather(held_last, level)
        held = one.place(parts, level)
        held_last = two.place(parts_last, level)
    g_down, g_up, g_out, early = held
    g_key, g_value, g_query, g_pos, late = held_last
    shard = lambda x: lax.dynamic_slice_in_dim(x, core * half, half)
    gb_down, gg1, gs1, gg2, gs2, gb_out = (shard(early[n]) for n in range(6))
    gb_up = lax.dynamic_slice_in_dim(early[7:11].reshape(-1), core * (units // 2), units // 2)
    gb_value, gb_query = shard(late[0]), shard(late[1])

    landed = lax.all_to_all(leaving, "ctx", split_axis=0, concat_axis=0, tiled=True)
    landed = landed.reshape(chips, 2, 2, 2 * slot, width)
    keep = jnp.where(core == 0, landed[:, 0], landed[:, 1])
    give = jnp.where(core == 0, landed[:, 1], landed[:, 0])
    sides = by_core(core, keep, swap_core(give))
    output = jnp.transpose(sides, (2, 1, 0, 3, 4)).reshape(2, 1, block, width)

    back_same = jnp.where(micro == 0, dh0_low[:block], dh0_low[block:])
    back_cross = jnp.where(micro == 0, dh0_low[block:], dh0_low[:block])
    home_same = lax.ppermute(back_same, BOTH, [(b, a) for a, b in straight])
    home_cross = lax.ppermute(back_cross, BOTH, [(b, a) for a, b in crossing])
    grad_tokens = jnp.where(
        even, jnp.stack([home_same, home_cross]), jnp.stack([home_cross, home_same])
    )[:, None]

    return (
        output,
        grad_tokens,
        g_query,
        g_key,
        g_value,
        g_out,
        g_up,
        g_down,
        gb_query,
        gb_value,
        gb_out,
        gb_up,
        gb_down,
        gg1,
        gs1,
        gg2,
        gs2,
        g_pos,
    )


def solution(mesh):
    data = P(None, "fsdp", "ctx", None)
    groups = P(None, "fsdp", None)
    matrix, vector = P("fsdp", None), P("fsdp")
    return jax.shard_map(
        shards,
        mesh=mesh,
        in_specs=(data, data, groups, groups) + (matrix,) * 6 + (vector,) * 9 + (matrix,),
        out_specs=(data, data) + (matrix,) * 6 + (vector,) * 9 + (matrix,),
        check_vma=False,
    )
```

time: 1160 us -> 296 us (0.26)
  waiting for transfers between devices: 575 us -> 103 us
  blocking collectives: 337 us -> 0 us
  matrix products: 111 us -> 0 us
  Pallas kernels: 0 us -> 95.1 us
  starting transfers between devices: 26.8 us -> 60 us
  other arithmetic: 36.9 us -> 9.98 us
  local copies, waits for them, and re-layouts: 41.8 us -> 23.1 us
  between operations: 17.8 us -> 1.7 us
    reduce_scatter x11 -> x0, waiting for transfers between devices: 361 us -> none  [the longest x2 187 us: shards(): lax.psum_scatter(value_parts.reshape(group_rows, feat_width), 'ctx', scat...]
    psum x1 -> x0, blocking collectives: 309 us -> none  [shards(): totals = lax.psum(shares, 'ctx')]
    all_gather x7 -> x0, waiting for transfers between devices: 200 us -> none  [the longest x2 109 us: shards(): lax.all_gather(value_low, 'ctx', axis=0, tiled=True)]
    dot_general x50 -> x0, matrix products: 111 us -> none  [the longest x12 20 us: project_back(): lax.dot_general(left_side, right_side, (((0,), (0,)), ((), ())), preferre...]
    ppermute x0 -> x53, waiting for transfers between devices: none -> 95.3 us  [the longest x24 63.9 us: exchange(): lax.ppermute(piece, 'ctx', [(i, i ^ (k + 1) * stride) for i in range(rank...]
    pallas_call x0 -> x17, Pallas kernels: none -> 95.1 us  [the longest x6 17.4 us: cut(): pl.pallas_call(functools.partial(cut_kernel, terms=len(terms), radix=radi...]
    ppermute x0 -> x53, starting transfers between devices: none -> 47.3 us  [the longest x24 23.9 us: exchange(): lax.ppermute(piece, 'ctx', [(i, i ^ (k + 1) * stride) for i in range(rank...]
    all_gather x13 -> x0, blocking collectives: 24.7 us -> none  [the longest x1 2.18 us: shards(): lax.all_gather(attn_local[1], 'fsdp', axis=0, tiled=True)]
  transfers between devices with their start and end apart: 22 -> 55, of which waited for: 19 -> 20; matrix products, arithmetic and copies ran while one was open for 11% -> 4% of each run, Pallas kernels for 0% -> 22%
where the time goes in v1:
time: 296 us; the launch traced here: 293 us
  waiting for transfers between devices  103 us (35%)
  Pallas kernels  95.1 us (32%)
  starting transfers between devices  60 us (20%)
  local copies, waits for them, and re-layouts  23.1 us (8%)
  other arithmetic  9.98 us (3%)
    ppermute x24, waiting for transfers between devices, exchange(): lax.ppermute(piece, 'ctx', [(i, i ^ (k + 1) * stride) for i in range(rank...  63.9 us
    ppermute x24, starting transfers between devices, exchange(): lax.ppermute(piece, 'ctx', [(i, i ^ (k + 1) * stride) for i in range(rank...  23.9 us
    pallas_call x6, Pallas kernels, cut(): pl.pallas_call(functools.partial(cut_kernel, terms=len(terms), radix=radi...  17.4 us
    pallas_call x1, Pallas kernels, last(): pl.pallas_call(functools.partial(last_kernel, reach=count // 2, quarter=q...  14.9 us
    unnamed x125, local copies, waits for them, and re-layouts  14 us
    ppermute x4, waiting for transfers between devices, send_window(): far.append(lax.ppermute(own, 'ctx', pairs))  13.9 us
    pallas_call x4, Pallas kernels, place(): pl.pallas_call(functools.partial(place_kernel, radix=radix, sizes=sizes),...  12.5 us
    pallas_call x1, Pallas kernels, attend_forward(): pl.pallas_call(forward_kernel, grid_spec=pltpu.PrefetchScalarGridSpec(num...  11.7 us
  transfers between devices with their start and end apart: 55, of which 20 were waited for; matrix products, arithmetic and copies ran while one was open for 4% of the time, Pallas kernels for 22%

profile of v1, /device:TPU:16, one launch (start us, length us, event | category | flops | bytes accessed | tf_op | source)
XLA Modules:
  0.0 292.8 jit_solution(10141657796653493628)
XLA Ops:
  10.2 6.7 %all-to-all-start = ((bf16[16,16,512]{2,1,0:T(8,128)(2,1)}), bf16[16,16,512]{2,1,0:T(8,128)(2,1)S(1)}, u32[]{:S(2)}, u32[]{:S(2)}) async-start(bf16[16,16,512]{2,1,0:T(8,128)(2,1)} %bitcast.12), calls=%async_computation | async-start | bytes 524288 | tf_op jit(solution)/shard_map/all_to_all | solution.py:908
  17.2 7.6 %all-to-all-done = bf16[16,16,512]{2,1,0:T(8,128)(2,1)S(1)} async-done(((bf16[16,16,512]{2,1,0:T(8,128)(2,1)}), bf16[16,16,512]{2,1,0:T(8,128)(2,1)S(1)}, u32[]{:S(2)}, u32[]{:S(2)}) %all-to-all-start) | async-done | bytes 262176 | tf_op jit(solution)/shard_map/all_to_all | solution.py:908
  32.4 4.5 %collective-permute-done.10.refs_0_ = bf16[256,512]{1,0:T(8,128)(2,1)S(1)} collective-permute-done((bf16[256,512]{1,0:T(8,128)(2,1)S(1)}, bf16[256,512]{1,0:T(8,128)(2,1)S(1)}, u32[]{:S(2)}, u32[]{:S(2)}) %collective-permute-start.10) | collective-permute-done | bytes 262176 | tf_op jit(solution)/shard_map/ppermute | solution.py:824
  36.9 9.4 %collective-permute-done.9.refs_2_ = bf16[256,512]{1,0:T(8,128)(2,1)S(1)} collective-permute-done((bf16[256,512]{1,0:T(8,128)(2,1)S(1)}, bf16[256,512]{1,0:T(8,128)(2,1)S(1)}, u32[]{:S(2)}, u32[]{:S(2)}) %collective-permute-start.9) | collective-permute-done | bytes 262176 | tf_op jit(solution)/shard_map/ppermute | solution.py:824
  49.1 4.2 %project.2 = (bf16[256,512]{1,0:T(8,128)(2,1)}, bf16[256,512]{1,0:T(8,128)(2,1)}, bf16[256,512]{1,0:T(8,128)(2,1)}, f32[256,512]{1,0:T(8,128)}, bf16[256,512]{1,0:T(8,128)(2,1)}) custom-call(s32[11]{0:T(128)} %pad_add_fusion.1.info, bf16[256,512]{1,0:T(8,128)(2,1)} %copy-done.15, bf16[512,512]{1,0:T(8,128)(2,1)} %refs_4_.1, bf16[512,512]{1,0:T(8,128)(2,1)} %copy-done.17, ...), custom_call_target="tpu_custom_call" | custom-call | flops 4 | bytes 4 | tf_op jit(solution)/shard_map/project/pallas_call | solution.py:159
  58.4 7.1 %project.3 = (bf16[1024,512]{1,0:T(8,128)(2,1)}, bf16[1024,512]{1,0:T(8,128)(2,1)}) custom-call(s32[11]{0:T(128)} %pad_add_fusion.1.info, bf16[256,512]{1,0:T(8,128)(2,1)} %copy-done.19, bf16[256,512]{1,0:T(8,128)(2,1)} %copy-done.33, bf16[256,512]{1,0:T(8,128)(2,1)} %copy-done.20, bf16[256,512]{1,0:T(8,128)(2,1)} %collective-permute-done.16.refs_3_, ...), custom_call_target="tpu_custom_call" | custom-call | flops 10 | bytes 10 | tf_op jit(solution)/shard_map/project/pallas_call | solution.py:159
  65.5 11.7 %attend_forward.1 = (bf16[256,512]{1,0:T(8,128)(2,1)}, f32[256,512]{1,0:T(8,128)}, f32[256,512]{1,0:T(8,128)}, bf16[16,512]{1,0:T(8,128)(2,1)}) custom-call(s32[11]{0:T(128)} %pad_add_fusion.1.info, bf16[256,512]{1,0:T(8,128)(2,1)} %get-tuple-element.87.q_ref.refs_0_, bf16[1024,512]{1,0:T(8,128)(2,1)} %get-tuple-element.88.kp_ref, ...), custom_call_target="tpu_custom_call" | custom-call | flops 12 | bytes 12 | tf_op jit(solution)/shard_map/attend_forward/pallas_call | solution.py:284
  78.0 10.1 %feed_forward.1 = (bf16[256,512]{1,0:T(8,128)(2,1)}, bf16[288,512]{1,0:T(8,128)(2,1)}, f32[256,512]{1,0:T(8,128)}, bf16[256,2048]{1,0:T(8,128)(2,1)}, bf16[256,5...) custom-call(s32[11]{0:T(128)} %pad_add_fusion.1.info, ...), custom_call_target="tpu_custom_call" | custom-call | flops 10 | bytes 10 | tf_op jit(solution)/shard_map/feed_forward/pallas_call | solution.py:400
  90.2 7.2 %ffn_grads.1 = (bf16[2432,512]{1,0:T(8,128)(2,1)}, bf16[2432,512]{1,0:T(8,128)(2,1)}) custom-call(s32[11]{0:T(128)} %pad_add_fusion.1.info, bf16[256,512]{1,0:T(8,128)(2,1)} %get-tuple-element.92.a_ref.a_own.a_other, bf16[256,512]{1,0:T(8,128)(2,1)} %get-tuple-element.92.a_ref.a_own.a_other, bf16[256,512]{1,0:T(8,128)(2,1)} %get-tuple-element.100.do_ref, ...), custom_call_target="tpu_custom_call" | custom-call | flops 10 | bytes 10 | tf_op jit(solution)/shard_map/ffn_grads/pallas_call | solution.py:472
  101.7 9.2 %collective-permute-done.22.refs_9_ = bf16[288,512]{1,0:T(8,128)(2,1)} collective-permute-done((bf16[288,512]{1,0:T(8,128)(2,1)S(1)}, bf16[288,512]{1,0:T(8,128)(2,1)}, u32[]{:S(2)}, u32[]{:S(2)}) %collective-permute-start.22) | collective-permute-done | bytes 294944 | tf_op jit(solution)/shard_map/ppermute | solution.py:814
  117.1 4.7 %cut.6 = (f32[608,512]{1,0:T(8,128)}, bf16[608,512]{1,0:T(8,128)(2,1)}, bf16[608,512]{1,0:T(8,128)(2,1)}, bf16[608,512]{1,0:T(8,128)(2,1)}) custom-call(s32[1]{0:T(128)} %bitcast.digit_ref, bf16[2432,512]{1,0:T(8,128)(2,1)} %get-tuple-element.106.refs_0_.refs_2_.refs_4_.refs_6_, bf16[2432,512]{1,0:T(8,128)(2,1)} %copy-done, ...), custom_call_target="tpu_custom_call" | custom-call | flops 3 | bytes 3 | tf_op jit(solution)/shard_map/cut/pallas_call | solution.py:701
  121.8 10.0 %attend_query.1 = (bf16[256,512]{1,0:T(8,128)(2,1)}, f32[256,512]{1,0:T(8,128)}) custom-call(s32[11]{0:T(128)} %pad_add_fusion.1.info, bf16[256,512]{1,0:T(8,128)(2,1)} %get-tuple-element.87.q_ref.refs_0_, bf16[1024,512]{1,0:T(8,128)(2,1)} %get-tuple-element.88.kp_ref, bf16[256,512]{1,0:T(8,128)(2,1)} %get-tuple-element.89.k_ref.refs_10_, ...), custom_call_target="tpu_custom_call" | custom-call | flops 10 | bytes 10 | tf_op jit(solution)/shard_map/attend_query/pallas_call | solution.py:547
  132.6 14.9 %last.1 = (bf16[1408,512]{1,0:T(8,128)(2,1)}, bf16[1408,512]{1,0:T(8,128)(2,1)}, bf16[256,512]{1,0:T(8,128)(2,1)}) custom-call(s32[11]{0:T(128)} %pad_add_fusion.1.info, bf16[256,512]{1,0:T(8,128)(2,1)} %get-tuple-element.87.q_ref.refs_0_, bf16[256,512]{1,0:T(8,128)(2,1)} %copy-done.34, bf16[256,512]{1,0:T(8,128)(2,1)} %copy-done.21, ...), custom_call_target="tpu_custom_call" | custom-call | flops 15 | bytes 15 | tf_op jit(solution)/shard_map/last/pallas_call | solution.py:660
  152.3 3.9 %cut.7 = (f32[352,512]{1,0:T(8,128)}, bf16[352,512]{1,0:T(8,128)(2,1)}, bf16[352,512]{1,0:T(8,128)(2,1)}, bf16[352,512]{1,0:T(8,128)(2,1)}) custom-call(s32[1]{0:T(128)} %bitcast.digit_ref, bf16[1408,512]{1,0:T(8,128)(2,1)} %get-tuple-element.117.refs_0_.refs_2_.refs_4_.refs_6_, bf16[1408,512]{1,0:T(8,128)(2,1)} %copy-done.1, ...), custom_call_target="tpu_custom_call" | custom-call | flops 3 | bytes 3 | tf_op jit(solution)/shard_map/cut/pallas_call | solution.py:701
  157.4 7.1 %collective-permute-done.41.refs_1_.refs_5_.refs_9_.refs_13_ = bf16[608,512]{1,0:T(8,128)(2,1)S(1)} collective-permute-done((bf16[608,512]{1,0:T(8,128)(2,1)S(1)}, bf16[608,512]{1,0:T(8,128)(2,1)S(1)}, u32[]{:S(2)}, u32[]{:S(2)}) %collective-permute-start.41) | collective-permute-done | bytes 622624 | tf_op jit(solution)/shard_map/ppermute | solution.py:754
  165.1 6.0 %all-to-all-start.1 = ((bf16[16,16,512]{2,1,0:T(8,128)(2,1)}), bf16[16,16,512]{2,1,0:T(8,128)(2,1)S(1)}, u32[]{:S(2)}, u32[]{:S(2)}) async-start(bf16[16,16,512]{2,1,0:T(8,128)(2,1)} %bitcast.16), calls=%async_computation.1 | async-start | bytes 524288 | tf_op jit(solution)/shard_map/all_to_all | solution.py:972
  171.1 9.6 %collective-permute-done.42.refs_2_.refs_6_.refs_10_.refs_14_ = bf16[608,512]{1,0:T(8,128)(2,1)S(1)} collective-permute-done((bf16[608,512]{1,0:T(8,128)(2,1)}, bf16[608,512]{1,0:T(8,128)(2,1)S(1)}, u32[]{:S(2)}, u32[]{:S(2)}) %collective-permute-start.42) | collective-permute-done | bytes 622624 | tf_op jit(solution)/shard_map/ppermute | solution.py:754
  188.7 7.2 %collective-permute-done.30.refs_2_.refs_6_.refs_10_.refs_14_ = bf16[352,512]{1,0:T(8,128)(2,1)S(1)} collective-permute-done((bf16[352,512]{1,0:T(8,128)(2,1)}, bf16[352,512]{1,0:T(8,128)(2,1)S(1)}, u32[]{:S(2)}, u32[]{:S(2)}) %collective-permute-start.30) | collective-permute-done | bytes 360480 | tf_op jit(solution)/shard_map/ppermute | solution.py:754
  219.5 5.0 %collective-permute-done.36.refs_2_ = bf16[88,512]{1,0:T(8,128)(2,1)S(1)} collective-permute-done((bf16[88,512]{1,0:T(8,128)(2,1)}, bf16[88,512]{1,0:T(8,128)(2,1)S(1)}, u32[]{:S(2)}, u32[]{:S(2)}) %collective-permute-start.36) | collective-permute-done | bytes 90144 | tf_op jit(solution)/shard_map/ppermute | solution.py:754
  240.8 4.7 %collective-permute-done.28 = bf16[128,512]{1,0:T(8,128)(2,1)S(1)} collective-permute-done((bf16[128,512]{1,0:T(8,128)(2,1)S(1)}, bf16[128,512]{1,0:T(8,128)(2,1)S(1)}, u32[]{:S(2)}, u32[]{:S(2)}) %collective-permute-start.28) | collective-permute-done | bytes 131104 | tf_op jit(solution)/shard_map/ppermute | solution.py:982
  250.5 4.9 %collective-permute-done.39.refs_2_ = bf16[352,512]{1,0:T(8,128)(2,1)S(1)} collective-permute-done((bf16[352,512]{1,0:T(8,128)(2,1)}, bf16[352,512]{1,0:T(8,128)(2,1)S(1)}, u32[]{:S(2)}, u32[]{:S(2)}) %collective-permute-start.39) | collective-permute-done | bytes 360480 | tf_op jit(solution)/shard_map/ppermute | solution.py:754
  262.1 4.5 %collective-permute-done.50.refs_1_ = bf16[608,512]{1,0:T(8,128)(2,1)S(1)} collective-permute-done((bf16[608,512]{1,0:T(8,128)(2,1)}, bf16[608,512]{1,0:T(8,128)(2,1)S(1)}, u32[]{:S(2)}, u32[]{:S(2)}) %collective-permute-start.50) | collective-permute-done | bytes 622624 | tf_op jit(solution)/shard_map/ppermute | solution.py:754
  266.6 14.6 %collective-permute-done.51.refs_2_ = bf16[608,512]{1,0:T(8,128)(2,1)S(1)} collective-permute-done((bf16[608,512]{1,0:T(8,128)(2,1)}, bf16[608,512]{1,0:T(8,128)(2,1)S(1)}, u32[]{:S(2)}, u32[]{:S(2)}) %collective-permute-start.51) | collective-permute-done | bytes 622624 | tf_op jit(solution)/shard_map/ppermute | solution.py:754
  282.8 4.2 %place.7 = (f32[1024,512]{1,0:T(8,128)}, f32[256,2048]{1,0:T(8,128)}, f32[256,512]{1,0:T(8,128)}, f32[128,512]{1,0:T(8,128)}) custom-call(s32[1]{0:T(128)} %bitcast.digit_ref, bf16[608,512]{1,0:T(8,128)(2,1)} %place.6.refs_0_, bf16[608,512]{1,0:T(8,128)(2,1)} %copy-done.24, bf16[608,512]{1,0:T(8,128)(2,1)} %copy-done.25, bf16[608,512]{1,0:T(8,128)(2,1)} %copy-done.26), custom_call_target="tpu_custom_call" | custom-call | flops 3 | bytes 3 | tf_op jit(solution)/shard_map/place/pallas_call | solution.py:732
  (279 shorter events, 111.9 us)
Async XLA Ops:
  7.5 24.5 %collective-permute-start.5 = (bf16[256,512]{1,0:T(8,128)(2,1)}, bf16[256,512]{1,0:T(8,128)(2,1)S(1)}, u32[]{:S(2)}, u32[]{:S(2)}) collective-permute-start(bf16[256,512]{1,0:T(8,128)(2,1)} %refs_15_.1), channel_id=1, source_target_pairs={{0,1},{1,0},{2,3},{3,2},{4,5},{5,4},{6,7},{7,6},{8,9},{9,8},{10,11... | collective-permute-start | bytes 786440 | tf_op jit(solution)/shard_map/ppermute | solution.py:805
  26.1 20.2 %collective-permute-start.9 = (bf16[256,512]{1,0:T(8,128)(2,1)S(1)}, bf16[256,512]{1,0:T(8,128)(2,1)S(1)}, u32[]{:S(2)}, u32[]{:S(2)}) collective-permute-start(bf16[256,512]{1,0:T(8,128)(2,1)S(1)} %pad_maximum_fusion.refs_0_), channel_id=1, source_target_pairs={{0,8},{2,10},{4,12},{6,14},{8,16},{10,18},{12,20},{14,22},{16,24},... | collective-permute-start | bytes 786440 | tf_op jit(solution)/shard_map/ppermute | solution.py:824
  31.5 45.8 %collective-permute-start.18 = (bf16[256,2048]{1,0:T(8,128)(2,1)}, bf16[256,2048]{1,0:T(8,128)(2,1)}, u32[]{:S(2)}, u32[]{:S(2)}) collective-permute-start(bf16[256,2048]{1,0:T(8,128)(2,1)} %wu_a.1), channel_id=1, source_target_pairs={{0,1},{1,0},{2,3},{3,2},{4,5},{5,4},{6,7},{7,6},{8,9},{9,8},{10,11... | collective-permute-start | bytes 3145736 | tf_op jit(solution)/shard_map/ppermute | solution.py:805
  31.8 45.5 %collective-permute-start.19 = (bf16[1024,512]{1,0:T(8,128)(2,1)}, bf16[1024,512]{1,0:T(8,128)(2,1)}, u32[]{:S(2)}, u32[]{:S(2)}) collective-permute-start(bf16[1024,512]{1,0:T(8,128)(2,1)} %wd_a.1), channel_id=1, source_target_pairs={{0,1},{1,0},{2,3},{3,2},{4,5},{5,4},{6,7},{7,6},{8,9},{9,8},{10,11... | collective-permute-start | bytes 3145736 | tf_op jit(solution)/shard_map/ppermute | solution.py:805
  53.3 23.9 %collective-permute-start.11 = (bf16[256,512]{1,0:T(8,128)(2,1)}, bf16[256,512]{1,0:T(8,128)(2,1)S(1)}, u32[]{:S(2)}, u32[]{:S(2)}) collective-permute-start(bf16[256,512]{1,0:T(8,128)(2,1)} %get-tuple-element.87.q_ref.refs_0_), channel_id=1, source_target_pairs={{8,0},{10,2},{12,4},{14,6},{16,8},{18,10},{20,12},{22,14},{24,16},... | collective-permute-start | bytes 786440 | tf_op jit(solution)/shard_map/ppermute | solution.py:824
  55.3 21.9 %collective-permute-start.13 = (bf16[256,512]{1,0:T(8,128)(2,1)}, bf16[256,512]{1,0:T(8,128)(2,1)S(1)}, u32[]{:S(2)}, u32[]{:S(2)}) collective-permute-start(bf16[256,512]{1,0:T(8,128)(2,1)} %get-tuple-element.87.q_ref.refs_0_), channel_id=1, source_target_pairs={{16,0},{18,2},{20,4},{22,6},{24,8},{26,10},{28,12},{30,14},{17,1},... | collective-permute-start | bytes 786440 | tf_op jit(solution)/shard_map/ppermute | solution.py:824
  56.6 20.6 %collective-permute-start.17 = (bf16[256,512]{1,0:T(8,128)(2,1)S(1)}, bf16[256,512]{1,0:T(8,128)(2,1)S(1)}, u32[]{:S(2)}, u32[]{:S(2)}) collective-permute-start(bf16[256,512]{1,0:T(8,128)(2,1)S(1)} %copy-done.32), channel_id=1, source_target_pairs={{0,1},{1,0},{2,3},{3,2},{4,5},{5,4},{6,7},{7,6},{8,9},{9,8},{10,11... | collective-permute-start | bytes 786440 | tf_op jit(solution)/shard_map/ppermute | solution.py:805
  112.7 19.1 %collective-permute-start.21 = (bf16[288,512]{1,0:T(8,128)(2,1)}, bf16[288,512]{1,0:T(8,128)(2,1)S(1)}, u32[]{:S(2)}, u32[]{:S(2)}) collective-permute-start(bf16[288,512]{1,0:T(8,128)(2,1)} %get-tuple-element.153), channel_id=1, source_target_pairs={{0,1},{1,0},{2,3},{3,2},{4,5},{5,4},{6,7},{7,6},{8,9},{9,8},{10,11... | collective-permute-start | bytes 884744 | tf_op jit(solution)/shard_map/ppermute | solution.py:805
  112.7 19.1 %collective-permute-start.23 = (bf16[288,512]{1,0:T(8,128)(2,1)}, bf16[288,512]{1,0:T(8,128)(2,1)}, u32[]{:S(2)}, u32[]{:S(2)}) collective-permute-start(bf16[288,512]{1,0:T(8,128)(2,1)} %get-tuple-element.152), channel_id=1, source_target_pairs={{0,1},{1,0},{2,3},{3,2},{4,5},{5,4},{6,7},{7,6},{8,9},{9,8},{10,11... | collective-permute-start | bytes 884744 | tf_op jit(solution)/shard_map/ppermute | solution.py:805
  148.2 32.5 %collective-permute-start.42 = (bf16[608,512]{1,0:T(8,128)(2,1)}, bf16[608,512]{1,0:T(8,128)(2,1)S(1)}, u32[]{:S(2)}, u32[]{:S(2)}) collective-permute-start(bf16[608,512]{1,0:T(8,128)(2,1)} %get-tuple-element.111), channel_id=1, source_target_pairs={{0,4},{2,6},{4,0},{6,2},{8,12},{10,14},{12,8},{14,10},{16,20},{18,... | collective-permute-start | bytes 1867784 | tf_op jit(solution)/shard_map/ppermute | solution.py:754
  148.8 31.9 %collective-permute-start.43 = (bf16[608,512]{1,0:T(8,128)(2,1)}, bf16[608,512]{1,0:T(8,128)(2,1)S(1)}, u32[]{:S(2)}, u32[]{:S(2)}) collective-permute-start(bf16[608,512]{1,0:T(8,128)(2,1)} %get-tuple-element.112), channel_id=1, source_target_pairs={{0,6},{2,4},{4,2},{6,0},{8,14},{10,12},{12,10},{14,8},{16,22},{18,... | collective-permute-start | bytes 1867784 | tf_op jit(solution)/shard_map/ppermute | solution.py:754
  156.2 32.0 %collective-permute-start.29 = (bf16[352,512]{1,0:T(8,128)(2,1)}, bf16[352,512]{1,0:T(8,128)(2,1)S(1)}, u32[]{:S(2)}, u32[]{:S(2)}) collective-permute-start(bf16[352,512]{1,0:T(8,128)(2,1)} %get-tuple-element.120), channel_id=1, source_target_pairs={{0,2},{2,0},{4,6},{6,4},{8,10},{10,8},{12,14},{14,12},{16,18},{18,... | collective-permute-start | bytes 1081352 | tf_op jit(solution)/shard_map/ppermute | solution.py:754
  156.8 39.1 %collective-permute-start.30 = (bf16[352,512]{1,0:T(8,128)(2,1)}, bf16[352,512]{1,0:T(8,128)(2,1)S(1)}, u32[]{:S(2)}, u32[]{:S(2)}) collective-permute-start(bf16[352,512]{1,0:T(8,128)(2,1)} %get-tuple-element.121), channel_id=1, source_target_pairs={{0,4},{2,6},{4,0},{6,2},{8,12},{10,14},{12,8},{14,10},{16,20},{18,... | collective-permute-start | bytes 1081352 | tf_op jit(solution)/shard_map/ppermute | solution.py:754
  164.5 31.4 %collective-permute-start.31 = (bf16[352,512]{1,0:T(8,128)(2,1)}, bf16[352,512]{1,0:T(8,128)(2,1)S(1)}, u32[]{:S(2)}, u32[]{:S(2)}) collective-permute-start(bf16[352,512]{1,0:T(8,128)(2,1)} %get-tuple-element.122), channel_id=1, source_target_pairs={{0,6},{2,4},{4,2},{6,0},{8,14},{10,12},{12,10},{14,8},{16,22},{18,... | collective-permute-start | bytes 1081352 | tf_op jit(solution)/shard_map/ppermute | solution.py:754
  165.1 50.4 %all-to-all-start.1 = ((bf16[16,16,512]{2,1,0:T(8,128)(2,1)}), bf16[16,16,512]{2,1,0:T(8,128)(2,1)S(1)}, u32[]{:S(2)}, u32[]{:S(2)}) async-start(bf16[16,16,512]{2,1,0:T(8,128)(2,1)} %bitcast.16), calls=%async_computation.1 | async-start | bytes 524288 | tf_op jit(solution)/shard_map/all_to_all | solution.py:972
  184.6 18.6 %collective-permute-start.45 = (bf16[152,512]{1,0:T(8,128)(2,1)}, bf16[152,512]{1,0:T(8,128)(2,1)S(1)}, u32[]{:S(2)}, u32[]{:S(2)}) collective-permute-start(bf16[152,512]{1,0:T(8,128)(2,1)} %get-tuple-element.140), channel_id=1, source_target_pairs={{0,16},{2,18},{4,20},{6,22},{8,24},{10,26},{12,28},{14,30},{16,0},... | collective-permute-start | bytes 466952 | tf_op jit(solution)/shard_map/ppermute | solution.py:754
  203.3 29.6 %collective-permute-start.27 = (bf16[128,512]{1,0:T(8,128)(2,1)S(1)}, bf16[128,512]{1,0:T(8,128)(2,1)S(1)}, u32[]{:S(2)}, u32[]{:S(2)}) collective-permute-start(bf16[128,512]{1,0:T(8,128)(2,1)S(1)} %get-tuple-element.162), channel_id=1, source_target_pairs={{0,0},{4,1},{2,2},{6,3},{1,4},{5,5},{3,6},{7,7},{8,8},{12,9},{10,1... | collective-permute-start | bytes 393224 | tf_op jit(solution)/shard_map/ppermute | solution.py:981
  206.8 26.5 %collective-permute-start.47 = (bf16[152,512]{1,0:T(8,128)(2,1)}, bf16[152,512]{1,0:T(8,128)(2,1)S(1)}, u32[]{:S(2)}, u32[]{:S(2)}) collective-permute-start(bf16[152,512]{1,0:T(8,128)(2,1)} %cut.11.refs_0_), channel_id=1, source_target_pairs={{0,8},{2,10},{4,12},{6,14},{8,0},{10,2},{12,4},{14,6},{16,24},{18,... | collective-permute-start | bytes 466952 | tf_op jit(solution)/shard_map/ppermute | solution.py:754
  217.6 17.1 %collective-permute-start.48 = (bf16[152,512]{1,0:T(8,128)(2,1)}, bf16[152,512]{1,0:T(8,128)(2,1)S(1)}, u32[]{:S(2)}, u32[]{:S(2)}) collective-permute-start(bf16[152,512]{1,0:T(8,128)(2,1)} %cut.11.refs_0_), channel_id=1, source_target_pairs={{0,16},{2,18},{4,20},{6,22},{8,24},{10,26},{12,28},{14,30},{16,0},... | collective-permute-start | bytes 466952 | tf_op jit(solution)/shard_map/ppermute | solution.py:754
  234.8 20.6 %collective-permute-start.39 = (bf16[352,512]{1,0:T(8,128)(2,1)}, bf16[352,512]{1,0:T(8,128)(2,1)S(1)}, u32[]{:S(2)}, u32[]{:S(2)}) collective-permute-start(bf16[352,512]{1,0:T(8,128)(2,1)} %place.4.refs_0_), channel_id=1, source_target_pairs={{0,4},{2,6},{4,0},{6,2},{8,12},{10,14},{12,8},{14,10},{16,20},{18,... | collective-permute-start | bytes 1081352 | tf_op jit(solution)/shard_map/ppermute | solution.py:754
  237.5 17.8 %collective-permute-start.40 = (bf16[352,512]{1,0:T(8,128)(2,1)}, bf16[352,512]{1,0:T(8,128)(2,1)S(1)}, u32[]{:S(2)}, u32[]{:S(2)}) collective-permute-start(bf16[352,512]{1,0:T(8,128)(2,1)} %place.4.refs_0_), channel_id=1, source_target_pairs={{0,6},{2,4},{4,2},{6,0},{8,14},{10,12},{12,10},{14,8},{16,22},{18,... | collective-permute-start | bytes 1081352 | tf_op jit(solution)/shard_map/ppermute | solution.py:754
  245.5 21.1 %collective-permute-start.50 = (bf16[608,512]{1,0:T(8,128)(2,1)}, bf16[608,512]{1,0:T(8,128)(2,1)S(1)}, u32[]{:S(2)}, u32[]{:S(2)}) collective-permute-start(bf16[608,512]{1,0:T(8,128)(2,1)} %place.6.refs_0_), channel_id=1, source_target_pairs={{0,2},{2,0},{4,6},{6,4},{8,10},{10,8},{12,14},{14,12},{16,18},{18,... | collective-permute-start | bytes 1867784 | tf_op jit(solution)/shard_map/ppermute | solution.py:754
  247.3 33.9 %collective-permute-start.51 = (bf16[608,512]{1,0:T(8,128)(2,1)}, bf16[608,512]{1,0:T(8,128)(2,1)S(1)}, u32[]{:S(2)}, u32[]{:S(2)}) collective-permute-start(bf16[608,512]{1,0:T(8,128)(2,1)} %place.6.refs_0_), channel_id=1, source_target_pairs={{0,4},{2,6},{4,0},{6,2},{8,12},{10,14},{12,8},{14,10},{16,20},{18,... | collective-permute-start | bytes 1867784 | tf_op jit(solution)/shard_map/ppermute | solution.py:754
  247.3 33.9 %collective-permute-start.52 = (bf16[608,512]{1,0:T(8,128)(2,1)}, bf16[608,512]{1,0:T(8,128)(2,1)S(1)}, u32[]{:S(2)}, u32[]{:S(2)}) collective-permute-start(bf16[608,512]{1,0:T(8,128)(2,1)} %place.6.refs_0_), channel_id=1, source_target_pairs={{0,6},{2,4},{4,2},{6,0},{8,14},{10,12},{12,10},{14,8},{16,22},{18,... | collective-permute-start | bytes 1867784 | tf_op jit(solution)/shard_map/ppermute | solution.py:754
  (92 other events, 1016.0 us)

commit v2 on v1

--- a/solution.py
+++ b/solution.py
@@ -79,21 +79,21 @@
 
 def stack_vectors(vectors, width):
     row, at = iota((16, width), 0), 0
-    table = jnp.zeros((16, width), F32)
+    table = jnp.zeros((16, width), BF)
     for x in vectors:
         for n in range(x.shape[0] // width):
-            part = x[n * width : n * width + width].astype(F32)
+            part = x[n * width : n * width + width]
             table = jnp.where(row == at, part[None, :], table)
             at += 1
-    return table
+    return table.astype(F32)
 
 
 def iota(shape, axis):
     return lax.broadcasted_iota(jnp.int32, shape, axis)
 
 
-def params(limit=56):
-    return pltpu.CompilerParams(vmem_limit_bytes=limit * 1024 * 1024)
+def params(cols=0):
+    return pltpu.CompilerParams(vmem_limit_bytes=(32 if cols <= 2048 else 56) * 1024 * 1024)
 
 
 def lasting(us):
@@ -166,7 +166,7 @@
             scratch_shapes=[square, square, square, pltpu.VMEM((rows, width), BF)],
         ),
         out_shape=[flat] * 3 + [jax.ShapeDtypeStruct((rows, width), F32), flat] if own else [flat] * 2,
-        compiler_params=params(),
+        compiler_params=params(pos[0].shape[0] + blocks * rows),
         cost_estimate=lasting(2 * blocks + 2),
         name="project",
     )(info, *args)
@@ -300,7 +300,7 @@
             jax.ShapeDtypeStruct((rows, width), F32),
             jax.ShapeDtypeStruct((16, width), BF),
         ],
-        compiler_params=params(),
+        compiler_params=params(cols),
         cost_estimate=lasting(12),
         name="attend_forward",
     )(info, q, kp, k, vp, v)
@@ -560,7 +560,7 @@
             ],
         ),
         out_shape=outs,
-        compiler_params=params(),
+        compiler_params=params(cols),
         cost_estimate=lasting(10),
         name="attend_query",
     )(info, q, kp, k, vp, v, logs, da, exact, dz1, *wq)
@@ -675,7 +675,7 @@
             ],
         ),
         out_shape=outs,
-        compiler_params=params(),
+        compiler_params=params(cols),
         cost_estimate=lasting(15),
         name="last",
     )(info, *q_parts, *da_parts, k, v, *rest)
@@ -907,20 +907,21 @@
     sends = jnp.transpose(streams, (2, 0, 1, 3, 4)).reshape(rows, width)
     arrived = lax.all_to_all(sends, "ctx", split_axis=0, concat_axis=0, tiled=True)
 
-    own = after(arrived, own)
     fixed_args = (pos, wk, wv, wq, vec)
     far = send_window(own, reach, chips, 1)
+    own = after(arrived, own)
     k, v, q, hidden, low = project(info, [own], 0, True, *fixed_args)
+    far[1:] = after(k, far[1:])
+
     earlier = both_cores(far, core, 1)[::-1]
     before = len(earlier) * rows
-    far_q = send_window(after(far[1:], q), reach, chips, -1)
     kp, vp = project(info, earlier, -before, False, *fixed_args)
+    far_q = send_window(after(kp, q), reach, chips, -1)
     att, exact, logs, log_stats = attend_forward(info, q, kp, k, vp, v)
-    exact = after(far_q[1:], exact)
-    later_q = [q] + both_cores(far_q, core, -1)
     leaving, da_msg, dz1, active, df, h1, du, do, sums = feed_forward(
         info, att, exact, log_stats, hidden, arrived, mine, wo, wu, wd, vec
     )
+    da_msg, do, leaving = after(far_q[1:], (da_msg, do, leaving))
     far_da = [da_msg, next_chip(da_msg, chips, -1)]
 
     half = width // 2
@@ -943,24 +944,33 @@
     exact = after(pieces, exact)
     terms = one.scatter(pieces, 0)
     dq, dh = attend_query(info, q, kp, k, vp, v, logs, da_msg, exact, dz1, wq)
+    far_da[1:], far_q[1:] = after(dq, (far_da[1:], far_q[1:]))
     later_da = [da_msg] + both_cores(far_da, core, -1)
+    later_q = [q] + both_cores(far_q, core, -1)
     keep, give, dh0_low = last(info, later_q, later_da, k, v, low, dq, dh, wk, wv, quarter_last, longest)
 
+    keep, give, dh0_low = after(terms[1:], (keep, give, dh0_low))
     terms_last = [keep, swap_core(give)]
     for level in range(levels):
-        pieces_last = two.cut(terms_last, level)
-        terms_last = two.scatter(pieces_last, level)
-        pieces = one.cut(after(pieces_last, terms), level + 1)
+        pieces = one.cut(terms, level + 1)
         if level + 1 < levels:
             terms = one.scatter(pieces, level + 1)
+        pieces_last = two.cut(after(pieces, terms_last), level)
+        terms_last = two.scatter(pieces_last, level)
         if level == 0:
             leaving, dh0_low = after(pieces_last, (leaving, dh0_low))
     held = pieces[0]
-    (held_last,) = two.cut(terms_last, levels)
+    parts = one.gather(held, levels - 1)
     for level in reversed(range(levels)):
-        parts = one.gather(held, level)
+        if level == levels - 1:
+            held = one.place(after(pieces_last, parts), level)
+            (held_last,) = two.cut(after(held, terms_last), levels)
+        else:
+            held = one.place(parts, level)
         parts_last = two.gather(held_last, level)
-        held = one.place(parts, level)
+        if level:
+            parts = one.gather(held, level - 1)
+            parts_last = after(parts[1:], parts_last)
         held_last = two.place(parts_last, level)
     g_down, g_up, g_out, early = held
     g_key, g_value, g_query, g_pos, late = held_last

time: 296 us -> 247 us (0.83)
  waiting for transfers between devices: 103 us -> 66.7 us
  Pallas kernels: 95.1 us -> 62.2 us
  local copies, waits for them, and re-layouts: 23.1 us -> 34 us
  starting transfers between devices: 60 us -> 67.5 us
  other arithmetic: 9.98 us -> 13.5 us
    ppermute x24, waiting for transfers between devices: 63.9 us -> 46 us  [exchange(): lax.ppermute(piece, 'ctx', [(i, i ^ (k + 1) * stride) for i in range(rank...]
    pallas_call x6, Pallas kernels: 17.4 us -> 6.07 us  [cut(): pl.pallas_call(functools.partial(cut_kernel, terms=len(terms), radix=radi...]
    unnamed x125 -> x161, local copies, waits for them, and re-layouts: 14 us -> 22.8 us
    all_to_all x1, waiting for transfers between devices: 7.63 us -> 0.01 us  [shards(): lax.all_to_all(sends, 'ctx', split_axis=0, concat_axis=0, tiled=True)]
    pallas_call x4, Pallas kernels: 12.5 us -> 4.88 us  [place(): pl.pallas_call(functools.partial(place_kernel, radix=radix, sizes=sizes),...]
    ppermute x2, waiting for transfers between devices: 11.3 us -> 4.12 us  [next_chip(): lax.ppermute(block, 'ctx', pairs if step > 0 else [(b, a) for a, b in pai...]
    ppermute x24, starting transfers between devices: 23.9 us -> 30 us  [exchange(): lax.ppermute(piece, 'ctx', [(i, i ^ (k + 1) * stride) for i in range(rank...]
    ppermute x19, waiting for transfers between devices: 1.44 us -> 6.7 us  [swap_core(): return lax.ppermute(x, 'fsdp', SWAP)]
  transfers between devices with their start and end apart: 55 -> 55, of which waited for: 20 -> 20; matrix products, arithmetic and copies ran while one was open for 4% -> 9% of each run, Pallas kernels for 22% -> 24%
where the time goes in v2:
time: 247 us; the launch traced here: 246 us
  starting transfers between devices  67.5 us (27%)
  waiting for transfers between devices  66.7 us (27%)
  Pallas kernels  62.2 us (25%)
  local copies, waits for them, and re-layouts  34 us (14%)
  other arithmetic  13.5 us (5%)
    ppermute x24, waiting for transfers between devices, exchange(): lax.ppermute(piece, 'ctx', [(i, i ^ (k + 1) * stride) for i in range(rank...  46 us
    ppermute x24, starting transfers between devices, exchange(): lax.ppermute(piece, 'ctx', [(i, i ^ (k + 1) * stride) for i in range(rank...  30 us
    unnamed x161, local copies, waits for them, and re-layouts  22.8 us
    pallas_call x1, Pallas kernels, last(): pl.pallas_call(functools.partial(last_kernel, reach=count // 2, quarter=q...  13.3 us
    pallas_call x1, Pallas kernels, attend_forward(): pl.pallas_call(forward_kernel, grid_spec=pltpu.PrefetchScalarGridSpec(num...  10.4 us
    ppermute x4, waiting for transfers between devices, send_window(): far.append(lax.ppermute(own, 'ctx', pairs))  9.87 us
    pallas_call x1, Pallas kernels, feed_forward(): pl.pallas_call(ffn_kernel, grid_spec=pltpu.PrefetchScalarGridSpec(num_sca...  8.14 us
    ppermute x4, starting transfers between devices, send_window(): far.append(lax.ppermute(own, 'ctx', pairs))  8.02 us
  transfers between devices with their start and end apart: 55, of which 20 were waited for; matrix products, arithmetic and copies ran while one was open for 9% of the time, Pallas kernels for 24%

profile of v2, /device:TPU:16, one launch (start us, length us, event | category | flops | bytes accessed | tf_op | source)
XLA Modules:
  0.0 245.6 jit_solution(5833773764604576904)
XLA Ops:
  13.7 6.8 %all-to-all-start = ((bf16[16,16,512]{2,1,0:T(8,128)(2,1)}), bf16[16,16,512]{2,1,0:T(8,128)(2,1)S(1)}, u32[]{:S(2)}, u32[]{:S(2)}) async-start(bf16[16,16,512]{2,1,0:T(8,128)(2,1)} %bitcast.13), calls=%async_computation | async-start | bytes 524288 | tf_op jit(solution)/shard_map/all_to_all | solution.py:908
  25.3 3.4 %collective-permute-start.9 = (bf16[256,512]{1,0:T(8,128)(2,1)}, bf16[256,512]{1,0:T(8,128)(2,1)S(1)}, u32[]{:S(2)}, u32[]{:S(2)}) collective-permute-start(bf16[256,512]{1,0:T(8,128)(2,1)} %pad_maximum_fusion.refs_0_), channel_id=1, source_target_pairs={{0,8},{2,10},{4,12},{6,14},{8,16},{10,18},{12,20},{14,22},{16,24},... | collective-permute-start | bytes 786440 | tf_op jit(solution)/shard_map/ppermute | solution.py:824
  36.8 9.9 %collective-permute-done.9.refs_2_ = bf16[256,512]{1,0:T(8,128)(2,1)S(1)} collective-permute-done((bf16[256,512]{1,0:T(8,128)(2,1)}, bf16[256,512]{1,0:T(8,128)(2,1)S(1)}, u32[]{:S(2)}, u32[]{:S(2)}) %collective-permute-start.9) | collective-permute-done | bytes 262176 | tf_op jit(solution)/shard_map/ppermute | solution.py:824
  53.6 4.2 %project.3 = (bf16[1024,512]{1,0:T(8,128)(2,1)S(1)}, bf16[1024,512]{1,0:T(8,128)(2,1)S(1)}) custom-call(s32[11]{0:T(128)S(1)} %copy-done.68, bf16[256,512]{1,0:T(8,128)(2,1)S(1)} %copy-done.45, bf16[256,512]{1,0:T(8,128)(2,1)S(1)} %collective-permute-done.11.refs_1_, bf16[256,512]{1,0:T(8,128)(2,1)S(1)} %copy-done.47, ...), custom_call_target="tpu_custom_call" | custom-call | flops 10 | bytes 10 | tf_op jit(solution)/shard_map/project/pallas_call | solution.py:159
  66.7 10.4 %attend_forward.1 = (bf16[256,512]{1,0:T(8,128)(2,1)S(1)}, f32[256,512]{1,0:T(8,128)S(1)}, f32[256,512]{1,0:T(8,128)S(1)}, bf16[16,512]{1,0:T(8,128)(2,1)S(1)}) custom-call(s32[11]{0:T(128)S(1)} %copy-done.69, bf16[256,512]{1,0:T(8,128)(2,1)S(1)} %get-tuple-element.115.q_ref.refs_0_, bf16[1024,512]{1,0:T(8,128)(2,1)S(1)} %get-tuple-element.111.kp_ref, ...), custom_call_target="tpu_custom_call" | custom-call | flops 12 | bytes 12 | tf_op jit(solution)/shard_map/attend_forward/pallas_call | solution.py:284
  78.8 8.1 %feed_forward.1 = (bf16[256,512]{1,0:T(8,128)(2,1)}, bf16[288,512]{1,0:T(8,128)(2,1)S(1)}, f32[256,512]{1,0:T(8,128)S(1)}, bf16[256,2048]{1,0:T(8,128)(2,1)S(1)}...) custom-call(s32[11]{0:T(128)S(1)} %copy-done.69, ...), custom_call_target="tpu_custom_call" | custom-call | flops 10 | bytes 10 | tf_op jit(solution)/shard_map/feed_forward/pallas_call | solution.py:400
  89.1 4.8 %ffn_grads.1 = (bf16[2432,512]{1,0:T(8,128)(2,1)S(1)}, bf16[2432,512]{1,0:T(8,128)(2,1)}) custom-call(s32[11]{0:T(128)S(1)} %copy-done.69, bf16[256,512]{1,0:T(8,128)(2,1)S(1)} %get-tuple-element.114.a_ref.a_own.a_other, bf16[256,512]{1,0:T(8,128)(2,1)S(1)} %get-tuple-element.114.a_ref.a_own.a_other, bf16[256,512]{1,0:T(8,128)(2,1)S(1)} %get-tuple-element.122.do_ref, ...), custom_call_target="tpu_custom_call" | custom-call | flops 10 | bytes 10 | tf_op jit(solution)/shard_map/ffn_grads/pallas_call | solution.py:472
  93.9 4.1 %collective-permute-done.18.refs_7_ = bf16[288,512]{1,0:T(8,128)(2,1)} collective-permute-done((bf16[288,512]{1,0:T(8,128)(2,1)S(1)}, bf16[288,512]{1,0:T(8,128)(2,1)}, u32[]{:S(2)}, u32[]{:S(2)}) %collective-permute-start.18) | collective-permute-done | bytes 294944 | tf_op jit(solution)/shard_map/ppermute | solution.py:814
  100.3 2.9 %collective-permute-done.19.refs_1_.refs_3_.refs_5_.refs_7_ = bf16[2432,512]{1,0:T(8,128)(2,1)} collective-permute-done((bf16[2432,512]{1,0:T(8,128)(2,1)}, bf16[2432,512]{1,0:T(8,128)(2,1)}, u32[]{:S(2)}, u32[]{:S(2)}) %collective-permute-start.19) | collective-permute-done | bytes 2490400 | tf_op jit(solution)/shard_map/ppermute | solution.py:805
  103.2 3.4 %cut.6 = (f32[608,512]{1,0:T(8,128)S(1)}, bf16[608,512]{1,0:T(8,128)(2,1)S(1)}, bf16[608,512]{1,0:T(8,128)(2,1)S(1)}, bf16[608,512]{1,0:T(8,128)(2,1)S(1)}) custom-call(s32[1]{0:T(128)} %bitcast.digit_ref, bf16[2432,512]{1,0:T(8,128)(2,1)S(1)} %get-tuple-element.128.refs_0_.refs_2_.refs_4_.refs_6_, ...), custom_call_target="tpu_custom_call" | custom-call | flops 3 | bytes 3 | tf_op jit(solution)/shard_map/cut/pallas_call | solution.py:701
  111.2 7.9 %attend_query.1 = (bf16[256,512]{1,0:T(8,128)(2,1)S(1)}, f32[256,512]{1,0:T(8,128)S(1)}) custom-call(s32[11]{0:T(128)S(1)} %copy-done.70, bf16[256,512]{1,0:T(8,128)(2,1)S(1)} %get-tuple-element.115.q_ref.refs_0_, bf16[1024,512]{1,0:T(8,128)(2,1)S(1)} %copy-done.9, bf16[256,512]{1,0:T(8,128)(2,1)S(1)} %copy-done.30, bf16[1024,512]{1,0:T(8,128)(2,1)S(1)} %copy-done.11, ...), custom_call_target="tpu_custom_call" | custom-call | flops 10 | bytes 10 | tf_op jit(solution)/shard_map/attend_query/pallas_call | solution.py:547
  123.1 13.3 %last.1 = (bf16[1408,512]{1,0:T(8,128)(2,1)S(1)}, bf16[1408,512]{1,0:T(8,128)(2,1)}, bf16[256,512]{1,0:T(8,128)(2,1)S(1)}) custom-call(s32[11]{0:T(128)S(1)} %copy-done.70, bf16[256,512]{1,0:T(8,128)(2,1)S(1)} %get-tuple-element.115.q_ref.refs_0_, bf16[256,512]{1,0:T(8,128)(2,1)S(1)} %collective-permute-done.24.refs_1_, bf16[256,512]{1,0:T(8,128)(2,1)S(1)} %copy-done.41, ...), custom_call_target="tpu_custom_call" | custom-call | flops 15 | bytes 15 | tf_op jit(solution)/shard_map/last/pallas_call | solution.py:660
  147.8 7.6 %all-to-all-start.1 = ((bf16[16,16,512]{2,1,0:T(8,128)(2,1)}), bf16[16,16,512]{2,1,0:T(8,128)(2,1)}, u32[]{:S(2)}, u32[]{:S(2)}) async-start(bf16[16,16,512]{2,1,0:T(8,128)(2,1)} %bitcast.17), calls=%async_computation.1 | async-start | bytes 524288 | tf_op jit(solution)/shard_map/all_to_all | solution.py:982
  155.6 2.7 %collective-permute-start.34 = (bf16[152,512]{1,0:T(8,128)(2,1)}, bf16[152,512]{1,0:T(8,128)(2,1)S(1)}, u32[]{:S(2)}, u32[]{:S(2)}) collective-permute-start(bf16[152,512]{1,0:T(8,128)(2,1)} %copy-done.73), channel_id=1, source_target_pairs={{0,24},{2,26},{4,28},{6,30},{8,16},{10,18},{12,20},{14,22},{16,8},... | collective-permute-start | bytes 466952 | tf_op jit(solution)/shard_map/ppermute | solution.py:754
  161.3 10.9 %collective-permute-done.33.refs_2_ = bf16[152,512]{1,0:T(8,128)(2,1)S(1)} collective-permute-done((bf16[152,512]{1,0:T(8,128)(2,1)}, bf16[152,512]{1,0:T(8,128)(2,1)S(1)}, u32[]{:S(2)}, u32[]{:S(2)}) %collective-permute-start.33) | collective-permute-done | bytes 155680 | tf_op jit(solution)/shard_map/ppermute | solution.py:754
  172.2 3.2 %collective-permute-done.34.refs_3_ = bf16[152,512]{1,0:T(8,128)(2,1)S(1)} collective-permute-done((bf16[152,512]{1,0:T(8,128)(2,1)}, bf16[152,512]{1,0:T(8,128)(2,1)S(1)}, u32[]{:S(2)}, u32[]{:S(2)}) %collective-permute-start.34) | collective-permute-done | bytes 155680 | tf_op jit(solution)/shard_map/ppermute | solution.py:754
  176.5 2.9 %collective-permute-start.39 = (bf16[152,512]{1,0:T(8,128)(2,1)S(1)}, bf16[152,512]{1,0:T(8,128)(2,1)S(1)}, u32[]{:S(2)}, u32[]{:S(2)}) collective-permute-start(bf16[152,512]{1,0:T(8,128)(2,1)S(1)} %cut.9.refs_0_), channel_id=1, source_target_pairs={{0,16},{2,18},{4,20},{6,22},{8,24},{10,26},{12,28},{14,30},{16,0},... | collective-permute-start | bytes 466952 | tf_op jit(solution)/shard_map/ppermute | solution.py:754
  183.6 6.3 %collective-permute-done.39.refs_2_ = bf16[152,512]{1,0:T(8,128)(2,1)S(1)} collective-permute-done((bf16[152,512]{1,0:T(8,128)(2,1)S(1)}, bf16[152,512]{1,0:T(8,128)(2,1)S(1)}, u32[]{:S(2)}, u32[]{:S(2)}) %collective-permute-start.39) | collective-permute-done | bytes 155680 | tf_op jit(solution)/shard_map/ppermute | solution.py:754
  190.0 3.1 %collective-permute-done.40.refs_3_ = bf16[152,512]{1,0:T(8,128)(2,1)S(1)} collective-permute-done((bf16[152,512]{1,0:T(8,128)(2,1)S(1)}, bf16[152,512]{1,0:T(8,128)(2,1)S(1)}, u32[]{:S(2)}, u32[]{:S(2)}) %collective-permute-start.40) | collective-permute-done | bytes 155680 | tf_op jit(solution)/shard_map/ppermute | solution.py:754
  208.8 4.4 %collective-permute-start.47 = (bf16[88,512]{1,0:T(8,128)(2,1)S(1)}, bf16[88,512]{1,0:T(8,128)(2,1)S(1)}, u32[]{:S(2)}, u32[]{:S(2)}) collective-permute-start(bf16[88,512]{1,0:T(8,128)(2,1)S(1)} %cut.11.refs_0_), channel_id=1, source_target_pairs={{0,8},{2,10},{4,12},{6,14},{8,0},{10,2},{12,4},{14,6},{16,24},{18,... | collective-permute-start | bytes 270344 | tf_op jit(solution)/shard_map/ppermute | solution.py:754
  216.5 6.1 %collective-permute-done.42.refs_2_ = bf16[608,512]{1,0:T(8,128)(2,1)S(1)} collective-permute-done((bf16[608,512]{1,0:T(8,128)(2,1)S(1)}, bf16[608,512]{1,0:T(8,128)(2,1)S(1)}, u32[]{:S(2)}, u32[]{:S(2)}) %collective-permute-start.42) | collective-permute-done | bytes 622624 | tf_op jit(solution)/shard_map/ppermute | solution.py:754
  222.6 2.6 %place.7 = (f32[1024,512]{1,0:T(8,128)}, f32[256,2048]{1,0:T(8,128)}, f32[256,512]{1,0:T(8,128)}, f32[128,512]{1,0:T(8,128)S(1)}) custom-call(s32[1]{0:T(128)} %bitcast.digit_ref, bf16[608,512]{1,0:T(8,128)(2,1)S(1)} %place.4.refs_0_, bf16[608,512]{1,0:T(8,128)(2,1)S(1)} %collective-permute-done.41.refs_1_, ...), custom_call_target="tpu_custom_call" | custom-call | flops 3 | bytes 3 | tf_op jit(solution)/shard_map/place/pallas_call | solution.py:732
  232.9 3.9 %collective-permute-done.50.refs_1_ = bf16[352,512]{1,0:T(8,128)(2,1)S(1)} collective-permute-done((bf16[352,512]{1,0:T(8,128)(2,1)S(1)}, bf16[352,512]{1,0:T(8,128)(2,1)S(1)}, u32[]{:S(2)}, u32[]{:S(2)}) %collective-permute-start.50) | collective-permute-done | bytes 360480 | tf_op jit(solution)/shard_map/ppermute | solution.py:754
  236.8 5.7 %collective-permute-done.51.refs_2_ = bf16[352,512]{1,0:T(8,128)(2,1)S(1)} collective-permute-done((bf16[352,512]{1,0:T(8,128)(2,1)S(1)}, bf16[352,512]{1,0:T(8,128)(2,1)S(1)}, u32[]{:S(2)}, u32[]{:S(2)}) %collective-permute-start.51) | collective-permute-done | bytes 360480 | tf_op jit(solution)/shard_map/ppermute | solution.py:754
  (307 shorter events, 105.3 us)
Async XLA Ops:
  1.8 18.7 %collective-permute-start.2 = (bf16[128,512]{1,0:T(8,128)(2,1)S(1)}, bf16[128,512]{1,0:T(8,128)(2,1)S(1)}, u32[]{:S(2)}, u32[]{:S(2)}) collective-permute-start(bf16[128,512]{1,0:T(8,128)(2,1)S(1)} %get-tuple-element.216), channel_id=1, source_target_pairs={{0,0},{1,4},{2,2},{3,6},{4,1},{5,5},{6,3},{7,7},{8,8},{9,12},{10,1... | collective-permute-start | bytes 393224 | tf_op jit(solution)/shard_map/ppermute | solution.py:881
  2.5 18.1 %collective-permute-start.3 = (bf16[128,512]{1,0:T(8,128)(2,1)S(1)}, bf16[128,512]{1,0:T(8,128)(2,1)S(1)}, u32[]{:S(2)}, u32[]{:S(2)}) collective-permute-start(bf16[128,512]{1,0:T(8,128)(2,1)S(1)} %get-tuple-element.217), channel_id=1, source_target_pairs={{0,2},{1,6},{2,0},{3,4},{4,3},{5,7},{6,1},{7,5},{8,10},{9,14},{10,... | collective-permute-start | bytes 393224 | tf_op jit(solution)/shard_map/ppermute | solution.py:882
  13.7 17.6 %all-to-all-start = ((bf16[16,16,512]{2,1,0:T(8,128)(2,1)}), bf16[16,16,512]{2,1,0:T(8,128)(2,1)S(1)}, u32[]{:S(2)}, u32[]{:S(2)}) async-start(bf16[16,16,512]{2,1,0:T(8,128)(2,1)} %bitcast.13), calls=%async_computation | async-start | bytes 524288 | tf_op jit(solution)/shard_map/all_to_all | solution.py:908
  23.5 54.5 %collective-permute-start.16 = (bf16[256,2048]{1,0:T(8,128)(2,1)}, bf16[256,2048]{1,0:T(8,128)(2,1)}, u32[]{:S(2)}, u32[]{:S(2)}) collective-permute-start(bf16[256,2048]{1,0:T(8,128)(2,1)} %wu_a.1), channel_id=1, source_target_pairs={{0,1},{1,0},{2,3},{3,2},{4,5},{5,4},{6,7},{7,6},{8,9},{9,8},{10,11... | collective-permute-start | bytes 3145736 | tf_op jit(solution)/shard_map/ppermute | solution.py:805
  23.6 54.3 %collective-permute-start.17 = (bf16[1024,512]{1,0:T(8,128)(2,1)}, bf16[1024,512]{1,0:T(8,128)(2,1)}, u32[]{:S(2)}, u32[]{:S(2)}) collective-permute-start(bf16[1024,512]{1,0:T(8,128)(2,1)} %wd_a.1), channel_id=1, source_target_pairs={{0,1},{1,0},{2,3},{3,2},{4,5},{5,4},{6,7},{7,6},{8,9},{9,8},{10,11... | collective-permute-start | bytes 3145736 | tf_op jit(solution)/shard_map/ppermute | solution.py:805
  25.3 21.3 %collective-permute-start.9 = (bf16[256,512]{1,0:T(8,128)(2,1)}, bf16[256,512]{1,0:T(8,128)(2,1)S(1)}, u32[]{:S(2)}, u32[]{:S(2)}) collective-permute-start(bf16[256,512]{1,0:T(8,128)(2,1)} %pad_maximum_fusion.refs_0_), channel_id=1, source_target_pairs={{0,8},{2,10},{4,12},{6,14},{8,16},{10,18},{12,20},{14,22},{16,24},... | collective-permute-start | bytes 786440 | tf_op jit(solution)/shard_map/ppermute | solution.py:824
  47.4 30.6 %collective-permute-start.15 = (bf16[256,512]{1,0:T(8,128)(2,1)}, bf16[256,512]{1,0:T(8,128)(2,1)}, u32[]{:S(2)}, u32[]{:S(2)}) collective-permute-start(bf16[256,512]{1,0:T(8,128)(2,1)} %wo_a.1), channel_id=1, source_target_pairs={{0,1},{1,0},{2,3},{3,2},{4,5},{5,4},{6,7},{7,6},{8,9},{9,8},{10,11... | collective-permute-start | bytes 786440 | tf_op jit(solution)/shard_map/ppermute | solution.py:805
  57.9 29.1 %collective-permute-start.13 = (bf16[256,512]{1,0:T(8,128)(2,1)S(1)}, bf16[256,512]{1,0:T(8,128)(2,1)S(1)}, u32[]{:S(2)}, u32[]{:S(2)}) collective-permute-start(bf16[256,512]{1,0:T(8,128)(2,1)S(1)} %get-tuple-element.115.q_ref.refs_0_), channel_id=1, source_target_pairs={{8,0},{10,2},{12,4},{14,6},{16,8},{18,10},{20,12},{22,14},{24,16},... | collective-permute-start | bytes 786440 | tf_op jit(solution)/shard_map/ppermute | solution.py:824
  59.9 27.1 %collective-permute-start.14 = (bf16[256,512]{1,0:T(8,128)(2,1)S(1)}, bf16[256,512]{1,0:T(8,128)(2,1)S(1)}, u32[]{:S(2)}, u32[]{:S(2)}) collective-permute-start(bf16[256,512]{1,0:T(8,128)(2,1)S(1)} %get-tuple-element.115.q_ref.refs_0_), channel_id=1, source_target_pairs={{16,0},{18,2},{20,4},{22,6},{24,8},{26,10},{28,12},{30,14},{17,1},... | collective-permute-start | bytes 786440 | tf_op jit(solution)/shard_map/ppermute | solution.py:824
  98.1 21.1 %collective-permute-start.23 = (bf16[288,512]{1,0:T(8,128)(2,1)}, bf16[288,512]{1,0:T(8,128)(2,1)}, u32[]{:S(2)}, u32[]{:S(2)}) collective-permute-start(bf16[288,512]{1,0:T(8,128)(2,1)} %collective-permute-done.18.refs_7_), channel_id=1, source_target_pairs={{8,0},{10,2},{12,4},{14,6},{16,8},{18,10},{20,12},{22,14},{24,16},... | collective-permute-start | bytes 884744 | tf_op jit(solution)/shard_map/ppermute | solution.py:814
  107.6 29.4 %collective-permute-start.20 = (bf16[608,512]{1,0:T(8,128)(2,1)S(1)}, bf16[608,512]{1,0:T(8,128)(2,1)S(1)}, u32[]{:S(2)}, u32[]{:S(2)}) collective-permute-start(bf16[608,512]{1,0:T(8,128)(2,1)S(1)} %get-tuple-element.133), channel_id=1, source_target_pairs={{0,2},{2,0},{4,6},{6,4},{8,10},{10,8},{12,14},{14,12},{16,18},{18,... | collective-permute-start | bytes 1867784 | tf_op jit(solution)/shard_map/ppermute | solution.py:754
  109.1 29.1 %collective-permute-start.21 = (bf16[608,512]{1,0:T(8,128)(2,1)S(1)}, bf16[608,512]{1,0:T(8,128)(2,1)S(1)}, u32[]{:S(2)}, u32[]{:S(2)}) collective-permute-start(bf16[608,512]{1,0:T(8,128)(2,1)S(1)} %get-tuple-element.134), channel_id=1, source_target_pairs={{0,4},{2,6},{4,0},{6,2},{8,12},{10,14},{12,8},{14,10},{16,20},{18,... | collective-permute-start | bytes 1867784 | tf_op jit(solution)/shard_map/ppermute | solution.py:754
  110.6 28.5 %collective-permute-start.22 = (bf16[608,512]{1,0:T(8,128)(2,1)S(1)}, bf16[608,512]{1,0:T(8,128)(2,1)S(1)}, u32[]{:S(2)}, u32[]{:S(2)}) collective-permute-start(bf16[608,512]{1,0:T(8,128)(2,1)S(1)} %get-tuple-element.135), channel_id=1, source_target_pairs={{0,6},{2,4},{4,2},{6,0},{8,14},{10,12},{12,10},{14,8},{16,22},{18,... | collective-permute-start | bytes 1867784 | tf_op jit(solution)/shard_map/ppermute | solution.py:754
  147.4 32.1 %collective-permute-start.35 = (bf16[352,512]{1,0:T(8,128)(2,1)}, bf16[352,512]{1,0:T(8,128)(2,1)S(1)}, u32[]{:S(2)}, u32[]{:S(2)}) collective-permute-start(bf16[352,512]{1,0:T(8,128)(2,1)} %get-tuple-element.158), channel_id=1, source_target_pairs={{0,2},{2,0},{4,6},{6,4},{8,10},{10,8},{12,14},{14,12},{16,18},{18,... | collective-permute-start | bytes 1081352 | tf_op jit(solution)/shard_map/ppermute | solution.py:754
  147.8 49.0 %all-to-all-start.1 = ((bf16[16,16,512]{2,1,0:T(8,128)(2,1)}), bf16[16,16,512]{2,1,0:T(8,128)(2,1)}, u32[]{:S(2)}, u32[]{:S(2)}) async-start(bf16[16,16,512]{2,1,0:T(8,128)(2,1)} %bitcast.17), calls=%async_computation.1 | async-start | bytes 524288 | tf_op jit(solution)/shard_map/all_to_all | solution.py:982
  155.4 16.7 %collective-permute-start.33 = (bf16[152,512]{1,0:T(8,128)(2,1)}, bf16[152,512]{1,0:T(8,128)(2,1)S(1)}, u32[]{:S(2)}, u32[]{:S(2)}) collective-permute-start(bf16[152,512]{1,0:T(8,128)(2,1)} %copy-done.74), channel_id=1, source_target_pairs={{0,16},{2,18},{4,20},{6,22},{8,24},{10,26},{12,28},{14,30},{16,0},... | collective-permute-start | bytes 466952 | tf_op jit(solution)/shard_map/ppermute | solution.py:754
  155.6 19.7 %collective-permute-start.34 = (bf16[152,512]{1,0:T(8,128)(2,1)}, bf16[152,512]{1,0:T(8,128)(2,1)S(1)}, u32[]{:S(2)}, u32[]{:S(2)}) collective-permute-start(bf16[152,512]{1,0:T(8,128)(2,1)} %copy-done.73), channel_id=1, source_target_pairs={{0,24},{2,26},{4,28},{6,30},{8,16},{10,18},{12,20},{14,22},{16,8},... | collective-permute-start | bytes 466952 | tf_op jit(solution)/shard_map/ppermute | solution.py:754
  158.3 22.3 %collective-permute-start.36 = (bf16[352,512]{1,0:T(8,128)(2,1)}, bf16[352,512]{1,0:T(8,128)(2,1)S(1)}, u32[]{:S(2)}, u32[]{:S(2)}) collective-permute-start(bf16[352,512]{1,0:T(8,128)(2,1)} %copy-done.72), channel_id=1, source_target_pairs={{0,4},{2,6},{4,0},{6,2},{8,12},{10,14},{12,8},{14,10},{16,20},{18,... | collective-permute-start | bytes 1081352 | tf_op jit(solution)/shard_map/ppermute | solution.py:754
  159.8 22.2 %collective-permute-start.37 = (bf16[352,512]{1,0:T(8,128)(2,1)S(1)}, bf16[352,512]{1,0:T(8,128)(2,1)S(1)}, u32[]{:S(2)}, u32[]{:S(2)}) collective-permute-start(bf16[352,512]{1,0:T(8,128)(2,1)S(1)} %get-tuple-element.160), channel_id=1, source_target_pairs={{0,6},{2,4},{4,2},{6,0},{8,14},{10,12},{12,10},{14,8},{16,22},{18,... | collective-permute-start | bytes 1081352 | tf_op jit(solution)/shard_map/ppermute | solution.py:754
  180.7 17.1 %collective-permute-start.30 = (bf16[128,512]{1,0:T(8,128)(2,1)S(1)}, bf16[128,512]{1,0:T(8,128)(2,1)}, u32[]{:S(2)}, u32[]{:S(2)}) collective-permute-start(bf16[128,512]{1,0:T(8,128)(2,1)S(1)} %get-tuple-element.204), channel_id=1, source_target_pairs={{0,0},{4,1},{2,2},{6,3},{1,4},{5,5},{3,6},{7,7},{8,8},{12,9},{10,1... | collective-permute-start | bytes 393224 | tf_op jit(solution)/shard_map/ppermute | solution.py:991
  193.2 22.3 %collective-permute-start.41 = (bf16[608,512]{1,0:T(8,128)(2,1)S(1)}, bf16[608,512]{1,0:T(8,128)(2,1)S(1)}, u32[]{:S(2)}, u32[]{:S(2)}) collective-permute-start(bf16[608,512]{1,0:T(8,128)(2,1)S(1)} %place.4.refs_0_), channel_id=1, source_target_pairs={{0,2},{2,0},{4,6},{6,4},{8,10},{10,8},{12,14},{14,12},{16,18},{18,... | collective-permute-start | bytes 1867784 | tf_op jit(solution)/shard_map/ppermute | solution.py:754
  194.8 27.8 %collective-permute-start.42 = (bf16[608,512]{1,0:T(8,128)(2,1)S(1)}, bf16[608,512]{1,0:T(8,128)(2,1)S(1)}, u32[]{:S(2)}, u32[]{:S(2)}) collective-permute-start(bf16[608,512]{1,0:T(8,128)(2,1)S(1)} %place.4.refs_0_), channel_id=1, source_target_pairs={{0,4},{2,6},{4,0},{6,2},{8,12},{10,14},{12,8},{14,10},{16,20},{18,... | collective-permute-start | bytes 1867784 | tf_op jit(solution)/shard_map/ppermute | solution.py:754
  196.3 26.3 %collective-permute-start.43 = (bf16[608,512]{1,0:T(8,128)(2,1)S(1)}, bf16[608,512]{1,0:T(8,128)(2,1)S(1)}, u32[]{:S(2)}, u32[]{:S(2)}) collective-permute-start(bf16[608,512]{1,0:T(8,128)(2,1)S(1)} %place.4.refs_0_), channel_id=1, source_target_pairs={{0,6},{2,4},{4,2},{6,0},{8,14},{10,12},{12,10},{14,8},{16,22},{18,... | collective-permute-start | bytes 1867784 | tf_op jit(solution)/shard_map/ppermute | solution.py:754
  208.8 16.4 %collective-permute-start.47 = (bf16[88,512]{1,0:T(8,128)(2,1)S(1)}, bf16[88,512]{1,0:T(8,128)(2,1)S(1)}, u32[]{:S(2)}, u32[]{:S(2)}) collective-permute-start(bf16[88,512]{1,0:T(8,128)(2,1)S(1)} %cut.11.refs_0_), channel_id=1, source_target_pairs={{0,8},{2,10},{4,12},{6,14},{8,0},{10,2},{12,4},{14,6},{16,24},{18,... | collective-permute-start | bytes 270344 | tf_op jit(solution)/shard_map/ppermute | solution.py:754
  (110 other events, 941.1 us)

commit v3 on v2

--- a/solution.py
+++ b/solution.py
@@ -166,7 +166,7 @@
             scratch_shapes=[square, square, square, pltpu.VMEM((rows, width), BF)],
         ),
         out_shape=[flat] * 3 + [jax.ShapeDtypeStruct((rows, width), F32), flat] if own else [flat] * 2,
-        compiler_params=params(pos[0].shape[0] + blocks * rows),
+        compiler_params=pltpu.CompilerParams(vmem_limit_bytes=60 * 1024 * 1024),
         cost_estimate=lasting(2 * blocks + 2),
         name="project",
     )(info, *args)
@@ -250,9 +250,8 @@
             total = jnp.sum(raised, axis=1, keepdims=True)
             probs = raised * (1.0 / total)
             low = probs.astype(BF)
-            rest = (probs - low.astype(F32)).astype(BF)
             attended = dot(low, values[:, lanes])
-            exact = attended + dot(rest, values[:, lanes])
+            weight = jnp.sum(low.astype(F32), axis=1, keepdims=True)
         else:
             top = jnp.full((rows, 1), -1e30, F32)
             for chunk in chunks:
@@ -260,16 +259,14 @@
             total = jnp.zeros((rows, 1), F32)
             for chunk in chunks:
                 total = total + jnp.sum(jnp.exp(scores_of(chunk) - top), axis=1, keepdims=True)
-            attended, exact = jnp.zeros((rows, 64), F32), jnp.zeros((rows, 64), F32)
+            attended, weight = jnp.zeros((rows, 64), F32), jnp.zeros((rows, 1), F32)
             for chunk in chunks:
                 probs = jnp.exp(scores_of(chunk) - top) * (1.0 / total)
                 low = probs.astype(BF)
-                rest = (probs - low.astype(F32)).astype(BF)
                 attended = attended + dot(low, values[chunk, lanes])
-                exact = exact + dot(rest, values[chunk, lanes])
-            exact = exact + attended
+                weight = weight + jnp.sum(low.astype(F32), axis=1, keepdims=True)
         a_ref[:, lanes] = attended.astype(BF)
-        exact_ref[:, lanes] = exact
+        exact_ref[:, lanes] = attended / weight
         logs.append(jnp.broadcast_to(top + jnp.log(total), (rows, 64)))
     wide = jnp.concatenate(logs, axis=1)
     log_ref[...] = wide
@@ -383,7 +380,7 @@
 def feed_forward(info, a, exact, log_stats, hidden, arrived, mine, wo, wu, wd, vec):
     rows, width = hidden.shape
     units = wu[0].shape[1]
-    args = (a, exact, log_stats, hidden, arrived, mine.reshape(1, rows), mine.reshape(rows, 1), *wo, *wu, *wd, *vec)
+    args = (a, exact, log_stats, hidden, arrived, *mine, *wo, *wu, *wd, *vec)
     low = jax.ShapeDtypeStruct((rows, width), BF)
     tall = jax.ShapeDtypeStruct((rows, units), BF)
     outs = [
@@ -442,7 +439,7 @@
 
 
 def grads_kernel(
-    info, a_own, a_other, do_ref, active_own, active_other, df_ref, h1_ref, du_ref, sums_ref, mine, send, *, quarter
+    info, a_own, a_other, do_ref, active_own, active_other, df_ref, h1_ref, du_ref, mine, send, *, quarter
 ):
     width = df_ref.shape[1]
     step = pl.program_id(0)
@@ -457,14 +454,11 @@
     for out, a_ref in ((mine, a_own), (send, a_other)):
         both = dot_tn(a_ref[...], do_ref[...]).astype(BF)
         out[at : at + 64, :] = jnp.where(step % 2 == 0, both[:64], both[64:])
-        out[at + 64 :, :] = jnp.zeros((quarter - at - 64, width), BF)
-
-        @pl.when(step == 0)
-        def _():
-            out[at + 64 : at + 80, :] = sums_ref[...].astype(BF)
-
-
-def ffn_grads(info, a, do, active, df, h1, du, sums, quarter):
+        if quarter > at + 64:
+            out[at + 64 :, :] = jnp.zeros((quarter - at - 64, width), BF)
+
+
+def ffn_grads(info, a, do, active, df, h1, du, quarter):
     rows, width = df.shape
     units = active.shape[1]
     out = jax.ShapeDtypeStruct((4 * quarter, width), BF)
@@ -483,7 +477,6 @@
                 fixed(df.shape),
                 fixed(h1.shape),
                 columns(units // 4, lambda j, core: j),
-                fixed(sums.shape),
             ],
             out_specs=[pl.BlockSpec((quarter, width), lambda j, *_: (j, 0))] * 2,
         ),
@@ -491,30 +484,25 @@
         compiler_params=params(),
         cost_estimate=lasting(10),
         name="ffn_grads",
-    )(info, a, a, do, active, active, df, h1, du, sums)
+    )(info, a, a, do, active, active, df, h1, du)
 
 
 def query_kernel(
-    info, q_ref, kp_ref, k_ref, vp_ref, v_ref, log_ref, da_ref, exact_ref, dz1_ref, wq_a, wq_b,
-    dq_ref, dh_ref, bias, keys, values, wq,
+    info, q_ref, kp_ref, k_ref, vp_ref, v_ref, log_ref, da_ref, exact_ref, dq_ref, bias, keys, values
 ):
     rows, before = q_ref.shape[0], kp_ref.shape[0]
-    width = dq_ref.shape[1]
-    step = pl.program_id(0)
     chunks = chunks_of(keys.shape[0])
     make_bias = functools.partial(query_bias, info, rows, before)
 
-    @pl.when(step == 0)
+    @pl.when(pl.program_id(0) == 0)
     def _():
         if len(chunks) == 1:
             bias[...] = make_bias(chunks[0])
-        lay(info, wq, wq_a, wq_b)
 
     keys[0:before, :] = kp_ref[...]
     keys[before:, :] = k_ref[...]
     values[0:before, :] = vp_ref[...]
     values[before:, :] = v_ref[...]
-    both = []
     for half in range(2):
         lanes = slice(64 * half, 64 * half + 64)
         delta = jnp.sum(da_ref[:, lanes].astype(F32) * exact_ref[:, lanes], axis=1, keepdims=True)
@@ -526,51 +514,39 @@
             dp = dot_nt(da_ref[:, lanes], values[chunk, lanes])
             ds = (probs * (dp - delta)).astype(BF)
             dq = dq + dot(ds, keys[chunk, lanes])
-        both.append((dq * 0.125).astype(BF))
-    pair = jnp.concatenate(both, axis=1)
-    for n in range(width // 128):
-
-        @pl.when(step == n)
-        def _():
-            dq_ref[:, 128 * n : 128 * n + 128] = pair
-
-    @pl.when(step == pl.num_programs(0) - 1)
-    def _():
-        dh_ref[...] = dz1_ref[...] + dot_nt(dq_ref[...], wq[...])
-
-
-def attend_query(info, q, kp, k, vp, v, logs, da, exact, dz1, wq):
-    rows, width = q.shape
+        dq_ref[:, lanes] = (dq * 0.125).astype(BF)
+
+
+def attend_query(info, first, count, q, kp, k, vp, v, logs, da, exact):
+    rows = q.shape[0]
     before = kp.shape[0]
     cols = before + rows
-    outs = [jax.ShapeDtypeStruct((rows, width), BF), jax.ShapeDtypeStruct((rows, width), F32)]
+    some = lambda n: pl.BlockSpec((n, 128), lambda p, *_: (0, p + first))
     return pl.pallas_call(
         query_kernel,
         grid_spec=pltpu.PrefetchScalarGridSpec(
             num_scalar_prefetch=1,
-            grid=(width // 128,),
-            in_specs=[paired(x.shape[0]) for x in (q, kp, k, vp, v, logs)]
-            + [paired(rows), paired(rows), fixed(dz1.shape), fixed(wq[0].shape), fixed(wq[1].shape)],
-            out_specs=[fixed(x.shape) for x in outs],
+            grid=(count,),
+            in_specs=[some(x.shape[0]) for x in (q, kp, k, vp, v, logs)] + [some(rows), some(rows)],
+            out_specs=paired(rows),
             scratch_shapes=[
                 bias_scratch(rows, cols),
                 pltpu.VMEM((cols, 128), BF),
                 pltpu.VMEM((cols, 128), BF),
-                pltpu.VMEM((width, width), BF),
             ],
         ),
-        out_shape=outs,
+        out_shape=jax.ShapeDtypeStruct((rows, 128 * count), BF),
         compiler_params=params(cols),
-        cost_estimate=lasting(10),
+        cost_estimate=lasting(5),
         name="attend_query",
-    )(info, q, kp, k, vp, v, logs, da, exact, dz1, *wq)
+    )(info, q, kp, k, vp, v, logs, da, exact)
 
 
 def last_kernel(info, *refs, reach, quarter, table):
     count = 2 * reach + 1
     q_parts, da_parts = refs[:count], refs[count : 2 * count]
-    k_ref, v_ref, low_ref, dq_ref, dh_ref, wk_a, wk_b, wv_a, wv_b = refs[2 * count : 2 * count + 9]
-    mine, send, dh_out, bias, queries, grads, dk_all, dv_all, wk, wv = refs[2 * count + 9 :]
+    k_ref, v_ref, low_ref, dq_a, dq_b, dz1_ref, sums_ref, wq_a, wq_b, wk_a, wk_b, wv_a, wv_b = refs[2 * count : 2 * count + 13]
+    mine, send, dh_out, bias, queries, grads, dk_all, dv_all, wq, wk, wv = refs[2 * count + 13 :]
     rows, width = low_ref.shape
     cols = queries.shape[0]
     step = pl.program_id(0)
@@ -580,6 +556,7 @@
 
     @pl.when(step == 0)
     def _():
+        lay(info, wq, wq_a, wq_b)
         lay(info, wk, wk_a, wk_b)
         lay(info, wv, wv_a, wv_b)
         if len(chunks) == 1:
@@ -618,9 +595,9 @@
         step_rows = width // 8
         split_halves(info, mine, send, [n * quarter for n in range(4)], dot_tn(low_ref[...], dk))
         split_halves(info, mine, send, [n * quarter + step_rows for n in range(4)], dot_tn(low_ref[...], dv))
-        dq = dq_ref[...]
+        dq = jnp.concatenate([dq_a[...], dq_b[...]], axis=1)
         split_halves(info, mine, send, [n * quarter + 2 * step_rows for n in range(4)], dot_tn(low_ref[...], dq))
-        dh = dh_ref[...] + dot_nt(dk, wk[...]) + dot_nt(dv, wv[...])
+        dh = dz1_ref[...] + dot_nt(dq, wq[...]) + dot_nt(dk, wk[...]) + dot_nt(dv, wv[...])
         dh_out[...] = dh.astype(BF)
         parts = []
         for _ in range(3):
@@ -642,12 +619,13 @@
             send[n * quarter + base : (n + 1) * quarter, :] = jnp.zeros((spare, width), BF)
         total_v = jnp.sum(dv.astype(F32), axis=0, keepdims=True)
         total_q = jnp.sum(dq.astype(F32), axis=0, keepdims=True)
-        total = jnp.where(iota((8, width), 0) == 0, total_v, total_q)
-        mine[base : base + 8, :] = total.astype(BF)
-        send[base : base + 8, :] = total.astype(BF)
-
-
-def last(info, q_parts, da_parts, k, v, low, dq, dh, wk, wv, quarter, table):
+        row = iota(sums_ref.shape, 0)
+        total = jnp.where(row == 6, total_q, jnp.where(row == 11, total_v, sums_ref[...])).astype(BF)
+        mine[base : base + 16, :] = total
+        send[base : base + 16, :] = total
+
+
+def last(info, q_parts, da_parts, k, v, low, dqs, dz1, sums, wq, wk, wv, quarter, table):
     rows, width = k.shape
     count = len(q_parts)
     cols = count * rows
@@ -656,7 +634,7 @@
         jax.ShapeDtypeStruct((4 * quarter, width), BF),
         jax.ShapeDtypeStruct((rows, width), BF),
     ]
-    rest = (low, dq, dh, *wk, *wv)
+    rest = (low, *dqs, dz1, sums, *wq, *wk, *wv)
     return pl.pallas_call(
         functools.partial(last_kernel, reach=count // 2, quarter=quarter, table=table),
         grid_spec=pltpu.PrefetchScalarGridSpec(
@@ -672,6 +650,7 @@
                 pltpu.VMEM((rows, width), BF),
                 pltpu.VMEM((width, width), BF),
                 pltpu.VMEM((width, width), BF),
+                pltpu.VMEM((width, width), BF),
             ],
         ),
         out_shape=outs,
@@ -690,13 +669,17 @@
         outs[k][...] = total.astype(outs[k].dtype)
 
 
+def rows_of(terms):
+    return terms[0][0].shape[0] // (1 + max(block for _, block in terms))
+
+
 def cut(terms, digit, radix, kept):
-    rows, width = terms[0].shape[0] // radix, terms[0].shape[1]
+    rows, width = rows_of(terms) // radix, terms[0][0].shape[1]
     subs = max(n for n in (1, 2, 3, 4) if rows % (8 * n) == 0 and rows // n >= 64 or n == 1)
     specs = [
-        pl.BlockSpec((rows // subs, width), lambda n, d, k=k: ((d[0] ^ k) * subs + n, 0))
+        pl.BlockSpec((rows // subs, width), lambda n, d, k=k, b=b: ((b * radix + (d[0] ^ k)) * subs + n, 0))
         for k in range(radix)
-        for _ in terms
+        for _, b in terms
     ]
     return pl.pallas_call(
         functools.partial(cut_kernel, terms=len(terms), radix=radix),
@@ -710,11 +693,80 @@
         compiler_params=params(),
         cost_estimate=lasting(3),
         name="cut",
-    )(digit.reshape(1), *([*terms] * radix))
-
-
-def place_kernel(digit_ref, *refs, radix, sizes):
-    parts, outs = refs[:radix], refs[radix:]
+    )(digit.reshape(1), *([x for x, _ in terms] * radix))
+
+
+def total_of(refs):
+    total = refs[0][...].astype(F32)
+    for ref in refs[1:]:
+        total = total + ref[...].astype(F32)
+    return total
+
+
+def join_kernel(digit_ref, *refs, ones, twos, radix):
+    done, held, *messages = refs[ones + twos * radix :]
+    rows = done.shape[0]
+    whole = total_of(refs[:ones]).astype(BF)
+    done[...] = whole
+    for k in range(radix):
+        piece = total_of(refs[ones + k * twos : ones + (k + 1) * twos])
+        if k:
+            messages[k - 1][0:rows, :] = whole
+            messages[k - 1][rows:, :] = piece.astype(BF)
+        else:
+            held[...] = piece
+
+
+def join(first, second, digit, radix):
+    (rows, width), part = first[0].shape, rows_of(second) // radix
+    specs = [
+        pl.BlockSpec((part, width), lambda n, d, k=k, b=b: (b * radix + (d[0] ^ k), 0))
+        for k in range(radix)
+        for _, b in second
+    ]
+    outs = [jax.ShapeDtypeStruct((rows, width), BF), jax.ShapeDtypeStruct((part, width), F32)]
+    outs += [jax.ShapeDtypeStruct((rows + part, width), BF)] * (radix - 1)
+    return pl.pallas_call(
+        functools.partial(join_kernel, ones=len(first), twos=len(second), radix=radix),
+        grid_spec=pltpu.PrefetchScalarGridSpec(
+            num_scalar_prefetch=1,
+            grid=(1,),
+            in_specs=[fixed((rows, width))] * len(first) + specs,
+            out_specs=[fixed(x.shape) for x in outs],
+        ),
+        out_shape=outs,
+        compiler_params=params(),
+        cost_estimate=lasting(3),
+        name="join",
+    )(digit.reshape(1), *first, *([x for x, _ in second] * radix))
+
+
+def below_kernel(held_ref, *refs, copies):
+    *parts, out = refs
+    rows = held_ref.shape[0]
+    total = held_ref[...]
+    for part in parts:
+        total = total + part[part.shape[0] - rows :, :].astype(F32)
+    for n in range(copies):
+        out[n * rows : n * rows + rows, :] = total.astype(BF)
+
+
+def add_below(held, messages, copies):
+    out = jax.ShapeDtypeStruct((copies * held.shape[0], held.shape[1]), BF)
+    return pl.pallas_call(
+        functools.partial(below_kernel, copies=copies),
+        grid=(1,),
+        in_specs=[fixed(x.shape) for x in (held, *messages)],
+        out_specs=fixed(out.shape),
+        out_shape=out,
+        compiler_params=params(),
+        cost_estimate=lasting(2),
+        name="add_below",
+    )(held, *messages)
+
+
+def place_kernel(digit_ref, *refs, radix, sizes, counts):
+    parts, outs, vectors = refs[:radix], refs[radix : radix + len(sizes)], refs[radix + len(sizes) :]
     for k in range(radix):
 
         @pl.when(pl.program_id(0) == k)
@@ -724,29 +776,45 @@
                 out[...] = parts[k][at : at + size, :].astype(out.dtype)
                 at += size
 
-
-def place(parts, digit, sizes, dtype, across):
-    radix, (rows, width) = len(parts), parts[0].shape
+            if not counts:
+                return
+
+            @pl.when(digit_ref[0] == k)
+            def _():
+                row = at
+                for out, count in zip(vectors, counts):
+                    whole = jnp.concatenate([parts[k][row + n : row + n + 1, :] for n in range(count)], axis=1)
+                    whole = whole.astype(F32)
+                    half = whole.shape[1] // 2
+                    out[...] = jnp.where(digit_ref[1] == 0, whole[:, :half], whole[:, half:])
+                    row += count
+
+
+def place(parts, digit, sizes, dtype, across=None, core=None, counts=()):
+    radix, width = len(parts), parts[0].shape[1]
     below = lambda k, d: (k ^ d[0], 0)
     beside = lambda k, d: (0, k ^ d[0])
+    outs = [
+        jax.ShapeDtypeStruct((n, width * radix) if i == across else (n * radix, width), dtype)
+        for i, n in enumerate(sizes)
+    ]
+    halves = [jax.ShapeDtypeStruct((1, n * width // 2), F32) for n in counts]
     return pl.pallas_call(
-        functools.partial(place_kernel, radix=radix, sizes=sizes),
+        functools.partial(place_kernel, radix=radix, sizes=sizes, counts=counts),
         grid_spec=pltpu.PrefetchScalarGridSpec(
             num_scalar_prefetch=1,
             grid=(radix,),
-            in_specs=[fixed((rows, width))] * radix,
+            in_specs=[fixed(x.shape) for x in parts],
             out_specs=[
                 pl.BlockSpec((n, width), beside if i == across else below) for i, n in enumerate(sizes)
-            ],
+            ]
+            + [fixed(x.shape) for x in halves],
         ),
-        out_shape=[
-            jax.ShapeDtypeStruct((n, width * radix) if i == across else (n * radix, width), dtype)
-            for i, n in enumerate(sizes)
-        ],
+        out_shape=outs + halves,
         compiler_params=params(),
-        cost_estimate=lasting(3),
+        cost_estimate=lasting(4),
         name="place",
-    )(digit.reshape(1), *parts)
+    )(digit.reshape(1) if core is None else jnp.stack([digit, core]), *parts)
 
 
 def exchange(pieces, here, stride, ranks):
@@ -779,12 +847,20 @@
         return (self.here // stride) % radix
 
     def cut(self, terms, level):
-        if level == len(self.stages):
-            return cut(terms, self.here * 0, 1, BF)
-        return cut(terms, self.digit(level), self.stages[level][1], F32)
+        return cut([(x, 0) for x in terms], self.digit(level), self.stages[level][1], F32)
+
+    def add(self, terms):
+        return cut([(x, 0) for x in terms], self.here * 0, 1, BF)[0]
 
     def scatter(self, pieces, level):
         return [pieces[0]] + exchange(pieces[1:], self.here, self.stages[level][0], self.ranks)
+
+    def trade(self, blocks, level):
+        stride, radix = self.stages[level]
+        groups = [
+            [i + n * stride for n in range(radix)] for i in range(self.ranks) if (i // stride) % radix == 0
+        ]
+        return lax.all_to_all(blocks, "ctx", split_axis=0, concat_axis=0, axis_index_groups=groups, tiled=True)
 
     def gather(self, held, level):
         stride, radix = self.stages[level]
@@ -900,6 +976,7 @@
 
     mine = order.reshape(ranks, ranks, slot)
     mine = lax.dynamic_slice_in_dim(mine, 4 * chip + 2 * core, 2, axis=1).reshape(rows) - base
+    mine = (mine.reshape(1, rows), mine.reshape(rows, 1))
     dealt = cotangent[:, 0].reshape(2, chips, 2, 2 * slot, width)
     keep = jnp.where(core == 0, dealt[:, :, 0], dealt[:, :, 1])
     give = jnp.where(core == 0, dealt[:, :, 1], dealt[:, :, 0])
@@ -911,7 +988,7 @@
     far = send_window(own, reach, chips, 1)
     own = after(arrived, own)
     k, v, q, hidden, low = project(info, [own], 0, True, *fixed_args)
-    far[1:] = after(k, far[1:])
+    mine, far[1:] = lax.optimization_barrier((mine, after(k, far[1:])))
 
     earlier = both_cores(far, core, 1)[::-1]
     before = len(earlier) * rows
@@ -927,64 +1004,45 @@
     half = width // 2
     units = 2 * b_up.shape[0]
     sizes = [units // 8, half, width // 8]
-    quarter = padded(sum(sizes) + 16, ranks)
-    sizes.append(quarter - sum(sizes))
+    quarter = padded(sum(sizes), ranks)
     sizes_last = [width // 8, width // 8, width // 8, longest // 8]
-    quarter_last = padded(sum(sizes_last) + 8, ranks)
-    sizes_last.append(quarter_last - sum(sizes_last))
+    quarter_last = padded(sum(sizes_last) + 16, ranks)
     one = Reduction(here, ranks, sizes, 1)
     two = Reduction(here, ranks, sizes_last, None)
     levels = len(one.stages)
 
-    keep, give = ffn_grads(info, att, do, active, df, h1, du, sums, quarter)
+    pairs = width // 256
+    query_args = (q, kp, k, vp, v, logs, da_msg)
+    dq_first = attend_query(info, 0, pairs, *query_args, exact)
+    do = after(dq_first, do)
+    keep, give = ffn_grads(info, att, do, active, df, h1, du, quarter)
     give = after(far_da[1], give)
     for _ in range(reach - 1):
         far_da.append(next_chip(far_da[-1], chips, -1))
     pieces = one.cut([keep, swap_core(give)], 0)
-    exact = after(pieces, exact)
     terms = one.scatter(pieces, 0)
-    dq, dh = attend_query(info, q, kp, k, vp, v, logs, da_msg, exact, dz1, wq)
-    far_da[1:], far_q[1:] = after(dq, (far_da[1:], far_q[1:]))
+    dq_second = attend_query(info, pairs, pairs, *query_args, after(pieces, exact))
+    far_da[1:], far_q[1:] = after(dq_second, (far_da[1:], far_q[1:]))
     later_da = [da_msg] + both_cores(far_da, core, -1)
     later_q = [q] + both_cores(far_q, core, -1)
-    keep, give, dh0_low = last(info, later_q, later_da, k, v, low, dq, dh, wk, wv, quarter_last, longest)
-
-    keep, give, dh0_low = after(terms[1:], (keep, give, dh0_low))
+    dqs = (dq_first, dq_second)
+    keep, give, dh0_low = last(
+        info, later_q, later_da, k, v, low, dqs, dz1, sums, wq, wk, wv, quarter_last, longest
+    )
+
+    keep, give = after(terms[1:], (keep, give))
     terms_last = [keep, swap_core(give)]
-    for level in range(levels):
+    end = levels - 1
+    for level in range(end):
         pieces = one.cut(terms, level + 1)
-        if level + 1 < levels:
-            terms = one.scatter(pieces, level + 1)
+        terms = one.scatter(pieces, level + 1)
         pieces_last = two.cut(after(pieces, terms_last), level)
         terms_last = two.scatter(pieces_last, level)
-        if level == 0:
-            leaving, dh0_low = after(pieces_last, (leaving, dh0_low))
-    held = pieces[0]
-    parts = one.gather(held, levels - 1)
-    for level in reversed(range(levels)):
-        if level == levels - 1:
-            held = one.place(after(pieces_last, parts), level)
-            (held_last,) = two.cut(after(held, terms_last), levels)
-        else:
-            held = one.place(parts, level)
-        parts_last = two.gather(held_last, level)
-        if level:
-            parts = one.gather(held, level - 1)
-            parts_last = after(parts[1:], parts_last)
-        held_last = two.place(parts_last, level)
-    g_down, g_up, g_out, early = held
-    g_key, g_value, g_query, g_pos, late = held_last
-    shard = lambda x: lax.dynamic_slice_in_dim(x, core * half, half)
-    gb_down, gg1, gs1, gg2, gs2, gb_out = (shard(early[n]) for n in range(6))
-    gb_up = lax.dynamic_slice_in_dim(early[7:11].reshape(-1), core * (units // 2), units // 2)
-    gb_value, gb_query = shard(late[0]), shard(late[1])
-
-    landed = lax.all_to_all(leaving, "ctx", split_axis=0, concat_axis=0, tiled=True)
-    landed = landed.reshape(chips, 2, 2, 2 * slot, width)
-    keep = jnp.where(core == 0, landed[:, 0], landed[:, 1])
-    give = jnp.where(core == 0, landed[:, 1], landed[:, 0])
-    sides = by_core(core, keep, swap_core(give))
-    output = jnp.transpose(sides, (2, 1, 0, 3, 4)).reshape(2, 1, block, width)
+    terms_last = [(x, 0) for x in terms_last]
+    stride, radix = one.stages[end]
+    held, held_last, *messages = join(terms, terms_last, one.digit(end), radix)
+    got = exchange(messages, here, stride, ranks)
+    dh0_low = after(held, dh0_low)
 
     back_same = jnp.where(micro == 0, dh0_low[:block], dh0_low[block:])
     back_cross = jnp.where(micro == 0, dh0_low[block:], dh0_low[:block])
@@ -993,6 +1051,30 @@
     grad_tokens = jnp.where(
         even, jnp.stack([home_same, home_cross]), jnp.stack([home_cross, home_same])
     )[:, None]
+
+    got = after((home_same, home_cross), got)
+    held = place([held] + got, one.digit(end), [held.shape[0]], BF, None)[0]
+    held_last = two.trade(add_below(held_last, after(held, got), radix), end)
+    for level in reversed(range(1, end)):
+        held = one.place(one.gather(held, level), level)
+        held_last = two.place(two.gather(held_last, level), level)
+    parts = one.gather(held, 0)
+    held_last = after(parts[1:], held_last)
+    parts_last = two.gather(held_last, 0)
+    held = one.place(parts, 0)
+    leaving = after(parts[1:], leaving)
+    landed = lax.all_to_all(leaving, "ctx", split_axis=0, concat_axis=0, tiled=True)
+
+    landed = landed.reshape(chips, 2, 2, 2 * slot, width)
+    keep = jnp.where(core == 0, landed[:, 0], landed[:, 1])
+    give = jnp.where(core == 0, landed[:, 1], landed[:, 0])
+    sides = by_core(core, keep, swap_core(give))
+    output = jnp.transpose(sides, (2, 1, 0, 3, 4)).reshape(2, 1, block, width)
+    counts = [1] * 7 + [units // width, 1]
+    results = place(parts_last, two.digit(0), sizes_last, F32, None, core, counts)
+    g_down, g_up, g_out = held
+    g_key, g_value, g_query, g_pos = results[:4]
+    gb_down, gg1, gs1, gg2, gs2, gb_out, gb_query, gb_up, gb_value = (x.reshape(-1) for x in results[4:])
 
     return (
         output,

time: 247 us -> 237 us (0.960)
  local copies, waits for them, and re-layouts: 34 us -> 16.6 us
  waiting for transfers between devices: 66.7 us -> 82.4 us
  starting transfers between devices: 67.5 us -> 58 us
  other arithmetic: 13.5 us -> 9.46 us
  Pallas kernels: 62.2 us -> 66.1 us
    ppermute x24 -> x18, starting transfers between devices: 30 us -> 19.6 us  [exchange(): lax.ppermute(piece, 'ctx', [(i, i ^ (k + 1) * stride) for i in range(rank...]
    ppermute x24 -> x18, waiting for transfers between devices: 46 us -> 56.2 us  [exchange(): lax.ppermute(piece, 'ctx', [(i, i ^ (k + 1) * stride) for i in range(rank...]
    unnamed x161 -> x127, local copies, waits for them, and re-layouts: 22.8 us -> 13.6 us
    dynamic_slice x9 -> x0, local copies, waits for them, and re-layouts: 5.1 us -> none  [the longest x8 4.5 us: shards(): shard = lambda x: lax.dynamic_slice_in_dim(x, core * half, half)]
    pallas_call x2, Pallas kernels: 6.67 us -> 11.4 us  [project(): pl.pallas_call(functools.partial(project_kernel, blocks=blocks, offset=of...]
    ppermute x1, waiting for transfers between devices: 0.01 us -> 4.51 us  [shards(): home_cross = lax.ppermute(back_cross, BOTH, [(b, a) for a, b in crossing])]
    all_to_all x0 -> x1, starting transfers between devices: none -> 4.19 us  [trade(): lax.all_to_all(blocks, 'ctx', split_axis=0, concat_axis=0, axis_index_gro...]
    ppermute x2, waiting for transfers between devices: 4.12 us -> 0.6 us  [next_chip(): lax.ppermute(block, 'ctx', pairs if step > 0 else [(b, a) for a, b in pai...]
  transfers between devices with their start and end apart: 55 -> 50, of which waited for: 20 -> 25; matrix products, arithmetic and copies ran while one was open for 9% -> 5% of each run, Pallas kernels for 24% -> 28%
where the time goes in v3:
time: 237 us; the launch traced here: 234 us
  waiting for transfers between devices  82.4 us (35%)
  Pallas kernels  66.1 us (28%)
  starting transfers between devices  58 us (24%)
  local copies, waits for them, and re-layouts  16.6 us (7%)
  other arithmetic  9.46 us (4%)
    ppermute x18, waiting for transfers between devices, exchange(): lax.ppermute(piece, 'ctx', [(i, i ^ (k + 1) * stride) for i in range(rank...  56.2 us
    ppermute x18, starting transfers between devices, exchange(): lax.ppermute(piece, 'ctx', [(i, i ^ (k + 1) * stride) for i in range(rank...  19.6 us
    unnamed x127, local copies, waits for them, and re-layouts  13.6 us
    pallas_call x1, Pallas kernels, last(): pl.pallas_call(functools.partial(last_kernel, reach=count // 2, quarter=q...  13.5 us
    pallas_call x2, Pallas kernels, project(): pl.pallas_call(functools.partial(project_kernel, blocks=blocks, offset=of...  11.4 us
    ppermute x4, waiting for transfers between devices, send_window(): far.append(lax.ppermute(own, 'ctx', pairs))  11.2 us
    pallas_call x1, Pallas kernels, attend_forward(): pl.pallas_call(forward_kernel, grid_spec=pltpu.PrefetchScalarGridSpec(num...  9.03 us
    pallas_call x1, Pallas kernels, feed_forward(): pl.pallas_call(ffn_kernel, grid_spec=pltpu.PrefetchScalarGridSpec(num_sca...  8.71 us
  transfers between devices with their start and end apart: 50, of which 25 were waited for; matrix products, arithmetic and copies ran while one was open for 5% of the time, Pallas kernels for 28%

profile of v3, /device:TPU:16, one launch (start us, length us, event | category | flops | bytes accessed | tf_op | source)
XLA Modules:
  0.0 234.4 jit_solution(8667184460463863439)
XLA Ops:
  13.2 6.8 %all-to-all-start = ((bf16[16,16,512]{2,1,0:T(8,128)(2,1)}), bf16[16,16,512]{2,1,0:T(8,128)(2,1)S(1)}, u32[]{:S(2)}, u32[]{:S(2)}) async-start(bf16[16,16,512]{2,1,0:T(8,128)(2,1)} %bitcast.13), calls=%async_computation | async-start | bytes 524288 | tf_op jit(solution)/shard_map/all_to_all | solution.py:985
  22.9 3.4 %collective-permute-start.9 = (bf16[256,512]{1,0:T(8,128)(2,1)S(1)}, bf16[256,512]{1,0:T(8,128)(2,1)S(1)}, u32[]{:S(2)}, u32[]{:S(2)}) collective-permute-start(bf16[256,512]{1,0:T(8,128)(2,1)S(1)} %pad_maximum_fusion.refs_0_), channel_id=1, source_target_pairs={{0,8},{2,10},{4,12},{6,14},{8,16},{10,18},{12,20},{14,22},{16,24},... | collective-permute-start | bytes 786440 | tf_op jit(solution)/shard_map/ppermute | solution.py:900
  28.7 4.2 %project.2 = (bf16[256,512]{1,0:T(8,128)(2,1)}, bf16[256,512]{1,0:T(8,128)(2,1)}, bf16[256,512]{1,0:T(8,128)(2,1)}, f32[256,512]{1,0:T(8,128)}, bf16[256,512]{1,0:T(8,128)(2,1)}) custom-call(s32[11]{0:T(128)} %pad_add_fusion.1.info, bf16[256,512]{1,0:T(8,128)(2,1)} %copy-done.58, bf16[512,512]{1,0:T(8,128)(2,1)} %refs_4_.1, bf16[512,512]{1,0:T(8,128)(2,1)} %copy-done.55, ...), custom_call_target="tpu_custom_call" | custom-call | flops 4 | bytes 4 | tf_op jit(solution)/shard_map/project/pallas_call | solution.py:159
  33.6 10.5 %collective-permute-done.9.refs_2_ = bf16[256,512]{1,0:T(8,128)(2,1)S(1)} collective-permute-done((bf16[256,512]{1,0:T(8,128)(2,1)S(1)}, bf16[256,512]{1,0:T(8,128)(2,1)S(1)}, u32[]{:S(2)}, u32[]{:S(2)}) %collective-permute-start.9) | collective-permute-done | bytes 262176 | tf_op jit(solution)/shard_map/ppermute | solution.py:900
  47.3 7.2 %project.3 = (bf16[1024,512]{1,0:T(8,128)(2,1)}, bf16[1024,512]{1,0:T(8,128)(2,1)}) custom-call(s32[11]{0:T(128)} %pad_add_fusion.1.info, bf16[256,512]{1,0:T(8,128)(2,1)} %copy-done.56, bf16[256,512]{1,0:T(8,128)(2,1)} %copy-done.59, bf16[256,512]{1,0:T(8,128)(2,1)} %copy-done.57, bf16[256,512]{1,0:T(8,128)(2,1)} %copy-done.60, bf16[512,512]{1,0:T(8,128)(2,1)} %refs_4_.1, ...), custom_call_target="tpu_custom_call" | custom-call | flops 10 | bytes 10 | tf_op jit(solution)/shard_map/project/pallas_call | solution.py:159
  60.5 9.0 %attend_forward.1 = (bf16[256,512]{1,0:T(8,128)(2,1)S(1)}, f32[256,512]{1,0:T(8,128)S(1)}, f32[256,512]{1,0:T(8,128)S(1)}, bf16[16,512]{1,0:T(8,128)(2,1)S(1)}) custom-call(s32[11]{0:T(128)S(1)} %copy-done.53, bf16[256,512]{1,0:T(8,128)(2,1)S(1)} %copy-done.12, bf16[1024,512]{1,0:T(8,128)(2,1)S(1)} %copy-done.6, bf16[256,512]{1,0:T(8,128)(2,1)S(1)} %copy-done.17, ...), custom_call_target="tpu_custom_call" | custom-call | flops 12 | bytes 12 | tf_op jit(solution)/shard_map/attend_forward/pallas_call | solution.py:281
  72.3 8.7 %feed_forward.1 = (bf16[256,512]{1,0:T(8,128)(2,1)}, bf16[288,512]{1,0:T(8,128)(2,1)S(1)}, f32[256,512]{1,0:T(8,128)S(1)}, bf16[256,2048]{1,0:T(8,128)(2,1)S(1)}...) custom-call(s32[11]{0:T(128)S(1)} %copy-done.53, ...), custom_call_target="tpu_custom_call" | custom-call | flops 10 | bytes 10 | tf_op jit(solution)/shard_map/feed_forward/pallas_call | solution.py:397
  83.2 4.1 %attend_query.2.refs_13_ = bf16[256,256]{1,0:T(8,128)(2,1)S(1)} custom-call(s32[11]{0:T(128)S(1)} %copy-done.53, bf16[256,512]{1,0:T(8,128)(2,1)S(1)} %copy-done.12, bf16[1024,512]{1,0:T(8,128)(2,1)S(1)} %copy-done.7, bf16[256,512]{1,0:T(8,128)(2,1)S(1)} %copy-done.17, bf16[1024,512]{1,0:T(8,128)(2,1)S(1)} %copy-done.10, bf16[256,512]{1,0:T(8,128)(2,1)S(1)} %copy-done.18, ...), custom_call_target="tpu_custom_call" | custom-call | flops 5 | bytes 5 | tf_op jit(solution)/shard_map/attend_query/pallas_call | solution.py:525
  87.4 4.2 %ffn_grads.1 = (bf16[2304,512]{1,0:T(8,128)(2,1)S(1)}, bf16[2304,512]{1,0:T(8,128)(2,1)}) custom-call(s32[11]{0:T(128)S(1)} %copy-done.53, bf16[256,512]{1,0:T(8,128)(2,1)S(1)} %get-tuple-element.117.a_ref.a_own.a_other, bf16[256,512]{1,0:T(8,128)(2,1)S(1)} %get-tuple-element.117.a_ref.a_own.a_other, bf16[256,512]{1,0:T(8,128)(2,1)S(1)} %get-tuple-element.130.do_ref, ...), custom_call_target="tpu_custom_call" | custom-call | flops 10 | bytes 10 | tf_op jit(solution)/shard_map/ffn_grads/pallas_call | solution.py:466
  103.7 4.1 %attend_query.3.refs_14_ = bf16[256,256]{1,0:T(8,128)(2,1)S(1)} custom-call(s32[11]{0:T(128)S(1)} %copy-done.53, bf16[256,512]{1,0:T(8,128)(2,1)S(1)} %copy-done.12, bf16[1024,512]{1,0:T(8,128)(2,1)S(1)} %copy-done.8, bf16[256,512]{1,0:T(8,128)(2,1)S(1)} %copy-done.17, bf16[1024,512]{1,0:T(8,128)(2,1)S(1)} %copy-done.11, bf16[256,512]{1,0:T(8,128)(2,1)S(1)} %copy-done.19, ...), custom_call_target="tpu_custom_call" | custom-call | flops 5 | bytes 5 | tf_op jit(solution)/shard_map/attend_query/pallas_call | solution.py:525
  111.8 13.5 %last.1 = (bf16[1408,512]{1,0:T(8,128)(2,1)S(1)}, bf16[1408,512]{1,0:T(8,128)(2,1)}, bf16[256,512]{1,0:T(8,128)(2,1)S(1)}) custom-call(s32[11]{0:T(128)S(1)} %copy-done.53, bf16[256,512]{1,0:T(8,128)(2,1)S(1)} %copy-done.12, bf16[256,512]{1,0:T(8,128)(2,1)S(1)} %collective-permute-done.27.refs_1_, bf16[256,512]{1,0:T(8,128)(2,1)S(1)} %copy-done.34, ...), custom_call_target="tpu_custom_call" | custom-call | flops 15 | bytes 15 | tf_op jit(solution)/shard_map/last/pallas_call | solution.py:638
  140.7 4.8 %collective-permute-done.23.refs_1_ = bf16[144,512]{1,0:T(8,128)(2,1)S(1)} collective-permute-done((bf16[144,512]{1,0:T(8,128)(2,1)S(1)}, bf16[144,512]{1,0:T(8,128)(2,1)S(1)}, u32[]{:S(2)}, u32[]{:S(2)}) %collective-permute-start.23) | collective-permute-done | bytes 147488 | tf_op jit(solution)/shard_map/ppermute | solution.py:822
  145.5 4.5 %collective-permute-done.24.refs_2_ = bf16[144,512]{1,0:T(8,128)(2,1)S(1)} collective-permute-done((bf16[144,512]{1,0:T(8,128)(2,1)S(1)}, bf16[144,512]{1,0:T(8,128)(2,1)S(1)}, u32[]{:S(2)}, u32[]{:S(2)}) %collective-permute-start.24) | collective-permute-done | bytes 147488 | tf_op jit(solution)/shard_map/ppermute | solution.py:822
  150.0 5.0 %collective-permute-done.25.refs_3_ = bf16[144,512]{1,0:T(8,128)(2,1)S(1)} collective-permute-done((bf16[144,512]{1,0:T(8,128)(2,1)S(1)}, bf16[144,512]{1,0:T(8,128)(2,1)S(1)}, u32[]{:S(2)}, u32[]{:S(2)}) %collective-permute-start.25) | collective-permute-done | bytes 147488 | tf_op jit(solution)/shard_map/ppermute | solution.py:822
  160.1 4.5 %collective-permute-done.36 = bf16[128,512]{1,0:T(8,128)(2,1)S(1)} collective-permute-done((bf16[128,512]{1,0:T(8,128)(2,1)S(1)}, bf16[128,512]{1,0:T(8,128)(2,1)S(1)}, u32[]{:S(2)}, u32[]{:S(2)}) %collective-permute-start.36) | collective-permute-done | bytes 131104 | tf_op jit(solution)/shard_map/ppermute | solution.py:1050
  165.7 8.1 %collective-permute-done.38.refs_2_.refs_1_ = bf16[232,512]{1,0:T(8,128)(2,1)S(1)} collective-permute-done((bf16[232,512]{1,0:T(8,128)(2,1)S(1)}, bf16[232,512]{1,0:T(8,128)(2,1)S(1)}, u32[]{:S(2)}, u32[]{:S(2)}) %collective-permute-start.38) | collective-permute-done | bytes 237600 | tf_op jit(solution)/shard_map/ppermute | solution.py:822
  173.8 5.4 %collective-permute-done.39.refs_3_.refs_2_ = bf16[232,512]{1,0:T(8,128)(2,1)S(1)} collective-permute-done((bf16[232,512]{1,0:T(8,128)(2,1)S(1)}, bf16[232,512]{1,0:T(8,128)(2,1)S(1)}, u32[]{:S(2)}, u32[]{:S(2)}) %collective-permute-start.39) | collective-permute-done | bytes 237600 | tf_op jit(solution)/shard_map/ppermute | solution.py:822
  183.7 4.2 %all-to-all-start.2 = ((bf16[4,88,512]{2,1,0:T(8,128)(2,1)}), bf16[4,88,512]{2,1,0:T(8,128)(2,1)S(1)}, u32[]{:S(2)}, u32[]{:S(2)}) async-start(bf16[4,88,512]{2,1,0:T(8,128)(2,1)} %bitcast.26), calls=%async_computation.2 | async-start | bytes 720896 | tf_op jit(solution)/shard_map/all_to_all | solution.py:863
  187.9 7.8 %collective-permute-done.40.refs_1_ = bf16[576,512]{1,0:T(8,128)(2,1)S(1)} collective-permute-done((bf16[576,512]{1,0:T(8,128)(2,1)S(1)}, bf16[576,512]{1,0:T(8,128)(2,1)S(1)}, u32[]{:S(2)}, u32[]{:S(2)}) %collective-permute-start.40) | collective-permute-done | bytes 589856 | tf_op jit(solution)/shard_map/ppermute | solution.py:822
  195.7 10.6 %collective-permute-done.41.refs_2_ = bf16[576,512]{1,0:T(8,128)(2,1)S(1)} collective-permute-done((bf16[576,512]{1,0:T(8,128)(2,1)S(1)}, bf16[576,512]{1,0:T(8,128)(2,1)S(1)}, u32[]{:S(2)}, u32[]{:S(2)}) %collective-permute-start.41) | collective-permute-done | bytes 589856 | tf_op jit(solution)/shard_map/ppermute | solution.py:822
  206.2 5.6 %all-to-all-start.1 = ((bf16[16,16,512]{2,1,0:T(8,128)(2,1)}), bf16[16,16,512]{2,1,0:T(8,128)(2,1)}, u32[]{:S(2)}, u32[]{:S(2)}) async-start(bf16[16,16,512]{2,1,0:T(8,128)(2,1)} %bitcast.17), calls=%async_computation.1 | async-start | bytes 524288 | tf_op jit(solution)/shard_map/all_to_all | solution.py:1066
  215.3 3.4 %all-to-all-done.1 = bf16[16,16,512]{2,1,0:T(8,128)(2,1)} async-done(((bf16[16,16,512]{2,1,0:T(8,128)(2,1)}), bf16[16,16,512]{2,1,0:T(8,128)(2,1)}, u32[]{:S(2)}, u32[]{:S(2)}) %all-to-all-start.1) | async-done | bytes 262176 | tf_op jit(solution)/shard_map/all_to_all | solution.py:1066
  224.6 3.7 %collective-permute-done.45.refs_2_ = bf16[352,512]{1,0:T(8,128)(2,1)S(1)} collective-permute-done((bf16[352,512]{1,0:T(8,128)(2,1)S(1)}, bf16[352,512]{1,0:T(8,128)(2,1)S(1)}, u32[]{:S(2)}, u32[]{:S(2)}) %collective-permute-start.45) | collective-permute-done | bytes 360480 | tf_op jit(solution)/shard_map/ppermute | solution.py:822
  230.0 3.6 %place.4 = (f32[256,512]{1,0:T(8,128)}, f32[256,512]{1,0:T(8,128)}, f32[256,512]{1,0:T(8,128)}, f32[512,512]{1,0:T(8,128)}, f32[1,256]{1,0:T(1,128)}, /*index=5*...) custom-call(s32[2]{0:T(128)S(1)} %pad_add_fusion.2.digit_ref, ...), custom_call_target="tpu_custom_call" | custom-call | flops 4 | bytes 4 | tf_op jit(solution)/shard_map/place/pallas_call | solution.py:802
  (253 shorter events, 85.6 us)
Async XLA Ops:
  1.8 18.2 %collective-permute-start.2 = (bf16[128,512]{1,0:T(8,128)(2,1)S(1)}, bf16[128,512]{1,0:T(8,128)(2,1)S(1)}, u32[]{:S(2)}, u32[]{:S(2)}) collective-permute-start(bf16[128,512]{1,0:T(8,128)(2,1)S(1)} %get-tuple-element.210), channel_id=1, source_target_pairs={{0,0},{1,4},{2,2},{3,6},{4,1},{5,5},{6,3},{7,7},{8,8},{9,12},{10,1... | collective-permute-start | bytes 393224 | tf_op jit(solution)/shard_map/ppermute | solution.py:957
  2.5 17.6 %collective-permute-start.3 = (bf16[128,512]{1,0:T(8,128)(2,1)S(1)}, bf16[128,512]{1,0:T(8,128)(2,1)S(1)}, u32[]{:S(2)}, u32[]{:S(2)}) collective-permute-start(bf16[128,512]{1,0:T(8,128)(2,1)S(1)} %get-tuple-element.211), channel_id=1, source_target_pairs={{0,2},{1,6},{2,0},{3,4},{4,3},{5,7},{6,1},{7,5},{8,10},{9,14},{10,... | collective-permute-start | bytes 393224 | tf_op jit(solution)/shard_map/ppermute | solution.py:958
  13.2 14.6 %all-to-all-start = ((bf16[16,16,512]{2,1,0:T(8,128)(2,1)}), bf16[16,16,512]{2,1,0:T(8,128)(2,1)S(1)}, u32[]{:S(2)}, u32[]{:S(2)}) async-start(bf16[16,16,512]{2,1,0:T(8,128)(2,1)} %bitcast.13), calls=%async_computation | async-start | bytes 524288 | tf_op jit(solution)/shard_map/all_to_all | solution.py:985
  20.8 49.5 %collective-permute-start.16 = (bf16[256,2048]{1,0:T(8,128)(2,1)}, bf16[256,2048]{1,0:T(8,128)(2,1)}, u32[]{:S(2)}, u32[]{:S(2)}) collective-permute-start(bf16[256,2048]{1,0:T(8,128)(2,1)} %wu_a.1), channel_id=1, source_target_pairs={{0,1},{1,0},{2,3},{3,2},{4,5},{5,4},{6,7},{7,6},{8,9},{9,8},{10,11... | collective-permute-start | bytes 3145736 | tf_op jit(solution)/shard_map/ppermute | solution.py:881
  21.3 49.1 %collective-permute-start.17 = (bf16[1024,512]{1,0:T(8,128)(2,1)}, bf16[1024,512]{1,0:T(8,128)(2,1)}, u32[]{:S(2)}, u32[]{:S(2)}) collective-permute-start(bf16[1024,512]{1,0:T(8,128)(2,1)} %wd_a.1), channel_id=1, source_target_pairs={{0,1},{1,0},{2,3},{3,2},{4,5},{5,4},{6,7},{7,6},{8,9},{9,8},{10,11... | collective-permute-start | bytes 3145736 | tf_op jit(solution)/shard_map/ppermute | solution.py:881
  22.9 21.2 %collective-permute-start.9 = (bf16[256,512]{1,0:T(8,128)(2,1)S(1)}, bf16[256,512]{1,0:T(8,128)(2,1)S(1)}, u32[]{:S(2)}, u32[]{:S(2)}) collective-permute-start(bf16[256,512]{1,0:T(8,128)(2,1)S(1)} %pad_maximum_fusion.refs_0_), channel_id=1, source_target_pairs={{0,8},{2,10},{4,12},{6,14},{8,16},{10,18},{12,20},{14,22},{16,24},... | collective-permute-start | bytes 786440 | tf_op jit(solution)/shard_map/ppermute | solution.py:900
  44.9 24.7 %collective-permute-start.15 = (bf16[256,512]{1,0:T(8,128)(2,1)S(1)}, bf16[256,512]{1,0:T(8,128)(2,1)S(1)}, u32[]{:S(2)}, u32[]{:S(2)}) collective-permute-start(bf16[256,512]{1,0:T(8,128)(2,1)S(1)} %copy-done.44), channel_id=1, source_target_pairs={{0,1},{1,0},{2,3},{3,2},{4,5},{5,4},{6,7},{7,6},{8,9},{9,8},{10,11... | collective-permute-start | bytes 786440 | tf_op jit(solution)/shard_map/ppermute | solution.py:881
  54.5 26.5 %collective-permute-start.13 = (bf16[256,512]{1,0:T(8,128)(2,1)S(1)}, bf16[256,512]{1,0:T(8,128)(2,1)S(1)}, u32[]{:S(2)}, u32[]{:S(2)}) collective-permute-start(bf16[256,512]{1,0:T(8,128)(2,1)S(1)} %copy-done.12), channel_id=1, source_target_pairs={{8,0},{10,2},{12,4},{14,6},{16,8},{18,10},{20,12},{22,14},{24,16},... | collective-permute-start | bytes 786440 | tf_op jit(solution)/shard_map/ppermute | solution.py:900
  56.6 24.5 %collective-permute-start.14 = (bf16[256,512]{1,0:T(8,128)(2,1)S(1)}, bf16[256,512]{1,0:T(8,128)(2,1)S(1)}, u32[]{:S(2)}, u32[]{:S(2)}) collective-permute-start(bf16[256,512]{1,0:T(8,128)(2,1)S(1)} %copy-done.12), channel_id=1, source_target_pairs={{16,0},{18,2},{20,4},{22,6},{24,8},{26,10},{28,12},{30,14},{17,1},... | collective-permute-start | bytes 786440 | tf_op jit(solution)/shard_map/ppermute | solution.py:900
  92.1 15.8 %collective-permute-start.26 = (bf16[288,512]{1,0:T(8,128)(2,1)}, bf16[288,512]{1,0:T(8,128)(2,1)}, u32[]{:S(2)}, u32[]{:S(2)}) collective-permute-start(bf16[288,512]{1,0:T(8,128)(2,1)} %collective-permute-done.18.refs_7_), channel_id=1, source_target_pairs={{8,0},{10,2},{12,4},{14,6},{16,8},{18,10},{20,12},{22,14},{24,16},... | collective-permute-start | bytes 884744 | tf_op jit(solution)/shard_map/ppermute | solution.py:890
  100.1 26.0 %collective-permute-start.20 = (bf16[576,512]{1,0:T(8,128)(2,1)S(1)}, bf16[576,512]{1,0:T(8,128)(2,1)S(1)}, u32[]{:S(2)}, u32[]{:S(2)}) collective-permute-start(bf16[576,512]{1,0:T(8,128)(2,1)S(1)} %get-tuple-element.139), channel_id=1, source_target_pairs={{0,2},{2,0},{4,6},{6,4},{8,10},{10,8},{12,14},{14,12},{16,18},{18,... | collective-permute-start | bytes 1769480 | tf_op jit(solution)/shard_map/ppermute | solution.py:822
  101.6 27.7 %collective-permute-start.21 = (bf16[576,512]{1,0:T(8,128)(2,1)S(1)}, bf16[576,512]{1,0:T(8,128)(2,1)S(1)}, u32[]{:S(2)}, u32[]{:S(2)}) collective-permute-start(bf16[576,512]{1,0:T(8,128)(2,1)S(1)} %get-tuple-element.140), channel_id=1, source_target_pairs={{0,4},{2,6},{4,0},{6,2},{8,12},{10,14},{12,8},{14,10},{16,20},{18,... | collective-permute-start | bytes 1769480 | tf_op jit(solution)/shard_map/ppermute | solution.py:822
  103.1 27.1 %collective-permute-start.22 = (bf16[576,512]{1,0:T(8,128)(2,1)S(1)}, bf16[576,512]{1,0:T(8,128)(2,1)S(1)}, u32[]{:S(2)}, u32[]{:S(2)}) collective-permute-start(bf16[576,512]{1,0:T(8,128)(2,1)S(1)} %get-tuple-element.141), channel_id=1, source_target_pairs={{0,6},{2,4},{4,2},{6,0},{8,14},{10,12},{12,10},{14,8},{16,22},{18,... | collective-permute-start | bytes 1769480 | tf_op jit(solution)/shard_map/ppermute | solution.py:822
  135.2 19.9 %collective-permute-start.32 = (bf16[352,512]{1,0:T(8,128)(2,1)S(1)}, bf16[352,512]{1,0:T(8,128)(2,1)S(1)}, u32[]{:S(2)}, u32[]{:S(2)}) collective-permute-start(bf16[352,512]{1,0:T(8,128)(2,1)S(1)} %get-tuple-element.161), channel_id=1, source_target_pairs={{0,2},{2,0},{4,6},{6,4},{8,10},{10,8},{12,14},{14,12},{16,18},{18,... | collective-permute-start | bytes 1081352 | tf_op jit(solution)/shard_map/ppermute | solution.py:822
  135.6 19.5 %collective-permute-start.33 = (bf16[352,512]{1,0:T(8,128)(2,1)S(1)}, bf16[352,512]{1,0:T(8,128)(2,1)S(1)}, u32[]{:S(2)}, u32[]{:S(2)}) collective-permute-start(bf16[352,512]{1,0:T(8,128)(2,1)S(1)} %get-tuple-element.162), channel_id=1, source_target_pairs={{0,4},{2,6},{4,0},{6,2},{8,12},{10,14},{12,8},{14,10},{16,20},{18,... | collective-permute-start | bytes 1081352 | tf_op jit(solution)/shard_map/ppermute | solution.py:822
  137.3 17.8 %collective-permute-start.34 = (bf16[352,512]{1,0:T(8,128)(2,1)S(1)}, bf16[352,512]{1,0:T(8,128)(2,1)S(1)}, u32[]{:S(2)}, u32[]{:S(2)}) collective-permute-start(bf16[352,512]{1,0:T(8,128)(2,1)S(1)} %get-tuple-element.163), channel_id=1, source_target_pairs={{0,6},{2,4},{4,2},{6,0},{8,14},{10,12},{12,10},{14,8},{16,22},{18,... | collective-permute-start | bytes 1081352 | tf_op jit(solution)/shard_map/ppermute | solution.py:822
  156.9 16.9 %collective-permute-start.38 = (bf16[232,512]{1,0:T(8,128)(2,1)S(1)}, bf16[232,512]{1,0:T(8,128)(2,1)S(1)}, u32[]{:S(2)}, u32[]{:S(2)}) collective-permute-start(bf16[232,512]{1,0:T(8,128)(2,1)S(1)} %get-tuple-element.168), channel_id=1, source_target_pairs={{0,16},{2,18},{4,20},{6,22},{8,24},{10,26},{12,28},{14,30},{16,0},... | collective-permute-start | bytes 712712 | tf_op jit(solution)/shard_map/ppermute | solution.py:822
  157.4 21.8 %collective-permute-start.39 = (bf16[232,512]{1,0:T(8,128)(2,1)S(1)}, bf16[232,512]{1,0:T(8,128)(2,1)S(1)}, u32[]{:S(2)}, u32[]{:S(2)}) collective-permute-start(bf16[232,512]{1,0:T(8,128)(2,1)S(1)} %get-tuple-element.169), channel_id=1, source_target_pairs={{0,24},{2,26},{4,28},{6,30},{8,16},{10,18},{12,20},{14,22},{16,8},... | collective-permute-start | bytes 712712 | tf_op jit(solution)/shard_map/ppermute | solution.py:822
  179.3 16.3 %collective-permute-start.40 = (bf16[576,512]{1,0:T(8,128)(2,1)S(1)}, bf16[576,512]{1,0:T(8,128)(2,1)S(1)}, u32[]{:S(2)}, u32[]{:S(2)}) collective-permute-start(bf16[576,512]{1,0:T(8,128)(2,1)S(1)} %place.3.refs_0_), channel_id=1, source_target_pairs={{0,2},{2,0},{4,6},{6,4},{8,10},{10,8},{12,14},{14,12},{16,18},{18,... | collective-permute-start | bytes 1769480 | tf_op jit(solution)/shard_map/ppermute | solution.py:822
  180.0 26.2 %collective-permute-start.41 = (bf16[576,512]{1,0:T(8,128)(2,1)S(1)}, bf16[576,512]{1,0:T(8,128)(2,1)S(1)}, u32[]{:S(2)}, u32[]{:S(2)}) collective-permute-start(bf16[576,512]{1,0:T(8,128)(2,1)S(1)} %place.3.refs_0_), channel_id=1, source_target_pairs={{0,4},{2,6},{4,0},{6,2},{8,12},{10,14},{12,8},{14,10},{16,20},{18,... | collective-permute-start | bytes 1769480 | tf_op jit(solution)/shard_map/ppermute | solution.py:822
  181.4 24.8 %collective-permute-start.42 = (bf16[576,512]{1,0:T(8,128)(2,1)S(1)}, bf16[576,512]{1,0:T(8,128)(2,1)S(1)}, u32[]{:S(2)}, u32[]{:S(2)}) collective-permute-start(bf16[576,512]{1,0:T(8,128)(2,1)S(1)} %place.3.refs_0_), channel_id=1, source_target_pairs={{0,6},{2,4},{4,2},{6,0},{8,14},{10,12},{12,10},{14,8},{16,22},{18,... | collective-permute-start | bytes 1769480 | tf_op jit(solution)/shard_map/ppermute | solution.py:822
  183.7 22.5 %all-to-all-start.2 = ((bf16[4,88,512]{2,1,0:T(8,128)(2,1)}), bf16[4,88,512]{2,1,0:T(8,128)(2,1)S(1)}, u32[]{:S(2)}, u32[]{:S(2)}) async-start(bf16[4,88,512]{2,1,0:T(8,128)(2,1)} %bitcast.26), calls=%async_computation.2 | async-start | bytes 720896 | tf_op jit(solution)/shard_map/all_to_all | solution.py:863
  213.3 15.0 %collective-permute-start.45 = (bf16[352,512]{1,0:T(8,128)(2,1)S(1)}, bf16[352,512]{1,0:T(8,128)(2,1)S(1)}, u32[]{:S(2)}, u32[]{:S(2)}) collective-permute-start(bf16[352,512]{1,0:T(8,128)(2,1)S(1)} %bitcast.58), channel_id=1, source_target_pairs={{0,4},{2,6},{4,0},{6,2},{8,12},{10,14},{12,8},{14,10},{16,20},{18,... | collective-permute-start | bytes 1081352 | tf_op jit(solution)/shard_map/ppermute | solution.py:822
  214.8 15.2 %collective-permute-start.46 = (bf16[352,512]{1,0:T(8,128)(2,1)S(1)}, bf16[352,512]{1,0:T(8,128)(2,1)}, u32[]{:S(2)}, u32[]{:S(2)}) collective-permute-start(bf16[352,512]{1,0:T(8,128)(2,1)S(1)} %bitcast.59), channel_id=1, source_target_pairs={{0,6},{2,4},{4,2},{6,0},{8,14},{10,12},{12,10},{14,8},{16,22},{18,... | collective-permute-start | bytes 1081352 | tf_op jit(solution)/shard_map/ppermute | solution.py:822
  (89 other events, 649.0 us)

commit v4 on v3

--- a/solution.py
+++ b/solution.py
@@ -974,6 +974,12 @@
     vec = whole(stack_vectors(vectors, width // 2))
     wo, wu, wd = whole(w_out), whole(w_up), whole(w_down)
 
+    fixed_args = (pos, wk, wv, wq, vec)
+    far = [own]
+    for _ in range(reach):
+        far.append(next_chip(far[-1], chips, 1))
+    k, v, q, hidden, low = project(info, [own], 0, True, *fixed_args)
+
     mine = order.reshape(ranks, ranks, slot)
     mine = lax.dynamic_slice_in_dim(mine, 4 * chip + 2 * core, 2, axis=1).reshape(rows) - base
     mine = (mine.reshape(1, rows), mine.reshape(rows, 1))
@@ -982,19 +988,17 @@
     give = jnp.where(core == 0, dealt[:, :, 1], dealt[:, :, 0])
     streams = by_core(core, keep, swap_core(give))
     sends = jnp.transpose(streams, (2, 0, 1, 3, 4)).reshape(rows, width)
+    sends = after(own, sends)
     arrived = lax.all_to_all(sends, "ctx", split_axis=0, concat_axis=0, tiled=True)
 
-    fixed_args = (pos, wk, wv, wq, vec)
-    far = send_window(own, reach, chips, 1)
-    own = after(arrived, own)
-    k, v, q, hidden, low = project(info, [own], 0, True, *fixed_args)
-    mine, far[1:] = lax.optimization_barrier((mine, after(k, far[1:])))
+    far[1:] = after((mine, k), far[1:])
+    arrived = after(far[1:], arrived)
 
     earlier = both_cores(far, core, 1)[::-1]
     before = len(earlier) * rows
     kp, vp = project(info, earlier, -before, False, *fixed_args)
     far_q = send_window(after(kp, q), reach, chips, -1)
-    att, exact, logs, log_stats = attend_forward(info, q, kp, k, vp, v)
+    att, exact, logs, log_stats = attend_forward(info, after(arrived, q), kp, k, vp, v)
     leaving, da_msg, dz1, active, df, h1, du, do, sums = feed_forward(
         info, att, exact, log_stats, hidden, arrived, mine, wo, wu, wd, vec
     )

time: 237 us -> 228 us (0.962)
  waiting for transfers between devices: 82.4 us -> 73.3 us
    ppermute x4 -> x2, waiting for transfers between devices: 11.2 us -> 0.01 us  [send_window(): far.append(lax.ppermute(own, 'ctx', pairs))]
    ppermute x2 -> x4, starting transfers between devices: 4.29 us -> 11.4 us  [next_chip(): lax.ppermute(block, 'ctx', pairs if step > 0 else [(b, a) for a, b in pai...]
    ppermute x2 -> x4, waiting for transfers between devices: 0.6 us -> 5.27 us  [next_chip(): lax.ppermute(block, 'ctx', pairs if step > 0 else [(b, a) for a, b in pai...]
    ppermute x4 -> x2, starting transfers between devices: 8.01 us -> 3.91 us  [send_window(): far.append(lax.ppermute(own, 'ctx', pairs))]
    unnamed x127 -> x121, local copies, waits for them, and re-layouts: 13.6 us -> 11.9 us
  transfers between devices with their start and end apart: 50 -> 50, of which waited for: 25 -> 20; matrix products, arithmetic and copies ran while one was open for 5% -> 5% of each run, Pallas kernels for 28% -> 29%
where the time goes in v4:
time: 228 us; the launch traced here: 225 us
  waiting for transfers between devices  73.3 us (32%)
  Pallas kernels  66.4 us (29%)
  starting transfers between devices  59.8 us (26%)
  local copies, waits for them, and re-layouts  14.9 us (7%)
  other arithmetic  9.15 us (4%)
    ppermute x18, waiting for transfers between devices, exchange(): lax.ppermute(piece, 'ctx', [(i, i ^ (k + 1) * stride) for i in range(rank...  55.8 us
    ppermute x18, starting transfers between devices, exchange(): lax.ppermute(piece, 'ctx', [(i, i ^ (k + 1) * stride) for i in range(rank...  19.7 us
    pallas_call x1, Pallas kernels, last(): pl.pallas_call(functools.partial(last_kernel, reach=count // 2, quarter=q...  13.5 us
    unnamed x121, local copies, waits for them, and re-layouts  11.9 us
    pallas_call x2, Pallas kernels, project(): pl.pallas_call(functools.partial(project_kernel, blocks=blocks, offset=of...  11.4 us
    ppermute x4, starting transfers between devices, next_chip(): lax.ppermute(block, 'ctx', pairs if step > 0 else [(b, a) for a, b in pai...  11.4 us
    pallas_call x1, Pallas kernels, attend_forward(): pl.pallas_call(forward_kernel, grid_spec=pltpu.PrefetchScalarGridSpec(num...  9.03 us
    pallas_call x1, Pallas kernels, feed_forward(): pl.pallas_call(ffn_kernel, grid_spec=pltpu.PrefetchScalarGridSpec(num_sca...  9.01 us
  transfers between devices with their start and end apart: 50, of which 20 were waited for; matrix products, arithmetic and copies ran while one was open for 5% of the time, Pallas kernels for 29%

profile of v4, /device:TPU:16, one launch (start us, length us, event | category | flops | bytes accessed | tf_op | source)
XLA Modules:
  0.0 225.3 jit_solution(17618470107103469711)
XLA Ops:
  10.4 3.5 %collective-permute-start.8 = (bf16[256,512]{1,0:T(8,128)(2,1)S(1)}, bf16[256,512]{1,0:T(8,128)(2,1)S(1)}, u32[]{:S(2)}, u32[]{:S(2)}) collective-permute-start(bf16[256,512]{1,0:T(8,128)(2,1)S(1)} %pad_maximum_fusion.refs_0_), channel_id=1, source_target_pairs={{0,8},{2,10},{4,12},{6,14},{8,16},{10,18},{12,20},{14,22},{16,24},... | collective-permute-start | bytes 786440 | tf_op jit(solution)/shard_map/ppermute | solution.py:890
  16.3 4.7 %collective-permute-done.8.refs_2_ = bf16[256,512]{1,0:T(8,128)(2,1)S(1)} collective-permute-done((bf16[256,512]{1,0:T(8,128)(2,1)S(1)}, bf16[256,512]{1,0:T(8,128)(2,1)S(1)}, u32[]{:S(2)}, u32[]{:S(2)}) %collective-permute-start.8) | collective-permute-done | bytes 262176 | tf_op jit(solution)/shard_map/ppermute | solution.py:890
  21.0 3.5 %collective-permute-start.9 = (bf16[256,512]{1,0:T(8,128)(2,1)S(1)}, bf16[256,512]{1,0:T(8,128)(2,1)S(1)}, u32[]{:S(2)}, u32[]{:S(2)}) collective-permute-start(bf16[256,512]{1,0:T(8,128)(2,1)S(1)} %collective-permute-done.8.refs_2_), channel_id=1, source_target_pairs={{0,8},{2,10},{4,12},{6,14},{8,16},{10,18},{12,20},{14,22},{16,24},... | collective-permute-start | bytes 786440 | tf_op jit(solution)/shard_map/ppermute | solution.py:890
  27.5 4.2 %project.2 = (bf16[256,512]{1,0:T(8,128)(2,1)}, bf16[256,512]{1,0:T(8,128)(2,1)}, bf16[256,512]{1,0:T(8,128)(2,1)}, f32[256,512]{1,0:T(8,128)}, bf16[256,512]{1,0:T(8,128)(2,1)}) custom-call(s32[11]{0:T(128)} %pad_add_fusion.1.info, bf16[256,512]{1,0:T(8,128)(2,1)} %copy-done.54, bf16[512,512]{1,0:T(8,128)(2,1)} %refs_4_.1, bf16[512,512]{1,0:T(8,128)(2,1)} %copy-done.51, ...), custom_call_target="tpu_custom_call" | custom-call | flops 4 | bytes 4 | tf_op jit(solution)/shard_map/project/pallas_call | solution.py:159
  33.2 5.5 %all-to-all-start = ((bf16[16,16,512]{2,1,0:T(8,128)(2,1)}), bf16[16,16,512]{2,1,0:T(8,128)(2,1)S(1)}, u32[]{:S(2)}, u32[]{:S(2)}) async-start(bf16[16,16,512]{2,1,0:T(8,128)(2,1)} %bitcast.16), calls=%async_computation | async-start | bytes 524288 | tf_op jit(solution)/shard_map/all_to_all | solution.py:992
  40.2 7.2 %project.3 = (bf16[1024,512]{1,0:T(8,128)(2,1)}, bf16[1024,512]{1,0:T(8,128)(2,1)}) custom-call(s32[11]{0:T(128)} %pad_add_fusion.1.info, bf16[256,512]{1,0:T(8,128)(2,1)} %copy-done.53, bf16[256,512]{1,0:T(8,128)(2,1)} %copy-done.56, bf16[256,512]{1,0:T(8,128)(2,1)} %copy-done.52, bf16[256,512]{1,0:T(8,128)(2,1)} %copy-done.57, bf16[512,512]{1,0:T(8,128)(2,1)} %refs_4_.1, ...), custom_call_target="tpu_custom_call" | custom-call | flops 10 | bytes 10 | tf_op jit(solution)/shard_map/project/pallas_call | solution.py:159
  54.0 9.0 %attend_forward.1 = (bf16[256,512]{1,0:T(8,128)(2,1)S(1)}, f32[256,512]{1,0:T(8,128)S(1)}, f32[256,512]{1,0:T(8,128)S(1)}, bf16[16,512]{1,0:T(8,128)(2,1)S(1)}) custom-call(s32[11]{0:T(128)S(1)} %copy-done.49, bf16[256,512]{1,0:T(8,128)(2,1)S(1)} %copy-done.12, bf16[1024,512]{1,0:T(8,128)(2,1)S(1)} %copy-done.6, bf16[256,512]{1,0:T(8,128)(2,1)S(1)} %copy-done.17, ...), custom_call_target="tpu_custom_call" | custom-call | flops 12 | bytes 12 | tf_op jit(solution)/shard_map/attend_forward/pallas_call | solution.py:281
  63.1 9.0 %feed_forward.1 = (bf16[256,512]{1,0:T(8,128)(2,1)}, bf16[288,512]{1,0:T(8,128)(2,1)S(1)}, f32[256,512]{1,0:T(8,128)S(1)}, bf16[256,2048]{1,0:T(8,128)(2,1)S(1)}...) custom-call(s32[11]{0:T(128)S(1)} %copy-done.49, ...), custom_call_target="tpu_custom_call" | custom-call | flops 10 | bytes 10 | tf_op jit(solution)/shard_map/feed_forward/pallas_call | solution.py:397
  74.4 4.1 %attend_query.2.refs_13_ = bf16[256,256]{1,0:T(8,128)(2,1)S(1)} custom-call(s32[11]{0:T(128)S(1)} %copy-done.49, bf16[256,512]{1,0:T(8,128)(2,1)S(1)} %copy-done.12, bf16[1024,512]{1,0:T(8,128)(2,1)S(1)} %copy-done.7, bf16[256,512]{1,0:T(8,128)(2,1)S(1)} %copy-done.17, bf16[1024,512]{1,0:T(8,128)(2,1)S(1)} %copy-done.10, bf16[256,512]{1,0:T(8,128)(2,1)S(1)} %copy-done.18, ...), custom_call_target="tpu_custom_call" | custom-call | flops 5 | bytes 5 | tf_op jit(solution)/shard_map/attend_query/pallas_call | solution.py:525
  78.6 4.2 %ffn_grads.1 = (bf16[2304,512]{1,0:T(8,128)(2,1)S(1)}, bf16[2304,512]{1,0:T(8,128)(2,1)}) custom-call(s32[11]{0:T(128)S(1)} %copy-done.49, bf16[256,512]{1,0:T(8,128)(2,1)S(1)} %get-tuple-element.115.a_ref.a_own.a_other, bf16[256,512]{1,0:T(8,128)(2,1)S(1)} %get-tuple-element.115.a_ref.a_own.a_other, bf16[256,512]{1,0:T(8,128)(2,1)S(1)} %get-tuple-element.126.do_ref, ...), custom_call_target="tpu_custom_call" | custom-call | flops 10 | bytes 10 | tf_op jit(solution)/shard_map/ffn_grads/pallas_call | solution.py:466
  94.8 4.1 %attend_query.3.refs_14_ = bf16[256,256]{1,0:T(8,128)(2,1)S(1)} custom-call(s32[11]{0:T(128)S(1)} %copy-done.49, bf16[256,512]{1,0:T(8,128)(2,1)S(1)} %copy-done.12, bf16[1024,512]{1,0:T(8,128)(2,1)S(1)} %copy-done.8, bf16[256,512]{1,0:T(8,128)(2,1)S(1)} %copy-done.17, bf16[1024,512]{1,0:T(8,128)(2,1)S(1)} %copy-done.11, bf16[256,512]{1,0:T(8,128)(2,1)S(1)} %copy-done.19, ...), custom_call_target="tpu_custom_call" | custom-call | flops 5 | bytes 5 | tf_op jit(solution)/shard_map/attend_query/pallas_call | solution.py:525
  103.0 13.5 %last.1 = (bf16[1408,512]{1,0:T(8,128)(2,1)S(1)}, bf16[1408,512]{1,0:T(8,128)(2,1)}, bf16[256,512]{1,0:T(8,128)(2,1)S(1)}) custom-call(s32[11]{0:T(128)S(1)} %copy-done.49, bf16[256,512]{1,0:T(8,128)(2,1)S(1)} %copy-done.12, bf16[256,512]{1,0:T(8,128)(2,1)S(1)} %collective-permute-done.27.refs_1_, bf16[256,512]{1,0:T(8,128)(2,1)S(1)} %copy-done.33, ...), custom_call_target="tpu_custom_call" | custom-call | flops 15 | bytes 15 | tf_op jit(solution)/shard_map/last/pallas_call | solution.py:638
  131.9 4.7 %collective-permute-done.23.refs_1_ = bf16[144,512]{1,0:T(8,128)(2,1)S(1)} collective-permute-done((bf16[144,512]{1,0:T(8,128)(2,1)S(1)}, bf16[144,512]{1,0:T(8,128)(2,1)S(1)}, u32[]{:S(2)}, u32[]{:S(2)}) %collective-permute-start.23) | collective-permute-done | bytes 147488 | tf_op jit(solution)/shard_map/ppermute | solution.py:822
  138.5 7.6 %collective-permute-done.25.refs_3_ = bf16[144,512]{1,0:T(8,128)(2,1)S(1)} collective-permute-done((bf16[144,512]{1,0:T(8,128)(2,1)S(1)}, bf16[144,512]{1,0:T(8,128)(2,1)S(1)}, u32[]{:S(2)}, u32[]{:S(2)}) %collective-permute-start.25) | collective-permute-done | bytes 147488 | tf_op jit(solution)/shard_map/ppermute | solution.py:822
  151.2 4.4 %collective-permute-done.36 = bf16[128,512]{1,0:T(8,128)(2,1)S(1)} collective-permute-done((bf16[128,512]{1,0:T(8,128)(2,1)S(1)}, bf16[128,512]{1,0:T(8,128)(2,1)S(1)}, u32[]{:S(2)}, u32[]{:S(2)}) %collective-permute-start.36) | collective-permute-done | bytes 131104 | tf_op jit(solution)/shard_map/ppermute | solution.py:1054
  156.8 8.1 %collective-permute-done.38.refs_2_.refs_1_ = bf16[232,512]{1,0:T(8,128)(2,1)S(1)} collective-permute-done((bf16[232,512]{1,0:T(8,128)(2,1)S(1)}, bf16[232,512]{1,0:T(8,128)(2,1)S(1)}, u32[]{:S(2)}, u32[]{:S(2)}) %collective-permute-start.38) | collective-permute-done | bytes 237600 | tf_op jit(solution)/shard_map/ppermute | solution.py:822
  164.9 5.4 %collective-permute-done.39.refs_3_.refs_2_ = bf16[232,512]{1,0:T(8,128)(2,1)S(1)} collective-permute-done((bf16[232,512]{1,0:T(8,128)(2,1)S(1)}, bf16[232,512]{1,0:T(8,128)(2,1)S(1)}, u32[]{:S(2)}, u32[]{:S(2)}) %collective-permute-start.39) | collective-permute-done | bytes 237600 | tf_op jit(solution)/shard_map/ppermute | solution.py:822
  174.7 4.2 %all-to-all-start.2 = ((bf16[4,88,512]{2,1,0:T(8,128)(2,1)}), bf16[4,88,512]{2,1,0:T(8,128)(2,1)S(1)}, u32[]{:S(2)}, u32[]{:S(2)}) async-start(bf16[4,88,512]{2,1,0:T(8,128)(2,1)} %bitcast.27), calls=%async_computation.2 | async-start | bytes 720896 | tf_op jit(solution)/shard_map/all_to_all | solution.py:863
  178.9 7.8 %collective-permute-done.40.refs_1_ = bf16[576,512]{1,0:T(8,128)(2,1)S(1)} collective-permute-done((bf16[576,512]{1,0:T(8,128)(2,1)S(1)}, bf16[576,512]{1,0:T(8,128)(2,1)S(1)}, u32[]{:S(2)}, u32[]{:S(2)}) %collective-permute-start.40) | collective-permute-done | bytes 589856 | tf_op jit(solution)/shard_map/ppermute | solution.py:822
  186.7 10.5 %collective-permute-done.41.refs_2_ = bf16[576,512]{1,0:T(8,128)(2,1)S(1)} collective-permute-done((bf16[576,512]{1,0:T(8,128)(2,1)S(1)}, bf16[576,512]{1,0:T(8,128)(2,1)S(1)}, u32[]{:S(2)}, u32[]{:S(2)}) %collective-permute-start.41) | collective-permute-done | bytes 589856 | tf_op jit(solution)/shard_map/ppermute | solution.py:822
  197.2 5.7 %all-to-all-start.1 = ((bf16[16,16,512]{2,1,0:T(8,128)(2,1)}), bf16[16,16,512]{2,1,0:T(8,128)(2,1)}, u32[]{:S(2)}, u32[]{:S(2)}) async-start(bf16[16,16,512]{2,1,0:T(8,128)(2,1)} %bitcast.18), calls=%async_computation.1 | async-start | bytes 524288 | tf_op jit(solution)/shard_map/all_to_all | solution.py:1070
  206.4 3.4 %all-to-all-done.1 = bf16[16,16,512]{2,1,0:T(8,128)(2,1)} async-done(((bf16[16,16,512]{2,1,0:T(8,128)(2,1)}), bf16[16,16,512]{2,1,0:T(8,128)(2,1)}, u32[]{:S(2)}, u32[]{:S(2)}) %all-to-all-start.1) | async-done | bytes 262176 | tf_op jit(solution)/shard_map/all_to_all | solution.py:1070
  215.7 3.6 %collective-permute-done.45.refs_2_ = bf16[352,512]{1,0:T(8,128)(2,1)S(1)} collective-permute-done((bf16[352,512]{1,0:T(8,128)(2,1)S(1)}, bf16[352,512]{1,0:T(8,128)(2,1)S(1)}, u32[]{:S(2)}, u32[]{:S(2)}) %collective-permute-start.45) | collective-permute-done | bytes 360480 | tf_op jit(solution)/shard_map/ppermute | solution.py:822
  220.9 3.6 %place.4 = (f32[256,512]{1,0:T(8,128)}, f32[256,512]{1,0:T(8,128)}, f32[256,512]{1,0:T(8,128)}, f32[512,512]{1,0:T(8,128)}, f32[1,256]{1,0:T(1,128)}, /*index=5*...) custom-call(s32[2]{0:T(128)S(1)} %pad_add_fusion.2.digit_ref, ...), custom_call_target="tpu_custom_call" | custom-call | flops 4 | bytes 4 | tf_op jit(solution)/shard_map/place/pallas_call | solution.py:802
  (247 shorter events, 82.0 us)
Async XLA Ops:
  9.8 14.8 %collective-permute-start.4 = (bf16[256,512]{1,0:T(8,128)(2,1)}, bf16[256,512]{1,0:T(8,128)(2,1)S(1)}, u32[]{:S(2)}, u32[]{:S(2)}) collective-permute-start(bf16[256,512]{1,0:T(8,128)(2,1)} %refs_19_.1), channel_id=1, source_target_pairs={{0,1},{1,0},{2,3},{3,2},{4,5},{5,4},{6,7},{7,6},{8,9},{9,8},{10,11... | collective-permute-start | bytes 786440 | tf_op jit(solution)/shard_map/ppermute | solution.py:881
  10.3 14.4 %collective-permute-start.5 = (bf16[256,512]{1,0:T(8,128)(2,1)}, bf16[256,512]{1,0:T(8,128)(2,1)S(1)}, u32[]{:S(2)}, u32[]{:S(2)}) collective-permute-start(bf16[256,512]{1,0:T(8,128)(2,1)} %refs_21_.1), channel_id=1, source_target_pairs={{0,1},{1,0},{2,3},{3,2},{4,5},{5,4},{6,7},{7,6},{8,9},{9,8},{10,11... | collective-permute-start | bytes 786440 | tf_op jit(solution)/shard_map/ppermute | solution.py:881
  24.6 38.4 %collective-permute-start.16 = (bf16[256,2048]{1,0:T(8,128)(2,1)}, bf16[256,2048]{1,0:T(8,128)(2,1)}, u32[]{:S(2)}, u32[]{:S(2)}) collective-permute-start(bf16[256,2048]{1,0:T(8,128)(2,1)} %wu_a.1), channel_id=1, source_target_pairs={{0,1},{1,0},{2,3},{3,2},{4,5},{5,4},{6,7},{7,6},{8,9},{9,8},{10,11... | collective-permute-start | bytes 3145736 | tf_op jit(solution)/shard_map/ppermute | solution.py:881
  24.7 38.3 %collective-permute-start.17 = (bf16[1024,512]{1,0:T(8,128)(2,1)}, bf16[1024,512]{1,0:T(8,128)(2,1)}, u32[]{:S(2)}, u32[]{:S(2)}) collective-permute-start(bf16[1024,512]{1,0:T(8,128)(2,1)} %wd_a.1), channel_id=1, source_target_pairs={{0,1},{1,0},{2,3},{3,2},{4,5},{5,4},{6,7},{7,6},{8,9},{9,8},{10,11... | collective-permute-start | bytes 3145736 | tf_op jit(solution)/shard_map/ppermute | solution.py:881
  33.2 18.3 %all-to-all-start = ((bf16[16,16,512]{2,1,0:T(8,128)(2,1)}), bf16[16,16,512]{2,1,0:T(8,128)(2,1)S(1)}, u32[]{:S(2)}, u32[]{:S(2)}) async-start(bf16[16,16,512]{2,1,0:T(8,128)(2,1)} %bitcast.16), calls=%async_computation | async-start | bytes 524288 | tf_op jit(solution)/shard_map/all_to_all | solution.py:992
  38.7 24.4 %collective-permute-start.15 = (bf16[256,512]{1,0:T(8,128)(2,1)S(1)}, bf16[256,512]{1,0:T(8,128)(2,1)S(1)}, u32[]{:S(2)}, u32[]{:S(2)}) collective-permute-start(bf16[256,512]{1,0:T(8,128)(2,1)S(1)} %copy-done.43), channel_id=1, source_target_pairs={{0,1},{1,0},{2,3},{3,2},{4,5},{5,4},{6,7},{7,6},{8,9},{9,8},{10,11... | collective-permute-start | bytes 786440 | tf_op jit(solution)/shard_map/ppermute | solution.py:881
  47.4 24.7 %collective-permute-start.13 = (bf16[256,512]{1,0:T(8,128)(2,1)S(1)}, bf16[256,512]{1,0:T(8,128)(2,1)S(1)}, u32[]{:S(2)}, u32[]{:S(2)}) collective-permute-start(bf16[256,512]{1,0:T(8,128)(2,1)S(1)} %copy-done.12), channel_id=1, source_target_pairs={{8,0},{10,2},{12,4},{14,6},{16,8},{18,10},{20,12},{22,14},{24,16},... | collective-permute-start | bytes 786440 | tf_op jit(solution)/shard_map/ppermute | solution.py:900
  50.0 22.1 %collective-permute-start.14 = (bf16[256,512]{1,0:T(8,128)(2,1)S(1)}, bf16[256,512]{1,0:T(8,128)(2,1)S(1)}, u32[]{:S(2)}, u32[]{:S(2)}) collective-permute-start(bf16[256,512]{1,0:T(8,128)(2,1)S(1)} %copy-done.12), channel_id=1, source_target_pairs={{16,0},{18,2},{20,4},{22,6},{24,8},{26,10},{28,12},{30,14},{17,1},... | collective-permute-start | bytes 786440 | tf_op jit(solution)/shard_map/ppermute | solution.py:900
  83.3 15.8 %collective-permute-start.26 = (bf16[288,512]{1,0:T(8,128)(2,1)}, bf16[288,512]{1,0:T(8,128)(2,1)}, u32[]{:S(2)}, u32[]{:S(2)}) collective-permute-start(bf16[288,512]{1,0:T(8,128)(2,1)} %collective-permute-done.18.refs_7_), channel_id=1, source_target_pairs={{8,0},{10,2},{12,4},{14,6},{16,8},{18,10},{20,12},{22,14},{24,16},... | collective-permute-start | bytes 884744 | tf_op jit(solution)/shard_map/ppermute | solution.py:890
  91.2 26.0 %collective-permute-start.20 = (bf16[576,512]{1,0:T(8,128)(2,1)S(1)}, bf16[576,512]{1,0:T(8,128)(2,1)S(1)}, u32[]{:S(2)}, u32[]{:S(2)}) collective-permute-start(bf16[576,512]{1,0:T(8,128)(2,1)S(1)} %get-tuple-element.135), channel_id=1, source_target_pairs={{0,2},{2,0},{4,6},{6,4},{8,10},{10,8},{12,14},{14,12},{16,18},{18,... | collective-permute-start | bytes 1769480 | tf_op jit(solution)/shard_map/ppermute | solution.py:822
  92.8 27.7 %collective-permute-start.21 = (bf16[576,512]{1,0:T(8,128)(2,1)S(1)}, bf16[576,512]{1,0:T(8,128)(2,1)S(1)}, u32[]{:S(2)}, u32[]{:S(2)}) collective-permute-start(bf16[576,512]{1,0:T(8,128)(2,1)S(1)} %get-tuple-element.136), channel_id=1, source_target_pairs={{0,4},{2,6},{4,0},{6,2},{8,12},{10,14},{12,8},{14,10},{16,20},{18,... | collective-permute-start | bytes 1769480 | tf_op jit(solution)/shard_map/ppermute | solution.py:822
  94.2 27.1 %collective-permute-start.22 = (bf16[576,512]{1,0:T(8,128)(2,1)S(1)}, bf16[576,512]{1,0:T(8,128)(2,1)S(1)}, u32[]{:S(2)}, u32[]{:S(2)}) collective-permute-start(bf16[576,512]{1,0:T(8,128)(2,1)S(1)} %get-tuple-element.137), channel_id=1, source_target_pairs={{0,6},{2,4},{4,2},{6,0},{8,14},{10,12},{12,10},{14,8},{16,22},{18,... | collective-permute-start | bytes 1769480 | tf_op jit(solution)/shard_map/ppermute | solution.py:822
  126.3 19.8 %collective-permute-start.32 = (bf16[352,512]{1,0:T(8,128)(2,1)S(1)}, bf16[352,512]{1,0:T(8,128)(2,1)S(1)}, u32[]{:S(2)}, u32[]{:S(2)}) collective-permute-start(bf16[352,512]{1,0:T(8,128)(2,1)S(1)} %get-tuple-element.157), channel_id=1, source_target_pairs={{0,2},{2,0},{4,6},{6,4},{8,10},{10,8},{12,14},{14,12},{16,18},{18,... | collective-permute-start | bytes 1081352 | tf_op jit(solution)/shard_map/ppermute | solution.py:822
  126.7 19.4 %collective-permute-start.33 = (bf16[352,512]{1,0:T(8,128)(2,1)S(1)}, bf16[352,512]{1,0:T(8,128)(2,1)S(1)}, u32[]{:S(2)}, u32[]{:S(2)}) collective-permute-start(bf16[352,512]{1,0:T(8,128)(2,1)S(1)} %get-tuple-element.158), channel_id=1, source_target_pairs={{0,4},{2,6},{4,0},{6,2},{8,12},{10,14},{12,8},{14,10},{16,20},{18,... | collective-permute-start | bytes 1081352 | tf_op jit(solution)/shard_map/ppermute | solution.py:822
  128.4 17.7 %collective-permute-start.34 = (bf16[352,512]{1,0:T(8,128)(2,1)S(1)}, bf16[352,512]{1,0:T(8,128)(2,1)S(1)}, u32[]{:S(2)}, u32[]{:S(2)}) collective-permute-start(bf16[352,512]{1,0:T(8,128)(2,1)S(1)} %get-tuple-element.159), channel_id=1, source_target_pairs={{0,6},{2,4},{4,2},{6,0},{8,14},{10,12},{12,10},{14,8},{16,22},{18,... | collective-permute-start | bytes 1081352 | tf_op jit(solution)/shard_map/ppermute | solution.py:822
  148.0 16.9 %collective-permute-start.38 = (bf16[232,512]{1,0:T(8,128)(2,1)S(1)}, bf16[232,512]{1,0:T(8,128)(2,1)S(1)}, u32[]{:S(2)}, u32[]{:S(2)}) collective-permute-start(bf16[232,512]{1,0:T(8,128)(2,1)S(1)} %get-tuple-element.164), channel_id=1, source_target_pairs={{0,16},{2,18},{4,20},{6,22},{8,24},{10,26},{12,28},{14,30},{16,0},... | collective-permute-start | bytes 712712 | tf_op jit(solution)/shard_map/ppermute | solution.py:822
  148.5 21.8 %collective-permute-start.39 = (bf16[232,512]{1,0:T(8,128)(2,1)S(1)}, bf16[232,512]{1,0:T(8,128)(2,1)S(1)}, u32[]{:S(2)}, u32[]{:S(2)}) collective-permute-start(bf16[232,512]{1,0:T(8,128)(2,1)S(1)} %get-tuple-element.165), channel_id=1, source_target_pairs={{0,24},{2,26},{4,28},{6,30},{8,16},{10,18},{12,20},{14,22},{16,8},... | collective-permute-start | bytes 712712 | tf_op jit(solution)/shard_map/ppermute | solution.py:822
  170.4 16.3 %collective-permute-start.40 = (bf16[576,512]{1,0:T(8,128)(2,1)S(1)}, bf16[576,512]{1,0:T(8,128)(2,1)S(1)}, u32[]{:S(2)}, u32[]{:S(2)}) collective-permute-start(bf16[576,512]{1,0:T(8,128)(2,1)S(1)} %place.3.refs_0_), channel_id=1, source_target_pairs={{0,2},{2,0},{4,6},{6,4},{8,10},{10,8},{12,14},{14,12},{16,18},{18,... | collective-permute-start | bytes 1769480 | tf_op jit(solution)/shard_map/ppermute | solution.py:822
  171.1 26.1 %collective-permute-start.41 = (bf16[576,512]{1,0:T(8,128)(2,1)S(1)}, bf16[576,512]{1,0:T(8,128)(2,1)S(1)}, u32[]{:S(2)}, u32[]{:S(2)}) collective-permute-start(bf16[576,512]{1,0:T(8,128)(2,1)S(1)} %place.3.refs_0_), channel_id=1, source_target_pairs={{0,4},{2,6},{4,0},{6,2},{8,12},{10,14},{12,8},{14,10},{16,20},{18,... | collective-permute-start | bytes 1769480 | tf_op jit(solution)/shard_map/ppermute | solution.py:822
  172.5 24.7 %collective-permute-start.42 = (bf16[576,512]{1,0:T(8,128)(2,1)S(1)}, bf16[576,512]{1,0:T(8,128)(2,1)S(1)}, u32[]{:S(2)}, u32[]{:S(2)}) collective-permute-start(bf16[576,512]{1,0:T(8,128)(2,1)S(1)} %place.3.refs_0_), channel_id=1, source_target_pairs={{0,6},{2,4},{4,2},{6,0},{8,14},{10,12},{12,10},{14,8},{16,22},{18,... | collective-permute-start | bytes 1769480 | tf_op jit(solution)/shard_map/ppermute | solution.py:822
  174.7 22.5 %all-to-all-start.2 = ((bf16[4,88,512]{2,1,0:T(8,128)(2,1)}), bf16[4,88,512]{2,1,0:T(8,128)(2,1)S(1)}, u32[]{:S(2)}, u32[]{:S(2)}) async-start(bf16[4,88,512]{2,1,0:T(8,128)(2,1)} %bitcast.27), calls=%async_computation.2 | async-start | bytes 720896 | tf_op jit(solution)/shard_map/all_to_all | solution.py:863
  204.4 14.9 %collective-permute-start.45 = (bf16[352,512]{1,0:T(8,128)(2,1)S(1)}, bf16[352,512]{1,0:T(8,128)(2,1)S(1)}, u32[]{:S(2)}, u32[]{:S(2)}) collective-permute-start(bf16[352,512]{1,0:T(8,128)(2,1)S(1)} %bitcast.59), channel_id=1, source_target_pairs={{0,4},{2,6},{4,0},{6,2},{8,12},{10,14},{12,8},{14,10},{16,20},{18,... | collective-permute-start | bytes 1081352 | tf_op jit(solution)/shard_map/ppermute | solution.py:822
  205.8 15.0 %collective-permute-start.46 = (bf16[352,512]{1,0:T(8,128)(2,1)S(1)}, bf16[352,512]{1,0:T(8,128)(2,1)}, u32[]{:S(2)}, u32[]{:S(2)}) collective-permute-start(bf16[352,512]{1,0:T(8,128)(2,1)S(1)} %bitcast.60), channel_id=1, source_target_pairs={{0,6},{2,4},{4,2},{6,0},{8,14},{10,12},{12,10},{14,8},{16,22},{18,... | collective-permute-start | bytes 1081352 | tf_op jit(solution)/shard_map/ppermute | solution.py:822
  210.8 13.7 %collective-permute-start.43 = (bf16[4,2,16,512]{3,2,0,1:T(8,128)(2,1)S(1)}, bf16[4,2,16,512]{3,2,0,1:T(8,128)(2,1)S(1)}, u32[]{:S(2)}, u32[]{:S(2)}) collective-permute-start(bf16[4,2,16,512]{3,2,0,1:T(8,128)(2,1)S(1)} %get-tuple-element.195), channel_id=1, source_target_pairs={{0,1},{1,0},{2,3},{3,2},{4,5},{5,4},{6,7},{7,6},{8,9},{9,8},{10,11... | collective-permute-start | bytes 393224 | tf_op jit(solution)/shard_map/ppermute | solution.py:881
  (86 other events, 651.0 us)

commit v5 on v4

--- a/solution.py
+++ b/solution.py
@@ -593,14 +593,15 @@
     def _():
         dk, dv = dk_all[...], dv_all[...]
         step_rows = width // 8
-        split_halves(info, mine, send, [n * quarter for n in range(4)], dot_tn(low_ref[...], dk))
-        split_halves(info, mine, send, [n * quarter + step_rows for n in range(4)], dot_tn(low_ref[...], dv))
+        turned = low_ref[...].T
+        split_halves(info, mine, send, [n * quarter for n in range(4)], dot(turned, dk))
+        split_halves(info, mine, send, [n * quarter + step_rows for n in range(4)], dot(turned, dv))
         dq = jnp.concatenate([dq_a[...], dq_b[...]], axis=1)
-        split_halves(info, mine, send, [n * quarter + 2 * step_rows for n in range(4)], dot_tn(low_ref[...], dq))
+        split_halves(info, mine, send, [n * quarter + 2 * step_rows for n in range(4)], dot(turned, dq))
         dh = dz1_ref[...] + dot_nt(dq, wq[...]) + dot_nt(dk, wk[...]) + dot_nt(dv, wv[...])
         dh_out[...] = dh.astype(BF)
         parts = []
-        for _ in range(3):
+        for _ in range(2):
             parts.append(dh.astype(BF))
             dh = dh - parts[-1].astype(F32)
         spots = info[1] + iota((1, rows), 1)
@@ -610,7 +611,7 @@
         for half in range(2):
             for n in range(4):
                 hot = (place - (half * 4 + n) * fourth == iota((fourth, rows), 0)).astype(F32).astype(BF)
-                total = dot(hot, parts[0]) + dot(hot, parts[1]) + dot(hot, parts[2])
+                total = dot(hot, parts[0]) + dot(hot, parts[1])
                 keep_or_send(info, half, mine, send, n * quarter + base, total)
         base += fourth
         spare = quarter - base
@@ -675,7 +676,7 @@
 
 def cut(terms, digit, radix, kept):
     rows, width = rows_of(terms) // radix, terms[0][0].shape[1]
-    subs = max(n for n in (1, 2, 3, 4) if rows % (8 * n) == 0 and rows // n >= 64 or n == 1)
+    subs = 1
     specs = [
         pl.BlockSpec((rows // subs, width), lambda n, d, k=k, b=b: ((b * radix + (d[0] ^ k)) * subs + n, 0))
         for k in range(radix)
@@ -1043,6 +1044,7 @@
         pieces_last = two.cut(after(pieces, terms_last), level)
         terms_last = two.scatter(pieces_last, level)
     terms_last = [(x, 0) for x in terms_last]
+    leaving = after(terms_last[1][0], leaving)
     stride, radix = one.stages[end]
     held, held_last, *messages = join(terms, terms_last, one.digit(end), radix)
     got = exchange(messages, here, stride, ranks)
@@ -1066,7 +1068,6 @@
     held_last = after(parts[1:], held_last)
     parts_last = two.gather(held_last, 0)
     held = one.place(parts, 0)
-    leaving = after(parts[1:], leaving)
     landed = lax.all_to_all(leaving, "ctx", split_axis=0, concat_axis=0, tiled=True)
 
     landed = landed.reshape(chips, 2, 2, 2 * slot, width)

time: 228 us -> 223 us (0.978)
  waiting for transfers between devices: 73.3 us -> 65.4 us
    ppermute x18, waiting for transfers between devices: 55.8 us -> 44.3 us  [exchange(): lax.ppermute(piece, 'ctx', [(i, i ^ (k + 1) * stride) for i in range(rank...]
    all_to_all x1, waiting for transfers between devices: 0.01 us -> 6.02 us  [trade(): lax.all_to_all(blocks, 'ctx', split_axis=0, concat_axis=0, axis_index_gro...]
    all_to_all x1, waiting for transfers between devices: 3.4 us -> 0.01 us  [shards(): lax.all_to_all(leaving, 'ctx', split_axis=0, concat_axis=0, tiled=True)]
    unnamed x121 -> x125, local copies, waits for them, and re-layouts: 11.9 us -> 14.8 us
  transfers between devices with their start and end apart: 50 -> 50, of which waited for: 20 -> 18; matrix products, arithmetic and copies ran while one was open for 5% -> 4% of each run, Pallas kernels for 29% -> 28%
where the time goes in v5:
time: 223 us; the launch traced here: 219 us
  Pallas kernels  65.5 us (29%)
  waiting for transfers between devices  65.4 us (29%)
  starting transfers between devices  61.1 us (27%)
  local copies, waits for them, and re-layouts  16.8 us (8%)
  other arithmetic  7.96 us (4%)
    ppermute x18, waiting for transfers between devices, exchange(): lax.ppermute(piece, 'ctx', [(i, i ^ (k + 1) * stride) for i in range(rank...  44.3 us
    ppermute x18, starting transfers between devices, exchange(): lax.ppermute(piece, 'ctx', [(i, i ^ (k + 1) * stride) for i in range(rank...  20.2 us
    unnamed x125, local copies, waits for them, and re-layouts  14.8 us
    pallas_call x1, Pallas kernels, last(): pl.pallas_call(functools.partial(last_kernel, reach=count // 2, quarter=q...  13.2 us
    pallas_call x2, Pallas kernels, project(): pl.pallas_call(functools.partial(project_kernel, blocks=blocks, offset=of...  11.4 us
    ppermute x4, starting transfers between devices, next_chip(): lax.ppermute(block, 'ctx', pairs if step > 0 else [(b, a) for a, b in pai...  11.4 us
    pallas_call x1, Pallas kernels, attend_forward(): pl.pallas_call(forward_kernel, grid_spec=pltpu.PrefetchScalarGridSpec(num...  9.04 us
    pallas_call x1, Pallas kernels, feed_forward(): pl.pallas_call(ffn_kernel, grid_spec=pltpu.PrefetchScalarGridSpec(num_sca...  9.01 us
  transfers between devices with their start and end apart: 50, of which 18 were waited for; matrix products, arithmetic and copies ran while one was open for 4% of the time, Pallas kernels for 28%

profile of v5, /device:TPU:16, one launch (start us, length us, event | category | flops | bytes accessed | tf_op | source)
XLA Modules:
  0.0 218.7 jit_solution(14947486223047861173)
XLA Ops:
  10.4 3.5 %collective-permute-start.8 = (bf16[256,512]{1,0:T(8,128)(2,1)S(1)}, bf16[256,512]{1,0:T(8,128)(2,1)S(1)}, u32[]{:S(2)}, u32[]{:S(2)}) collective-permute-start(bf16[256,512]{1,0:T(8,128)(2,1)S(1)} %pad_maximum_fusion.refs_0_), channel_id=1, source_target_pairs={{0,8},{2,10},{4,12},{6,14},{8,16},{10,18},{12,20},{14,22},{16,24},... | collective-permute-start | bytes 786440 | tf_op jit(solution)/shard_map/ppermute | solution.py:891
  16.3 4.7 %collective-permute-done.8.refs_2_ = bf16[256,512]{1,0:T(8,128)(2,1)S(1)} collective-permute-done((bf16[256,512]{1,0:T(8,128)(2,1)S(1)}, bf16[256,512]{1,0:T(8,128)(2,1)S(1)}, u32[]{:S(2)}, u32[]{:S(2)}) %collective-permute-start.8) | collective-permute-done | bytes 262176 | tf_op jit(solution)/shard_map/ppermute | solution.py:891
  21.0 3.5 %collective-permute-start.9 = (bf16[256,512]{1,0:T(8,128)(2,1)S(1)}, bf16[256,512]{1,0:T(8,128)(2,1)S(1)}, u32[]{:S(2)}, u32[]{:S(2)}) collective-permute-start(bf16[256,512]{1,0:T(8,128)(2,1)S(1)} %collective-permute-done.8.refs_2_), channel_id=1, source_target_pairs={{0,8},{2,10},{4,12},{6,14},{8,16},{10,18},{12,20},{14,22},{16,24},... | collective-permute-start | bytes 786440 | tf_op jit(solution)/shard_map/ppermute | solution.py:891
  27.5 4.2 %project.2 = (bf16[256,512]{1,0:T(8,128)(2,1)}, bf16[256,512]{1,0:T(8,128)(2,1)}, bf16[256,512]{1,0:T(8,128)(2,1)}, f32[256,512]{1,0:T(8,128)}, bf16[256,512]{1,0:T(8,128)(2,1)}) custom-call(s32[11]{0:T(128)} %pad_add_fusion.1.info, bf16[256,512]{1,0:T(8,128)(2,1)} %copy-done.58, bf16[512,512]{1,0:T(8,128)(2,1)} %refs_4_.1, bf16[512,512]{1,0:T(8,128)(2,1)} %copy-done.55, ...), custom_call_target="tpu_custom_call" | custom-call | flops 4 | bytes 4 | tf_op jit(solution)/shard_map/project/pallas_call | solution.py:159
  33.2 5.5 %all-to-all-start = ((bf16[16,16,512]{2,1,0:T(8,128)(2,1)}), bf16[16,16,512]{2,1,0:T(8,128)(2,1)S(1)}, u32[]{:S(2)}, u32[]{:S(2)}) async-start(bf16[16,16,512]{2,1,0:T(8,128)(2,1)} %bitcast.16), calls=%async_computation | async-start | bytes 524288 | tf_op jit(solution)/shard_map/all_to_all | solution.py:993
  40.2 7.2 %project.3 = (bf16[1024,512]{1,0:T(8,128)(2,1)}, bf16[1024,512]{1,0:T(8,128)(2,1)}) custom-call(s32[11]{0:T(128)} %pad_add_fusion.1.info, bf16[256,512]{1,0:T(8,128)(2,1)} %copy-done.57, bf16[256,512]{1,0:T(8,128)(2,1)} %copy-done.60, bf16[256,512]{1,0:T(8,128)(2,1)} %copy-done.56, bf16[256,512]{1,0:T(8,128)(2,1)} %copy-done.61, bf16[512,512]{1,0:T(8,128)(2,1)} %refs_4_.1, ...), custom_call_target="tpu_custom_call" | custom-call | flops 10 | bytes 10 | tf_op jit(solution)/shard_map/project/pallas_call | solution.py:159
  54.0 9.0 %attend_forward.1 = (bf16[256,512]{1,0:T(8,128)(2,1)S(1)}, f32[256,512]{1,0:T(8,128)S(1)}, f32[256,512]{1,0:T(8,128)S(1)}, bf16[16,512]{1,0:T(8,128)(2,1)S(1)}) custom-call(s32[11]{0:T(128)S(1)} %copy-done.53, bf16[256,512]{1,0:T(8,128)(2,1)S(1)} %copy-done.14, bf16[1024,512]{1,0:T(8,128)(2,1)S(1)} %copy-done.8, bf16[256,512]{1,0:T(8,128)(2,1)S(1)} %copy-done.19, ...), custom_call_target="tpu_custom_call" | custom-call | flops 12 | bytes 12 | tf_op jit(solution)/shard_map/attend_forward/pallas_call | solution.py:281
  63.1 9.0 %feed_forward.1 = (bf16[256,512]{1,0:T(8,128)(2,1)}, bf16[288,512]{1,0:T(8,128)(2,1)S(1)}, f32[256,512]{1,0:T(8,128)S(1)}, bf16[256,2048]{1,0:T(8,128)(2,1)S(1)}...) custom-call(s32[11]{0:T(128)S(1)} %copy-done.53, ...), custom_call_target="tpu_custom_call" | custom-call | flops 10 | bytes 10 | tf_op jit(solution)/shard_map/feed_forward/pallas_call | solution.py:397
  74.4 4.1 %attend_query.2.refs_13_ = bf16[256,256]{1,0:T(8,128)(2,1)S(1)} custom-call(s32[11]{0:T(128)S(1)} %copy-done.53, bf16[256,512]{1,0:T(8,128)(2,1)S(1)} %copy-done.14, bf16[1024,512]{1,0:T(8,128)(2,1)S(1)} %copy-done.9, bf16[256,512]{1,0:T(8,128)(2,1)S(1)} %copy-done.19, bf16[1024,512]{1,0:T(8,128)(2,1)S(1)} %copy-done.12, bf16[256,512]{1,0:T(8,128)(2,1)S(1)} %copy-done.20, ...), custom_call_target="tpu_custom_call" | custom-call | flops 5 | bytes 5 | tf_op jit(solution)/shard_map/attend_query/pallas_call | solution.py:525
  78.6 4.2 %ffn_grads.1 = (bf16[2304,512]{1,0:T(8,128)(2,1)S(1)}, bf16[2304,512]{1,0:T(8,128)(2,1)}) custom-call(s32[11]{0:T(128)S(1)} %copy-done.53, bf16[256,512]{1,0:T(8,128)(2,1)S(1)} %get-tuple-element.115.a_ref.a_own.a_other, bf16[256,512]{1,0:T(8,128)(2,1)S(1)} %get-tuple-element.115.a_ref.a_own.a_other, bf16[256,512]{1,0:T(8,128)(2,1)S(1)} %get-tuple-element.126.do_ref, ...), custom_call_target="tpu_custom_call" | custom-call | flops 10 | bytes 10 | tf_op jit(solution)/shard_map/ffn_grads/pallas_call | solution.py:466
  94.1 4.1 %attend_query.3.refs_14_ = bf16[256,256]{1,0:T(8,128)(2,1)S(1)} custom-call(s32[11]{0:T(128)S(1)} %copy-done.53, bf16[256,512]{1,0:T(8,128)(2,1)S(1)} %copy-done.14, bf16[1024,512]{1,0:T(8,128)(2,1)S(1)} %copy-done.10, bf16[256,512]{1,0:T(8,128)(2,1)S(1)} %copy-done.19, bf16[1024,512]{1,0:T(8,128)(2,1)S(1)} %copy-done.13, bf16[256,512]{1,0:T(8,128)(2,1)S(1)} %copy-done.21, ...), custom_call_target="tpu_custom_call" | custom-call | flops 5 | bytes 5 | tf_op jit(solution)/shard_map/attend_query/pallas_call | solution.py:525
  102.2 13.2 %last.1 = (bf16[1408,512]{1,0:T(8,128)(2,1)S(1)}, bf16[1408,512]{1,0:T(8,128)(2,1)}, bf16[256,512]{1,0:T(8,128)(2,1)S(1)}) custom-call(s32[11]{0:T(128)S(1)} %copy-done.53, bf16[256,512]{1,0:T(8,128)(2,1)S(1)} %copy-done.14, bf16[256,512]{1,0:T(8,128)(2,1)S(1)} %collective-permute-done.24.refs_1_, bf16[256,512]{1,0:T(8,128)(2,1)S(1)} %copy-done.35, ...), custom_call_target="tpu_custom_call" | custom-call | flops 15 | bytes 15 | tf_op jit(solution)/shard_map/last/pallas_call | solution.py:639
  116.1 3.6 %collective-permute-done.21.refs_2_.refs_6_.refs_10_.refs_14_ = bf16[576,512]{1,0:T(8,128)(2,1)S(1)} collective-permute-done((bf16[576,512]{1,0:T(8,128)(2,1)S(1)}, bf16[576,512]{1,0:T(8,128)(2,1)S(1)}, u32[]{:S(2)}, u32[]{:S(2)}) %collective-permute-start.21) | collective-permute-done | bytes 589856 | tf_op jit(solution)/shard_map/ppermute | solution.py:823
  133.0 5.7 %collective-permute-done.29.refs_5_.refs_9_.refs_13_.refs_17_ = bf16[352,512]{1,0:T(8,128)(2,1)S(1)} collective-permute-done((bf16[352,512]{1,0:T(8,128)(2,1)S(1)}, bf16[352,512]{1,0:T(8,128)(2,1)S(1)}, u32[]{:S(2)}, u32[]{:S(2)}) %collective-permute-start.29) | collective-permute-done | bytes 360480 | tf_op jit(solution)/shard_map/ppermute | solution.py:823
  139.3 7.0 %all-to-all-start.1 = ((bf16[16,16,512]{2,1,0:T(8,128)(2,1)}), bf16[16,16,512]{2,1,0:T(8,128)(2,1)S(1)}, u32[]{:S(2)}, u32[]{:S(2)}) async-start(bf16[16,16,512]{2,1,0:T(8,128)(2,1)} %bitcast.18), calls=%async_computation.1 | async-start | bytes 524288 | tf_op jit(solution)/shard_map/all_to_all | solution.py:1071
  146.3 4.6 %collective-permute-done.33.refs_3_ = bf16[144,512]{1,0:T(8,128)(2,1)S(1)} collective-permute-done((bf16[144,512]{1,0:T(8,128)(2,1)}, bf16[144,512]{1,0:T(8,128)(2,1)S(1)}, u32[]{:S(2)}, u32[]{:S(2)}) %collective-permute-start.33) | collective-permute-done | bytes 147488 | tf_op jit(solution)/shard_map/ppermute | solution.py:823
  153.7 3.2 %collective-permute-start.40 = (bf16[232,512]{1,0:T(8,128)(2,1)S(1)}, bf16[232,512]{1,0:T(8,128)(2,1)S(1)}, u32[]{:S(2)}, u32[]{:S(2)}) collective-permute-start(bf16[232,512]{1,0:T(8,128)(2,1)S(1)} %get-tuple-element.167), channel_id=1, source_target_pairs={{0,24},{2,26},{4,28},{6,30},{8,16},{10,18},{12,20},{14,22},{16,8},... | collective-permute-start | bytes 712712 | tf_op jit(solution)/shard_map/ppermute | solution.py:823
  157.7 4.9 %collective-permute-done.37 = bf16[128,512]{1,0:T(8,128)(2,1)S(1)} collective-permute-done((bf16[128,512]{1,0:T(8,128)(2,1)S(1)}, bf16[128,512]{1,0:T(8,128)(2,1)S(1)}, u32[]{:S(2)}, u32[]{:S(2)}) %collective-permute-start.37) | collective-permute-done | bytes 131104 | tf_op jit(solution)/shard_map/ppermute | solution.py:1056
  162.6 6.2 %collective-permute-done.39.refs_2_.refs_1_ = bf16[232,512]{1,0:T(8,128)(2,1)S(1)} collective-permute-done((bf16[232,512]{1,0:T(8,128)(2,1)S(1)}, bf16[232,512]{1,0:T(8,128)(2,1)S(1)}, u32[]{:S(2)}, u32[]{:S(2)}) %collective-permute-start.39) | collective-permute-done | bytes 237600 | tf_op jit(solution)/shard_map/ppermute | solution.py:823
  168.9 4.6 %collective-permute-done.40.refs_3_.refs_2_ = bf16[232,512]{1,0:T(8,128)(2,1)S(1)} collective-permute-done((bf16[232,512]{1,0:T(8,128)(2,1)S(1)}, bf16[232,512]{1,0:T(8,128)(2,1)S(1)}, u32[]{:S(2)}, u32[]{:S(2)}) %collective-permute-start.40) | collective-permute-done | bytes 237600 | tf_op jit(solution)/shard_map/ppermute | solution.py:823
  178.0 4.2 %all-to-all-start.2 = ((bf16[4,88,512]{2,1,0:T(8,128)(2,1)}), bf16[4,88,512]{2,1,0:T(8,128)(2,1)S(1)}, u32[]{:S(2)}, u32[]{:S(2)}) async-start(bf16[4,88,512]{2,1,0:T(8,128)(2,1)} %bitcast.27), calls=%async_computation.2 | async-start | bytes 720896 | tf_op jit(solution)/shard_map/all_to_all | solution.py:864
  182.2 6.0 %all-to-all-done.2 = bf16[4,88,512]{2,1,0:T(8,128)(2,1)S(1)} async-done(((bf16[4,88,512]{2,1,0:T(8,128)(2,1)}), bf16[4,88,512]{2,1,0:T(8,128)(2,1)S(1)}, u32[]{:S(2)}, u32[]{:S(2)}) %all-to-all-start.2) | async-done | bytes 360480 | tf_op jit(solution)/shard_map/all_to_all | solution.py:864
  189.9 10.4 %collective-permute-done.42.refs_2_ = bf16[576,512]{1,0:T(8,128)(2,1)S(1)} collective-permute-done((bf16[576,512]{1,0:T(8,128)(2,1)S(1)}, bf16[576,512]{1,0:T(8,128)(2,1)S(1)}, u32[]{:S(2)}, u32[]{:S(2)}) %collective-permute-start.42) | collective-permute-done | bytes 589856 | tf_op jit(solution)/shard_map/ppermute | solution.py:823
  210.6 5.3 %collective-permute-done.45.refs_2_ = bf16[352,512]{1,0:T(8,128)(2,1)S(1)} collective-permute-done((bf16[352,512]{1,0:T(8,128)(2,1)S(1)}, bf16[352,512]{1,0:T(8,128)(2,1)S(1)}, u32[]{:S(2)}, u32[]{:S(2)}) %collective-permute-start.45) | collective-permute-done | bytes 360480 | tf_op jit(solution)/shard_map/ppermute | solution.py:823
  (251 shorter events, 78.8 us)
Async XLA Ops:
  9.8 14.8 %collective-permute-start.4 = (bf16[256,512]{1,0:T(8,128)(2,1)}, bf16[256,512]{1,0:T(8,128)(2,1)S(1)}, u32[]{:S(2)}, u32[]{:S(2)}) collective-permute-start(bf16[256,512]{1,0:T(8,128)(2,1)} %refs_19_.1), channel_id=1, source_target_pairs={{0,1},{1,0},{2,3},{3,2},{4,5},{5,4},{6,7},{7,6},{8,9},{9,8},{10,11... | collective-permute-start | bytes 786440 | tf_op jit(solution)/shard_map/ppermute | solution.py:882
  10.3 14.4 %collective-permute-start.5 = (bf16[256,512]{1,0:T(8,128)(2,1)}, bf16[256,512]{1,0:T(8,128)(2,1)S(1)}, u32[]{:S(2)}, u32[]{:S(2)}) collective-permute-start(bf16[256,512]{1,0:T(8,128)(2,1)} %refs_21_.1), channel_id=1, source_target_pairs={{0,1},{1,0},{2,3},{3,2},{4,5},{5,4},{6,7},{7,6},{8,9},{9,8},{10,11... | collective-permute-start | bytes 786440 | tf_op jit(solution)/shard_map/ppermute | solution.py:882
  24.6 38.4 %collective-permute-start.16 = (bf16[256,2048]{1,0:T(8,128)(2,1)}, bf16[256,2048]{1,0:T(8,128)(2,1)}, u32[]{:S(2)}, u32[]{:S(2)}) collective-permute-start(bf16[256,2048]{1,0:T(8,128)(2,1)} %wu_a.1), channel_id=1, source_target_pairs={{0,1},{1,0},{2,3},{3,2},{4,5},{5,4},{6,7},{7,6},{8,9},{9,8},{10,11... | collective-permute-start | bytes 3145736 | tf_op jit(solution)/shard_map/ppermute | solution.py:882
  24.7 38.3 %collective-permute-start.17 = (bf16[1024,512]{1,0:T(8,128)(2,1)}, bf16[1024,512]{1,0:T(8,128)(2,1)}, u32[]{:S(2)}, u32[]{:S(2)}) collective-permute-start(bf16[1024,512]{1,0:T(8,128)(2,1)} %wd_a.1), channel_id=1, source_target_pairs={{0,1},{1,0},{2,3},{3,2},{4,5},{5,4},{6,7},{7,6},{8,9},{9,8},{10,11... | collective-permute-start | bytes 3145736 | tf_op jit(solution)/shard_map/ppermute | solution.py:882
  33.2 18.3 %all-to-all-start = ((bf16[16,16,512]{2,1,0:T(8,128)(2,1)}), bf16[16,16,512]{2,1,0:T(8,128)(2,1)S(1)}, u32[]{:S(2)}, u32[]{:S(2)}) async-start(bf16[16,16,512]{2,1,0:T(8,128)(2,1)} %bitcast.16), calls=%async_computation | async-start | bytes 524288 | tf_op jit(solution)/shard_map/all_to_all | solution.py:993
  38.7 24.4 %collective-permute-start.15 = (bf16[256,512]{1,0:T(8,128)(2,1)S(1)}, bf16[256,512]{1,0:T(8,128)(2,1)S(1)}, u32[]{:S(2)}, u32[]{:S(2)}) collective-permute-start(bf16[256,512]{1,0:T(8,128)(2,1)S(1)} %copy-done.47), channel_id=1, source_target_pairs={{0,1},{1,0},{2,3},{3,2},{4,5},{5,4},{6,7},{7,6},{8,9},{9,8},{10,11... | collective-permute-start | bytes 786440 | tf_op jit(solution)/shard_map/ppermute | solution.py:882
  47.4 24.7 %collective-permute-start.13 = (bf16[256,512]{1,0:T(8,128)(2,1)S(1)}, bf16[256,512]{1,0:T(8,128)(2,1)S(1)}, u32[]{:S(2)}, u32[]{:S(2)}) collective-permute-start(bf16[256,512]{1,0:T(8,128)(2,1)S(1)} %copy-done.14), channel_id=1, source_target_pairs={{8,0},{10,2},{12,4},{14,6},{16,8},{18,10},{20,12},{22,14},{24,16},... | collective-permute-start | bytes 786440 | tf_op jit(solution)/shard_map/ppermute | solution.py:901
  50.0 22.1 %collective-permute-start.14 = (bf16[256,512]{1,0:T(8,128)(2,1)S(1)}, bf16[256,512]{1,0:T(8,128)(2,1)S(1)}, u32[]{:S(2)}, u32[]{:S(2)}) collective-permute-start(bf16[256,512]{1,0:T(8,128)(2,1)S(1)} %copy-done.14), channel_id=1, source_target_pairs={{16,0},{18,2},{20,4},{22,6},{24,8},{26,10},{28,12},{30,14},{17,1},... | collective-permute-start | bytes 786440 | tf_op jit(solution)/shard_map/ppermute | solution.py:901
  83.3 15.0 %collective-permute-start.23 = (bf16[288,512]{1,0:T(8,128)(2,1)}, bf16[288,512]{1,0:T(8,128)(2,1)}, u32[]{:S(2)}, u32[]{:S(2)}) collective-permute-start(bf16[288,512]{1,0:T(8,128)(2,1)} %collective-permute-done.18.refs_7_), channel_id=1, source_target_pairs={{8,0},{10,2},{12,4},{14,6},{16,8},{18,10},{20,12},{22,14},{24,16},... | collective-permute-start | bytes 884744 | tf_op jit(solution)/shard_map/ppermute | solution.py:891
  90.5 25.6 %collective-permute-start.20 = (bf16[576,512]{1,0:T(8,128)(2,1)S(1)}, bf16[576,512]{1,0:T(8,128)(2,1)S(1)}, u32[]{:S(2)}, u32[]{:S(2)}) collective-permute-start(bf16[576,512]{1,0:T(8,128)(2,1)S(1)} %get-tuple-element.135), channel_id=1, source_target_pairs={{0,2},{2,0},{4,6},{6,4},{8,10},{10,8},{12,14},{14,12},{16,18},{18,... | collective-permute-start | bytes 1769480 | tf_op jit(solution)/shard_map/ppermute | solution.py:823
  92.0 27.7 %collective-permute-start.21 = (bf16[576,512]{1,0:T(8,128)(2,1)S(1)}, bf16[576,512]{1,0:T(8,128)(2,1)S(1)}, u32[]{:S(2)}, u32[]{:S(2)}) collective-permute-start(bf16[576,512]{1,0:T(8,128)(2,1)S(1)} %get-tuple-element.136), channel_id=1, source_target_pairs={{0,4},{2,6},{4,0},{6,2},{8,12},{10,14},{12,8},{14,10},{16,20},{18,... | collective-permute-start | bytes 1769480 | tf_op jit(solution)/shard_map/ppermute | solution.py:823
  93.5 27.1 %collective-permute-start.22 = (bf16[576,512]{1,0:T(8,128)(2,1)S(1)}, bf16[576,512]{1,0:T(8,128)(2,1)S(1)}, u32[]{:S(2)}, u32[]{:S(2)}) collective-permute-start(bf16[576,512]{1,0:T(8,128)(2,1)S(1)} %get-tuple-element.137), channel_id=1, source_target_pairs={{0,6},{2,4},{4,2},{6,0},{8,14},{10,12},{12,10},{14,8},{16,22},{18,... | collective-permute-start | bytes 1769480 | tf_op jit(solution)/shard_map/ppermute | solution.py:823
  127.9 23.1 %collective-permute-start.34 = (bf16[352,512]{1,0:T(8,128)(2,1)}, bf16[352,512]{1,0:T(8,128)(2,1)S(1)}, u32[]{:S(2)}, u32[]{:S(2)}) collective-permute-start(bf16[352,512]{1,0:T(8,128)(2,1)} %get-tuple-element.160), channel_id=1, source_target_pairs={{0,4},{2,6},{4,0},{6,2},{8,12},{10,14},{12,8},{14,10},{16,20},{18,... | collective-permute-start | bytes 1081352 | tf_op jit(solution)/shard_map/ppermute | solution.py:823
  129.6 21.4 %collective-permute-start.35 = (bf16[352,512]{1,0:T(8,128)(2,1)S(1)}, bf16[352,512]{1,0:T(8,128)(2,1)S(1)}, u32[]{:S(2)}, u32[]{:S(2)}) collective-permute-start(bf16[352,512]{1,0:T(8,128)(2,1)S(1)} %get-tuple-element.161), channel_id=1, source_target_pairs={{0,6},{2,4},{4,2},{6,0},{8,14},{10,12},{12,10},{14,8},{16,22},{18,... | collective-permute-start | bytes 1081352 | tf_op jit(solution)/shard_map/ppermute | solution.py:823
  131.0 15.3 %collective-permute-start.31 = (bf16[144,512]{1,0:T(8,128)(2,1)}, bf16[144,512]{1,0:T(8,128)(2,1)S(1)}, u32[]{:S(2)}, u32[]{:S(2)}) collective-permute-start(bf16[144,512]{1,0:T(8,128)(2,1)} %get-tuple-element.139), channel_id=1, source_target_pairs={{0,8},{2,10},{4,12},{6,14},{8,0},{10,2},{12,4},{14,6},{16,24},{18,... | collective-permute-start | bytes 442376 | tf_op jit(solution)/shard_map/ppermute | solution.py:823
  132.9 13.5 %collective-permute-start.32 = (bf16[144,512]{1,0:T(8,128)(2,1)}, bf16[144,512]{1,0:T(8,128)(2,1)S(1)}, u32[]{:S(2)}, u32[]{:S(2)}) collective-permute-start(bf16[144,512]{1,0:T(8,128)(2,1)} %get-tuple-element.140), channel_id=1, source_target_pairs={{0,16},{2,18},{4,20},{6,22},{8,24},{10,26},{12,28},{14,30},{16,0},... | collective-permute-start | bytes 442376 | tf_op jit(solution)/shard_map/ppermute | solution.py:823
  139.3 38.7 %all-to-all-start.1 = ((bf16[16,16,512]{2,1,0:T(8,128)(2,1)}), bf16[16,16,512]{2,1,0:T(8,128)(2,1)S(1)}, u32[]{:S(2)}, u32[]{:S(2)}) async-start(bf16[16,16,512]{2,1,0:T(8,128)(2,1)} %bitcast.18), calls=%async_computation.1 | async-start | bytes 524288 | tf_op jit(solution)/shard_map/all_to_all | solution.py:1071
  153.4 15.4 %collective-permute-start.39 = (bf16[232,512]{1,0:T(8,128)(2,1)S(1)}, bf16[232,512]{1,0:T(8,128)(2,1)S(1)}, u32[]{:S(2)}, u32[]{:S(2)}) collective-permute-start(bf16[232,512]{1,0:T(8,128)(2,1)S(1)} %get-tuple-element.166), channel_id=1, source_target_pairs={{0,16},{2,18},{4,20},{6,22},{8,24},{10,26},{12,28},{14,30},{16,0},... | collective-permute-start | bytes 712712 | tf_op jit(solution)/shard_map/ppermute | solution.py:823
  153.7 19.8 %collective-permute-start.40 = (bf16[232,512]{1,0:T(8,128)(2,1)S(1)}, bf16[232,512]{1,0:T(8,128)(2,1)S(1)}, u32[]{:S(2)}, u32[]{:S(2)}) collective-permute-start(bf16[232,512]{1,0:T(8,128)(2,1)S(1)} %get-tuple-element.167), channel_id=1, source_target_pairs={{0,24},{2,26},{4,28},{6,30},{8,16},{10,18},{12,20},{14,22},{16,8},... | collective-permute-start | bytes 712712 | tf_op jit(solution)/shard_map/ppermute | solution.py:823
  173.6 16.3 %collective-permute-start.41 = (bf16[576,512]{1,0:T(8,128)(2,1)S(1)}, bf16[576,512]{1,0:T(8,128)(2,1)S(1)}, u32[]{:S(2)}, u32[]{:S(2)}) collective-permute-start(bf16[576,512]{1,0:T(8,128)(2,1)S(1)} %place.3.refs_0_), channel_id=1, source_target_pairs={{0,2},{2,0},{4,6},{6,4},{8,10},{10,8},{12,14},{14,12},{16,18},{18,... | collective-permute-start | bytes 1769480 | tf_op jit(solution)/shard_map/ppermute | solution.py:823
  174.4 26.0 %collective-permute-start.42 = (bf16[576,512]{1,0:T(8,128)(2,1)S(1)}, bf16[576,512]{1,0:T(8,128)(2,1)S(1)}, u32[]{:S(2)}, u32[]{:S(2)}) collective-permute-start(bf16[576,512]{1,0:T(8,128)(2,1)S(1)} %place.3.refs_0_), channel_id=1, source_target_pairs={{0,4},{2,6},{4,0},{6,2},{8,12},{10,14},{12,8},{14,10},{16,20},{18,... | collective-permute-start | bytes 1769480 | tf_op jit(solution)/shard_map/ppermute | solution.py:823
  175.9 24.5 %collective-permute-start.43 = (bf16[576,512]{1,0:T(8,128)(2,1)S(1)}, bf16[576,512]{1,0:T(8,128)(2,1)S(1)}, u32[]{:S(2)}, u32[]{:S(2)}) collective-permute-start(bf16[576,512]{1,0:T(8,128)(2,1)S(1)} %place.3.refs_0_), channel_id=1, source_target_pairs={{0,6},{2,4},{4,2},{6,0},{8,14},{10,12},{12,10},{14,8},{16,22},{18,... | collective-permute-start | bytes 1769480 | tf_op jit(solution)/shard_map/ppermute | solution.py:823
  201.1 14.7 %collective-permute-start.45 = (bf16[352,512]{1,0:T(8,128)(2,1)S(1)}, bf16[352,512]{1,0:T(8,128)(2,1)S(1)}, u32[]{:S(2)}, u32[]{:S(2)}) collective-permute-start(bf16[352,512]{1,0:T(8,128)(2,1)S(1)} %bitcast.59), channel_id=1, source_target_pairs={{0,4},{2,6},{4,0},{6,2},{8,12},{10,14},{12,8},{14,10},{16,20},{18,... | collective-permute-start | bytes 1081352 | tf_op jit(solution)/shard_map/ppermute | solution.py:823
  202.1 13.8 %collective-permute-start.46 = (bf16[352,512]{1,0:T(8,128)(2,1)S(1)}, bf16[352,512]{1,0:T(8,128)(2,1)S(1)}, u32[]{:S(2)}, u32[]{:S(2)}) collective-permute-start(bf16[352,512]{1,0:T(8,128)(2,1)S(1)} %bitcast.60), channel_id=1, source_target_pairs={{0,6},{2,4},{4,2},{6,0},{8,14},{10,12},{12,10},{14,8},{16,22},{18,... | collective-permute-start | bytes 1081352 | tf_op jit(solution)/shard_map/ppermute | solution.py:823
  (88 other events, 603.7 us)

commit v6 on v5

--- a/solution.py
+++ b/solution.py
@@ -1065,7 +1065,7 @@
         held = one.place(one.gather(held, level), level)
         held_last = two.place(two.gather(held_last, level), level)
     parts = one.gather(held, 0)
-    held_last = after(parts[1:], held_last)
+    held_last = after(parts[1], held_last)
     parts_last = two.gather(held_last, 0)
     held = one.place(parts, 0)
     landed = lax.all_to_all(leaving, "ctx", split_axis=0, concat_axis=0, tiled=True)

time: 223 us -> 222 us (level)
    unnamed x125 -> x127, local copies, waits for them, and re-layouts: 14.8 us -> 14.9 us
  transfers between devices with their start and end apart: 50 -> 50, of which waited for: 18 -> 18; matrix products, arithmetic and copies ran while one was open for 4% -> 5% of each run, Pallas kernels for 28% -> 28%
where the time goes in v6:
time: 222 us; the launch traced here: 219 us
  Pallas kernels  65.5 us (30%)
  waiting for transfers between devices  64.3 us (29%)
  starting transfers between devices  61.1 us (28%)
  local copies, waits for them, and re-layouts  16.9 us (8%)
  other arithmetic  8.95 us (4%)
    ppermute x18, waiting for transfers between devices, exchange(): lax.ppermute(piece, 'ctx', [(i, i ^ (k + 1) * stride) for i in range(rank...  43.8 us
    ppermute x18, starting transfers between devices, exchange(): lax.ppermute(piece, 'ctx', [(i, i ^ (k + 1) * stride) for i in range(rank...  20.2 us
    unnamed x127, local copies, waits for them, and re-layouts  14.9 us
    pallas_call x1, Pallas kernels, last(): pl.pallas_call(functools.partial(last_kernel, reach=count // 2, quarter=q...  13.2 us
    pallas_call x2, Pallas kernels, project(): pl.pallas_call(functools.partial(project_kernel, blocks=blocks, offset=of...  11.4 us
    ppermute x4, starting transfers between devices, next_chip(): lax.ppermute(block, 'ctx', pairs if step > 0 else [(b, a) for a, b in pai...  11.4 us
    pallas_call x1, Pallas kernels, attend_forward(): pl.pallas_call(forward_kernel, grid_spec=pltpu.PrefetchScalarGridSpec(num...  9.03 us
    pallas_call x1, Pallas kernels, feed_forward(): pl.pallas_call(ffn_kernel, grid_spec=pltpu.PrefetchScalarGridSpec(num_sca...  9.01 us
  transfers between devices with their start and end apart: 50, of which 18 were waited for; matrix products, arithmetic and copies ran while one was open for 5% of the time, Pallas kernels for 28%

profile of v6, /device:TPU:16, one launch (start us, length us, event | category | flops | bytes accessed | tf_op | source)
XLA Modules:
  0.0 218.7 jit_solution(10310965979565717521)
XLA Ops:
  10.4 3.5 %collective-permute-start.8 = (bf16[256,512]{1,0:T(8,128)(2,1)S(1)}, bf16[256,512]{1,0:T(8,128)(2,1)S(1)}, u32[]{:S(2)}, u32[]{:S(2)}) collective-permute-start(bf16[256,512]{1,0:T(8,128)(2,1)S(1)} %pad_maximum_fusion.refs_0_), channel_id=1, source_target_pairs={{0,8},{2,10},{4,12},{6,14},{8,16},{10,18},{12,20},{14,22},{16,24},... | collective-permute-start | bytes 786440 | tf_op jit(solution)/shard_map/ppermute | solution.py:891
  16.3 4.7 %collective-permute-done.8.refs_2_ = bf16[256,512]{1,0:T(8,128)(2,1)S(1)} collective-permute-done((bf16[256,512]{1,0:T(8,128)(2,1)S(1)}, bf16[256,512]{1,0:T(8,128)(2,1)S(1)}, u32[]{:S(2)}, u32[]{:S(2)}) %collective-permute-start.8) | collective-permute-done | bytes 262176 | tf_op jit(solution)/shard_map/ppermute | solution.py:891
  21.0 3.5 %collective-permute-start.9 = (bf16[256,512]{1,0:T(8,128)(2,1)S(1)}, bf16[256,512]{1,0:T(8,128)(2,1)S(1)}, u32[]{:S(2)}, u32[]{:S(2)}) collective-permute-start(bf16[256,512]{1,0:T(8,128)(2,1)S(1)} %collective-permute-done.8.refs_2_), channel_id=1, source_target_pairs={{0,8},{2,10},{4,12},{6,14},{8,16},{10,18},{12,20},{14,22},{16,24},... | collective-permute-start | bytes 786440 | tf_op jit(solution)/shard_map/ppermute | solution.py:891
  27.5 4.2 %project.2 = (bf16[256,512]{1,0:T(8,128)(2,1)}, bf16[256,512]{1,0:T(8,128)(2,1)}, bf16[256,512]{1,0:T(8,128)(2,1)}, f32[256,512]{1,0:T(8,128)}, bf16[256,512]{1,0:T(8,128)(2,1)}) custom-call(s32[11]{0:T(128)} %pad_add_fusion.1.info, bf16[256,512]{1,0:T(8,128)(2,1)} %copy-done.58, bf16[512,512]{1,0:T(8,128)(2,1)} %refs_4_.1, bf16[512,512]{1,0:T(8,128)(2,1)} %copy-done.55, ...), custom_call_target="tpu_custom_call" | custom-call | flops 4 | bytes 4 | tf_op jit(solution)/shard_map/project/pallas_call | solution.py:159
  33.2 5.5 %all-to-all-start = ((bf16[16,16,512]{2,1,0:T(8,128)(2,1)}), bf16[16,16,512]{2,1,0:T(8,128)(2,1)S(1)}, u32[]{:S(2)}, u32[]{:S(2)}) async-start(bf16[16,16,512]{2,1,0:T(8,128)(2,1)} %bitcast.16), calls=%async_computation | async-start | bytes 524288 | tf_op jit(solution)/shard_map/all_to_all | solution.py:993
  40.2 7.2 %project.3 = (bf16[1024,512]{1,0:T(8,128)(2,1)}, bf16[1024,512]{1,0:T(8,128)(2,1)}) custom-call(s32[11]{0:T(128)} %pad_add_fusion.1.info, bf16[256,512]{1,0:T(8,128)(2,1)} %copy-done.57, bf16[256,512]{1,0:T(8,128)(2,1)} %copy-done.60, bf16[256,512]{1,0:T(8,128)(2,1)} %copy-done.56, bf16[256,512]{1,0:T(8,128)(2,1)} %copy-done.61, bf16[512,512]{1,0:T(8,128)(2,1)} %refs_4_.1, ...), custom_call_target="tpu_custom_call" | custom-call | flops 10 | bytes 10 | tf_op jit(solution)/shard_map/project/pallas_call | solution.py:159
  54.0 9.0 %attend_forward.1 = (bf16[256,512]{1,0:T(8,128)(2,1)S(1)}, f32[256,512]{1,0:T(8,128)S(1)}, f32[256,512]{1,0:T(8,128)S(1)}, bf16[16,512]{1,0:T(8,128)(2,1)S(1)}) custom-call(s32[11]{0:T(128)S(1)} %copy-done.53, bf16[256,512]{1,0:T(8,128)(2,1)S(1)} %copy-done.14, bf16[1024,512]{1,0:T(8,128)(2,1)S(1)} %copy-done.8, bf16[256,512]{1,0:T(8,128)(2,1)S(1)} %copy-done.19, ...), custom_call_target="tpu_custom_call" | custom-call | flops 12 | bytes 12 | tf_op jit(solution)/shard_map/attend_forward/pallas_call | solution.py:281
  63.1 9.0 %feed_forward.1 = (bf16[256,512]{1,0:T(8,128)(2,1)}, bf16[288,512]{1,0:T(8,128)(2,1)S(1)}, f32[256,512]{1,0:T(8,128)S(1)}, bf16[256,2048]{1,0:T(8,128)(2,1)S(1)}...) custom-call(s32[11]{0:T(128)S(1)} %copy-done.53, ...), custom_call_target="tpu_custom_call" | custom-call | flops 10 | bytes 10 | tf_op jit(solution)/shard_map/feed_forward/pallas_call | solution.py:397
  74.4 4.1 %attend_query.2.refs_13_ = bf16[256,256]{1,0:T(8,128)(2,1)S(1)} custom-call(s32[11]{0:T(128)S(1)} %copy-done.53, bf16[256,512]{1,0:T(8,128)(2,1)S(1)} %copy-done.14, bf16[1024,512]{1,0:T(8,128)(2,1)S(1)} %copy-done.9, bf16[256,512]{1,0:T(8,128)(2,1)S(1)} %copy-done.19, bf16[1024,512]{1,0:T(8,128)(2,1)S(1)} %copy-done.12, bf16[256,512]{1,0:T(8,128)(2,1)S(1)} %copy-done.20, ...), custom_call_target="tpu_custom_call" | custom-call | flops 5 | bytes 5 | tf_op jit(solution)/shard_map/attend_query/pallas_call | solution.py:525
  78.6 4.2 %ffn_grads.1 = (bf16[2304,512]{1,0:T(8,128)(2,1)S(1)}, bf16[2304,512]{1,0:T(8,128)(2,1)}) custom-call(s32[11]{0:T(128)S(1)} %copy-done.53, bf16[256,512]{1,0:T(8,128)(2,1)S(1)} %get-tuple-element.115.a_ref.a_own.a_other, bf16[256,512]{1,0:T(8,128)(2,1)S(1)} %get-tuple-element.115.a_ref.a_own.a_other, bf16[256,512]{1,0:T(8,128)(2,1)S(1)} %get-tuple-element.126.do_ref, ...), custom_call_target="tpu_custom_call" | custom-call | flops 10 | bytes 10 | tf_op jit(solution)/shard_map/ffn_grads/pallas_call | solution.py:466
  94.1 4.1 %attend_query.3.refs_14_ = bf16[256,256]{1,0:T(8,128)(2,1)S(1)} custom-call(s32[11]{0:T(128)S(1)} %copy-done.53, bf16[256,512]{1,0:T(8,128)(2,1)S(1)} %copy-done.14, bf16[1024,512]{1,0:T(8,128)(2,1)S(1)} %copy-done.10, bf16[256,512]{1,0:T(8,128)(2,1)S(1)} %copy-done.19, bf16[1024,512]{1,0:T(8,128)(2,1)S(1)} %copy-done.13, bf16[256,512]{1,0:T(8,128)(2,1)S(1)} %copy-done.21, ...), custom_call_target="tpu_custom_call" | custom-call | flops 5 | bytes 5 | tf_op jit(solution)/shard_map/attend_query/pallas_call | solution.py:525
  102.3 13.2 %last.1 = (bf16[1408,512]{1,0:T(8,128)(2,1)S(1)}, bf16[1408,512]{1,0:T(8,128)(2,1)}, bf16[256,512]{1,0:T(8,128)(2,1)S(1)}) custom-call(s32[11]{0:T(128)S(1)} %copy-done.53, bf16[256,512]{1,0:T(8,128)(2,1)S(1)} %copy-done.14, bf16[256,512]{1,0:T(8,128)(2,1)S(1)} %collective-permute-done.24.refs_1_, bf16[256,512]{1,0:T(8,128)(2,1)S(1)} %copy-done.35, ...), custom_call_target="tpu_custom_call" | custom-call | flops 15 | bytes 15 | tf_op jit(solution)/shard_map/last/pallas_call | solution.py:639
  116.1 3.6 %collective-permute-done.21.refs_2_.refs_6_.refs_10_.refs_14_ = bf16[576,512]{1,0:T(8,128)(2,1)S(1)} collective-permute-done((bf16[576,512]{1,0:T(8,128)(2,1)S(1)}, bf16[576,512]{1,0:T(8,128)(2,1)S(1)}, u32[]{:S(2)}, u32[]{:S(2)}) %collective-permute-start.21) | collective-permute-done | bytes 589856 | tf_op jit(solution)/shard_map/ppermute | solution.py:823
  133.1 5.7 %collective-permute-done.29.refs_5_.refs_9_.refs_13_.refs_17_ = bf16[352,512]{1,0:T(8,128)(2,1)S(1)} collective-permute-done((bf16[352,512]{1,0:T(8,128)(2,1)S(1)}, bf16[352,512]{1,0:T(8,128)(2,1)S(1)}, u32[]{:S(2)}, u32[]{:S(2)}) %collective-permute-start.29) | collective-permute-done | bytes 360480 | tf_op jit(solution)/shard_map/ppermute | solution.py:823
  139.3 7.1 %all-to-all-start.1 = ((bf16[16,16,512]{2,1,0:T(8,128)(2,1)}), bf16[16,16,512]{2,1,0:T(8,128)(2,1)S(1)}, u32[]{:S(2)}, u32[]{:S(2)}) async-start(bf16[16,16,512]{2,1,0:T(8,128)(2,1)} %bitcast.18), calls=%async_computation.1 | async-start | bytes 524288 | tf_op jit(solution)/shard_map/all_to_all | solution.py:1071
  146.4 4.6 %collective-permute-done.33.refs_3_ = bf16[144,512]{1,0:T(8,128)(2,1)S(1)} collective-permute-done((bf16[144,512]{1,0:T(8,128)(2,1)}, bf16[144,512]{1,0:T(8,128)(2,1)S(1)}, u32[]{:S(2)}, u32[]{:S(2)}) %collective-permute-start.33) | collective-permute-done | bytes 147488 | tf_op jit(solution)/shard_map/ppermute | solution.py:823
  157.7 4.9 %collective-permute-done.37 = bf16[128,512]{1,0:T(8,128)(2,1)S(1)} collective-permute-done((bf16[128,512]{1,0:T(8,128)(2,1)S(1)}, bf16[128,512]{1,0:T(8,128)(2,1)S(1)}, u32[]{:S(2)}, u32[]{:S(2)}) %collective-permute-start.37) | collective-permute-done | bytes 131104 | tf_op jit(solution)/shard_map/ppermute | solution.py:1056
  162.7 6.2 %collective-permute-done.39.refs_2_.refs_1_ = bf16[232,512]{1,0:T(8,128)(2,1)S(1)} collective-permute-done((bf16[232,512]{1,0:T(8,128)(2,1)S(1)}, bf16[232,512]{1,0:T(8,128)(2,1)S(1)}, u32[]{:S(2)}, u32[]{:S(2)}) %collective-permute-start.39) | collective-permute-done | bytes 237600 | tf_op jit(solution)/shard_map/ppermute | solution.py:823
  168.9 4.6 %collective-permute-done.40.refs_3_.refs_2_ = bf16[232,512]{1,0:T(8,128)(2,1)S(1)} collective-permute-done((bf16[232,512]{1,0:T(8,128)(2,1)S(1)}, bf16[232,512]{1,0:T(8,128)(2,1)S(1)}, u32[]{:S(2)}, u32[]{:S(2)}) %collective-permute-start.40) | collective-permute-done | bytes 237600 | tf_op jit(solution)/shard_map/ppermute | solution.py:823
  178.0 4.2 %all-to-all-start.2 = ((bf16[4,88,512]{2,1,0:T(8,128)(2,1)}), bf16[4,88,512]{2,1,0:T(8,128)(2,1)S(1)}, u32[]{:S(2)}, u32[]{:S(2)}) async-start(bf16[4,88,512]{2,1,0:T(8,128)(2,1)} %bitcast.27), calls=%async_computation.2 | async-start | bytes 720896 | tf_op jit(solution)/shard_map/all_to_all | solution.py:864
  182.3 5.9 %all-to-all-done.2 = bf16[4,88,512]{2,1,0:T(8,128)(2,1)S(1)} async-done(((bf16[4,88,512]{2,1,0:T(8,128)(2,1)}), bf16[4,88,512]{2,1,0:T(8,128)(2,1)S(1)}, u32[]{:S(2)}, u32[]{:S(2)}) %all-to-all-start.2) | async-done | bytes 360480 | tf_op jit(solution)/shard_map/all_to_all | solution.py:864
  198.6 5.0 %collective-permute-done.46.refs_3_ = bf16[576,512]{1,0:T(8,128)(2,1)S(1)} collective-permute-done((bf16[576,512]{1,0:T(8,128)(2,1)S(1)}, bf16[576,512]{1,0:T(8,128)(2,1)S(1)}, u32[]{:S(2)}, u32[]{:S(2)}) %collective-permute-start.46) | collective-permute-done | bytes 589856 | tf_op jit(solution)/shard_map/ppermute | solution.py:823
  206.2 4.2 %collective-permute-done.42.refs_1_ = bf16[352,512]{1,0:T(8,128)(2,1)S(1)} collective-permute-done((bf16[352,512]{1,0:T(8,128)(2,1)S(1)}, bf16[352,512]{1,0:T(8,128)(2,1)S(1)}, u32[]{:S(2)}, u32[]{:S(2)}) %collective-permute-start.42) | collective-permute-done | bytes 360480 | tf_op jit(solution)/shard_map/ppermute | solution.py:823
  210.4 5.4 %collective-permute-done.43.refs_2_ = bf16[352,512]{1,0:T(8,128)(2,1)S(1)} collective-permute-done((bf16[352,512]{1,0:T(8,128)(2,1)S(1)}, bf16[352,512]{1,0:T(8,128)(2,1)S(1)}, u32[]{:S(2)}, u32[]{:S(2)}) %collective-permute-start.43) | collective-permute-done | bytes 360480 | tf_op jit(solution)/shard_map/ppermute | solution.py:823
  (253 shorter events, 83.1 us)
Async XLA Ops:
  9.8 14.8 %collective-permute-start.4 = (bf16[256,512]{1,0:T(8,128)(2,1)}, bf16[256,512]{1,0:T(8,128)(2,1)S(1)}, u32[]{:S(2)}, u32[]{:S(2)}) collective-permute-start(bf16[256,512]{1,0:T(8,128)(2,1)} %refs_19_.1), channel_id=1, source_target_pairs={{0,1},{1,0},{2,3},{3,2},{4,5},{5,4},{6,7},{7,6},{8,9},{9,8},{10,11... | collective-permute-start | bytes 786440 | tf_op jit(solution)/shard_map/ppermute | solution.py:882
  10.3 14.4 %collective-permute-start.5 = (bf16[256,512]{1,0:T(8,128)(2,1)}, bf16[256,512]{1,0:T(8,128)(2,1)S(1)}, u32[]{:S(2)}, u32[]{:S(2)}) collective-permute-start(bf16[256,512]{1,0:T(8,128)(2,1)} %refs_21_.1), channel_id=1, source_target_pairs={{0,1},{1,0},{2,3},{3,2},{4,5},{5,4},{6,7},{7,6},{8,9},{9,8},{10,11... | collective-permute-start | bytes 786440 | tf_op jit(solution)/shard_map/ppermute | solution.py:882
  24.6 38.4 %collective-permute-start.16 = (bf16[256,2048]{1,0:T(8,128)(2,1)}, bf16[256,2048]{1,0:T(8,128)(2,1)}, u32[]{:S(2)}, u32[]{:S(2)}) collective-permute-start(bf16[256,2048]{1,0:T(8,128)(2,1)} %wu_a.1), channel_id=1, source_target_pairs={{0,1},{1,0},{2,3},{3,2},{4,5},{5,4},{6,7},{7,6},{8,9},{9,8},{10,11... | collective-permute-start | bytes 3145736 | tf_op jit(solution)/shard_map/ppermute | solution.py:882
  24.7 38.3 %collective-permute-start.17 = (bf16[1024,512]{1,0:T(8,128)(2,1)}, bf16[1024,512]{1,0:T(8,128)(2,1)}, u32[]{:S(2)}, u32[]{:S(2)}) collective-permute-start(bf16[1024,512]{1,0:T(8,128)(2,1)} %wd_a.1), channel_id=1, source_target_pairs={{0,1},{1,0},{2,3},{3,2},{4,5},{5,4},{6,7},{7,6},{8,9},{9,8},{10,11... | collective-permute-start | bytes 3145736 | tf_op jit(solution)/shard_map/ppermute | solution.py:882
  33.2 18.3 %all-to-all-start = ((bf16[16,16,512]{2,1,0:T(8,128)(2,1)}), bf16[16,16,512]{2,1,0:T(8,128)(2,1)S(1)}, u32[]{:S(2)}, u32[]{:S(2)}) async-start(bf16[16,16,512]{2,1,0:T(8,128)(2,1)} %bitcast.16), calls=%async_computation | async-start | bytes 524288 | tf_op jit(solution)/shard_map/all_to_all | solution.py:993
  38.7 24.4 %collective-permute-start.15 = (bf16[256,512]{1,0:T(8,128)(2,1)S(1)}, bf16[256,512]{1,0:T(8,128)(2,1)S(1)}, u32[]{:S(2)}, u32[]{:S(2)}) collective-permute-start(bf16[256,512]{1,0:T(8,128)(2,1)S(1)} %copy-done.47), channel_id=1, source_target_pairs={{0,1},{1,0},{2,3},{3,2},{4,5},{5,4},{6,7},{7,6},{8,9},{9,8},{10,11... | collective-permute-start | bytes 786440 | tf_op jit(solution)/shard_map/ppermute | solution.py:882
  47.4 24.7 %collective-permute-start.13 = (bf16[256,512]{1,0:T(8,128)(2,1)S(1)}, bf16[256,512]{1,0:T(8,128)(2,1)S(1)}, u32[]{:S(2)}, u32[]{:S(2)}) collective-permute-start(bf16[256,512]{1,0:T(8,128)(2,1)S(1)} %copy-done.14), channel_id=1, source_target_pairs={{8,0},{10,2},{12,4},{14,6},{16,8},{18,10},{20,12},{22,14},{24,16},... | collective-permute-start | bytes 786440 | tf_op jit(solution)/shard_map/ppermute | solution.py:901
  50.0 22.1 %collective-permute-start.14 = (bf16[256,512]{1,0:T(8,128)(2,1)S(1)}, bf16[256,512]{1,0:T(8,128)(2,1)S(1)}, u32[]{:S(2)}, u32[]{:S(2)}) collective-permute-start(bf16[256,512]{1,0:T(8,128)(2,1)S(1)} %copy-done.14), channel_id=1, source_target_pairs={{16,0},{18,2},{20,4},{22,6},{24,8},{26,10},{28,12},{30,14},{17,1},... | collective-permute-start | bytes 786440 | tf_op jit(solution)/shard_map/ppermute | solution.py:901
  83.3 15.0 %collective-permute-start.23 = (bf16[288,512]{1,0:T(8,128)(2,1)}, bf16[288,512]{1,0:T(8,128)(2,1)}, u32[]{:S(2)}, u32[]{:S(2)}) collective-permute-start(bf16[288,512]{1,0:T(8,128)(2,1)} %collective-permute-done.18.refs_7_), channel_id=1, source_target_pairs={{8,0},{10,2},{12,4},{14,6},{16,8},{18,10},{20,12},{22,14},{24,16},... | collective-permute-start | bytes 884744 | tf_op jit(solution)/shard_map/ppermute | solution.py:891
  90.5 25.6 %collective-permute-start.20 = (bf16[576,512]{1,0:T(8,128)(2,1)S(1)}, bf16[576,512]{1,0:T(8,128)(2,1)S(1)}, u32[]{:S(2)}, u32[]{:S(2)}) collective-permute-start(bf16[576,512]{1,0:T(8,128)(2,1)S(1)} %get-tuple-element.135), channel_id=1, source_target_pairs={{0,2},{2,0},{4,6},{6,4},{8,10},{10,8},{12,14},{14,12},{16,18},{18,... | collective-permute-start | bytes 1769480 | tf_op jit(solution)/shard_map/ppermute | solution.py:823
  92.0 27.7 %collective-permute-start.21 = (bf16[576,512]{1,0:T(8,128)(2,1)S(1)}, bf16[576,512]{1,0:T(8,128)(2,1)S(1)}, u32[]{:S(2)}, u32[]{:S(2)}) collective-permute-start(bf16[576,512]{1,0:T(8,128)(2,1)S(1)} %get-tuple-element.136), channel_id=1, source_target_pairs={{0,4},{2,6},{4,0},{6,2},{8,12},{10,14},{12,8},{14,10},{16,20},{18,... | collective-permute-start | bytes 1769480 | tf_op jit(solution)/shard_map/ppermute | solution.py:823
  93.5 27.1 %collective-permute-start.22 = (bf16[576,512]{1,0:T(8,128)(2,1)S(1)}, bf16[576,512]{1,0:T(8,128)(2,1)S(1)}, u32[]{:S(2)}, u32[]{:S(2)}) collective-permute-start(bf16[576,512]{1,0:T(8,128)(2,1)S(1)} %get-tuple-element.137), channel_id=1, source_target_pairs={{0,6},{2,4},{4,2},{6,0},{8,14},{10,12},{12,10},{14,8},{16,22},{18,... | collective-permute-start | bytes 1769480 | tf_op jit(solution)/shard_map/ppermute | solution.py:823
  127.9 23.1 %collective-permute-start.34 = (bf16[352,512]{1,0:T(8,128)(2,1)}, bf16[352,512]{1,0:T(8,128)(2,1)S(1)}, u32[]{:S(2)}, u32[]{:S(2)}) collective-permute-start(bf16[352,512]{1,0:T(8,128)(2,1)} %get-tuple-element.160), channel_id=1, source_target_pairs={{0,4},{2,6},{4,0},{6,2},{8,12},{10,14},{12,8},{14,10},{16,20},{18,... | collective-permute-start | bytes 1081352 | tf_op jit(solution)/shard_map/ppermute | solution.py:823
  129.6 21.5 %collective-permute-start.35 = (bf16[352,512]{1,0:T(8,128)(2,1)S(1)}, bf16[352,512]{1,0:T(8,128)(2,1)S(1)}, u32[]{:S(2)}, u32[]{:S(2)}) collective-permute-start(bf16[352,512]{1,0:T(8,128)(2,1)S(1)} %get-tuple-element.161), channel_id=1, source_target_pairs={{0,6},{2,4},{4,2},{6,0},{8,14},{10,12},{12,10},{14,8},{16,22},{18,... | collective-permute-start | bytes 1081352 | tf_op jit(solution)/shard_map/ppermute | solution.py:823
  131.1 15.3 %collective-permute-start.31 = (bf16[144,512]{1,0:T(8,128)(2,1)}, bf16[144,512]{1,0:T(8,128)(2,1)S(1)}, u32[]{:S(2)}, u32[]{:S(2)}) collective-permute-start(bf16[144,512]{1,0:T(8,128)(2,1)} %get-tuple-element.139), channel_id=1, source_target_pairs={{0,8},{2,10},{4,12},{6,14},{8,0},{10,2},{12,4},{14,6},{16,24},{18,... | collective-permute-start | bytes 442376 | tf_op jit(solution)/shard_map/ppermute | solution.py:823
  139.3 38.7 %all-to-all-start.1 = ((bf16[16,16,512]{2,1,0:T(8,128)(2,1)}), bf16[16,16,512]{2,1,0:T(8,128)(2,1)S(1)}, u32[]{:S(2)}, u32[]{:S(2)}) async-start(bf16[16,16,512]{2,1,0:T(8,128)(2,1)} %bitcast.18), calls=%async_computation.1 | async-start | bytes 524288 | tf_op jit(solution)/shard_map/all_to_all | solution.py:1071
  153.5 15.4 %collective-permute-start.39 = (bf16[232,512]{1,0:T(8,128)(2,1)S(1)}, bf16[232,512]{1,0:T(8,128)(2,1)S(1)}, u32[]{:S(2)}, u32[]{:S(2)}) collective-permute-start(bf16[232,512]{1,0:T(8,128)(2,1)S(1)} %get-tuple-element.166), channel_id=1, source_target_pairs={{0,16},{2,18},{4,20},{6,22},{8,24},{10,26},{12,28},{14,30},{16,0},... | collective-permute-start | bytes 712712 | tf_op jit(solution)/shard_map/ppermute | solution.py:823
  153.7 19.8 %collective-permute-start.40 = (bf16[232,512]{1,0:T(8,128)(2,1)S(1)}, bf16[232,512]{1,0:T(8,128)(2,1)S(1)}, u32[]{:S(2)}, u32[]{:S(2)}) collective-permute-start(bf16[232,512]{1,0:T(8,128)(2,1)S(1)} %get-tuple-element.167), channel_id=1, source_target_pairs={{0,24},{2,26},{4,28},{6,30},{8,16},{10,18},{12,20},{14,22},{16,8},... | collective-permute-start | bytes 712712 | tf_op jit(solution)/shard_map/ppermute | solution.py:823
  173.7 16.3 %collective-permute-start.41 = (bf16[576,512]{1,0:T(8,128)(2,1)S(1)}, bf16[576,512]{1,0:T(8,128)(2,1)S(1)}, u32[]{:S(2)}, u32[]{:S(2)}) collective-permute-start(bf16[576,512]{1,0:T(8,128)(2,1)S(1)} %place.3.refs_0_), channel_id=1, source_target_pairs={{0,2},{2,0},{4,6},{6,4},{8,10},{10,8},{12,14},{14,12},{16,18},{18,... | collective-permute-start | bytes 1769480 | tf_op jit(solution)/shard_map/ppermute | solution.py:823
  174.4 24.2 %collective-permute-start.45 = (bf16[576,512]{1,0:T(8,128)(2,1)S(1)}, bf16[576,512]{1,0:T(8,128)(2,1)S(1)}, u32[]{:S(2)}, u32[]{:S(2)}) collective-permute-start(bf16[576,512]{1,0:T(8,128)(2,1)S(1)} %place.3.refs_0_), channel_id=1, source_target_pairs={{0,4},{2,6},{4,0},{6,2},{8,12},{10,14},{12,8},{14,10},{16,20},{18,... | collective-permute-start | bytes 1769480 | tf_op jit(solution)/shard_map/ppermute | solution.py:823
  175.9 27.7 %collective-permute-start.46 = (bf16[576,512]{1,0:T(8,128)(2,1)S(1)}, bf16[576,512]{1,0:T(8,128)(2,1)S(1)}, u32[]{:S(2)}, u32[]{:S(2)}) collective-permute-start(bf16[576,512]{1,0:T(8,128)(2,1)S(1)} %place.3.refs_0_), channel_id=1, source_target_pairs={{0,6},{2,4},{4,2},{6,0},{8,14},{10,12},{12,10},{14,8},{16,22},{18,... | collective-permute-start | bytes 1769480 | tf_op jit(solution)/shard_map/ppermute | solution.py:823
  190.0 20.4 %collective-permute-start.42 = (bf16[352,512]{1,0:T(8,128)(2,1)S(1)}, bf16[352,512]{1,0:T(8,128)(2,1)S(1)}, u32[]{:S(2)}, u32[]{:S(2)}) collective-permute-start(bf16[352,512]{1,0:T(8,128)(2,1)S(1)} %bitcast.58), channel_id=1, source_target_pairs={{0,2},{2,0},{4,6},{6,4},{8,10},{10,8},{12,14},{14,12},{16,18},{18,... | collective-permute-start | bytes 1081352 | tf_op jit(solution)/shard_map/ppermute | solution.py:823
  190.7 25.1 %collective-permute-start.43 = (bf16[352,512]{1,0:T(8,128)(2,1)S(1)}, bf16[352,512]{1,0:T(8,128)(2,1)S(1)}, u32[]{:S(2)}, u32[]{:S(2)}) collective-permute-start(bf16[352,512]{1,0:T(8,128)(2,1)S(1)} %bitcast.59), channel_id=1, source_target_pairs={{0,4},{2,6},{4,0},{6,2},{8,12},{10,14},{12,8},{14,10},{16,20},{18,... | collective-permute-start | bytes 1081352 | tf_op jit(solution)/shard_map/ppermute | solution.py:823
  192.2 23.7 %collective-permute-start.44 = (bf16[352,512]{1,0:T(8,128)(2,1)S(1)}, bf16[352,512]{1,0:T(8,128)(2,1)S(1)}, u32[]{:S(2)}, u32[]{:S(2)}) collective-permute-start(bf16[352,512]{1,0:T(8,128)(2,1)S(1)} %bitcast.60), channel_id=1, source_target_pairs={{0,6},{2,4},{4,2},{6,0},{8,14},{10,12},{12,10},{14,8},{16,22},{18,... | collective-permute-start | bytes 1081352 | tf_op jit(solution)/shard_map/ppermute | solution.py:823
  (89 other events, 630.2 us)
